TPU v7x, 512 devices: a whole 4x8x8 slice. The times are simulated.
512 devices in a mesh: dp: 32 (over x, z), tp: 16 (over y, core).
Axes of the slice: x: 4, y: 8, z: 8, core: 2. Of those that a mesh axis runs over, the one named last changes fastest.
Arguments:
- queries: bfloat16 [1024, 128, 576], P(('dp', 'tp')), may hold values from -40 to 40
- latent_cache: bfloat16 [1024, 256, 576], P(('dp', 'tp')), may hold values from -5 to 5
- lengths: int32 [1024], P(('dp', 'tp')), may hold values from 1 to 256, 65536 in all
- value_weight: bfloat16 [128, 512, 128], P('tp'), may hold values from -0.25 to 0.25
- output_weight: bfloat16 [16384, 7168], P('tp', 'dp'), may hold values from -0.046875 to 0.046875
Outputs:
- attended: bfloat16 [1024, 7168], P(('dp', 'tp'))
All inputs are finite; a program needn't handle non-finite values. No bound on the sum of `lengths` on one device may be relied on, other than what follows from the above.
Results may differ from a plain program's by a relative error of at most 0.0065.
Values may be sent and summed in bfloat16 or wider, within the bound.
No kernel may reach another device: no remote copies, remote signals or barrier semaphores. Data moves between devices by JAX's collectives and lax.ppermute only.
A program may use at most 64 MiB of HBM per device.

v0:
```python
import jax
import jax.numpy as jnp
from jax import lax
from jax.sharding import PartitionSpec as P

score_scale = 192.0 ** (-0.5)


def local(queries, latent_cache, lengths, value_weight, output_weight):
    requests = queries.shape[0]
    groups = lax.axis_size("tp")
    columns = lax.axis_size("dp")
    latent_width = value_weight.shape[1]
    scores = (
        jnp.einsum("rhe,rje->rhj", queries, latent_cache, preferred_element_type=jnp.float32)
        * score_scale
    )
    alive_mask = lax.broadcasted_iota(jnp.int32, scores.shape, 2) < lengths[:, None, None]
    scores = jnp.where(alive_mask, scores, -1e30)
    row_max = jnp.max(scores, axis=2, keepdims=True)
    powers = jnp.exp(scores - row_max)
    weights = (powers / jnp.sum(powers, axis=2, keepdims=True)).astype(jnp.bfloat16)
    mixture = jnp.einsum("rhj,rje->rhe", weights, latent_cache, preferred_element_type=jnp.float32)
    latent = mixture[:, :, :latent_width].astype(jnp.bfloat16)
    swapped = lax.all_to_all(latent, "tp", split_axis=1, concat_axis=0, tiled=True)
    local_heads = swapped.shape[1]
    stacked = swapped.reshape(groups, requests, local_heads, latent_width)
    everyone = lax.all_gather(stacked, "dp", axis=1, tiled=True)
    values = jnp.einsum(
        "gqhd,hde->gqhe", everyone, value_weight, preferred_element_type=jnp.float32
    )
    values = values.astype(jnp.bfloat16)
    all_values = values.reshape(groups * columns * requests, -1)
    summed = lax.psum_scatter(
        jnp.dot(all_values, output_weight, preferred_element_type=jnp.float32),
        "tp",
        scatter_dimension=0,
        tiled=True,
    )
    rounded = summed.astype(jnp.bfloat16)
    return lax.all_to_all(rounded, "dp", split_axis=0, concat_axis=1, tiled=True)


def solution(mesh):
    return jax.shard_map(
        local,
        mesh=mesh,
        in_specs=(
            P(("dp", "tp"), None, None),
            P(("dp", "tp"), None, None),
            P(("dp", "tp")),
            P("tp", None, None),
            P("tp", "dp"),
        ),
        out_specs=P(("dp", "tp"), None),
        check_vma=False,
    )
```

profile of v0, /device:TPU:6, one launch (start us, length us, event | category | flops | bytes accessed | tf_op | source)
XLA Modules:
  0.0 229.7 jit_solution(6659828259434857418)
XLA Ops:
  6.5 0.0 copy-start
  6.5 0.0 all-gather.2.cloned.1.call-start
  6.5 1.5 fusion.10
  8.1 0.2 fusion.15
  8.3 1.6 fusion.12
  9.9 0.3 copy.11
  10.2 18.2 %all_to_all.34 = bf16[2,128,512]{2,0,1:T(2,128)(2,1)S(1)} all-to-all(bf16[2,128,512]{2,0,1:T(2,128)(2,1)S(1)} %copy.11), channel_id=1, replica_groups=mesh['dp'=32,'tp'=16] {'tp'}, dimensions={1} | all-to-all | bytes 524288 | tf_op jit(solution)/shard_map/all_to_all | solution.py:25
  28.4 0.7 copy.27
  29.1 0.0 all-gather.2.cloned.1.call-update
  29.1 0.0 reduce-scatter.2.cloned.1.call-start
  29.2 103.6 %all-gather.2.cloned.1.call-done = bf16[16,64,8,512]{3,2,0,1:T(8,128)(2,1)} async-done(((bf16[16,2,8,512]{3,2,0,1:T(8,128)(2,1)}), bf16[16,64,8,512]{3,2,0,1:T(8,128)(2,1)}) %all-gather.2.cloned.1.call-update) | async-done | bytes 8388624 | tf_op jit(solution)/shard_map/all_gather | solution.py:28
  132.8 0.0 copy-done
  132.8 8.2 %convert_bitcast_fusion = bf16[16,64,8,128]{3,1,0,2:T(8,128)(2,1)S(1)} fusion(bf16[16,64,8,512]{3,2,0,1:T(8,128)(2,1)} %all-gather.2.cloned.1.call-done, bf16[8,512,128]{2,1,0:T(8,128)(2,1)S(1)} %copy-done), kind=kOutput, calls=%fused_computation.6 | convolution fusion | flops 1074790400 | bytes 11534336 | tf_op jit(solution)/shard_map/gqhd,hde->gqhe/dot_general | solution.py:29
  141.0 0.0 copy-start.1
  141.0 1.8 copy.14
  142.8 0.0 copy-done.1
  142.8 1.7 fusion.3
  144.5 0.0 reduce-scatter.2.cloned.1.call-update
  144.6 58.3 %reduce-scatter.2.cloned.1.call-done = f32[64,224]{1,0:T(8,128)} async-done(((f32[1024,224]{1,0:T(8,128)}), f32[64,224]{1,0:T(8,128)}) %reduce-scatter.2.cloned.1.call-update) | async-done | bytes 57360 | tf_op jit(solution)/shard_map/reduce_scatter | solution.py:34
  202.9 0.8 convert_element_type.16
  203.8 18.4 %all_to_all.35 = bf16[32,2,224]{2,1,0:T(2,128)(2,1)S(1)} all-to-all(bf16[32,2,224]{2,1,0:T(2,128)(2,1)S(1)} %all_to_all.28), channel_id=1, replica_groups=mesh['dp'=32,'tp'=16] {'dp'}, dimensions={0} | all-to-all | bytes 57344 | tf_op jit(solution)/shard_map/all_to_all | solution.py:41
  222.1 0.7 all_to_all.31
  (3 shorter events, 0.1 us)
Async XLA Ops:
  6.5 126.3 %copy-start = (bf16[8,512,128]{2,1,0:T(8,128)(2,1)S(1)}, bf16[8,512,128]{2,1,0:T(8,128)(2,1)}, u32[]{:S(2)}) copy-start(bf16[8,512,128]{2,1,0:T(8,128)(2,1)} %param.8) | copy-start | bytes 3145732
  6.5 126.3 %all-gather.2.cloned.1.call-start = ((), (), s32[]{:S(2)}) async-start(), calls=%async_computation.3 | async-start | bytes 8650752 | tf_op jit(solution)/shard_map/all_gather | solution.py:28
  29.1 173.7 %reduce-scatter.2.cloned.1.call-start = ((), (), s32[]{:S(2)}) async-start(), calls=%async_computation.4 | async-start | bytes 1114112 | tf_op jit(solution)/shard_map/reduce_scatter | solution.py:34
  141.0 1.8 copy-start.1
Sparse Core Ops, SparseCore 0:
  29.3 103.4 all-gather.1
  144.7 58.1 reduce-scatter.1
where the time goes:
time: 231 us; the launch traced here: 230 us
  waiting for transfers between devices  162 us (70%)
  blocking collectives  36.6 us (16%)
  between operations  13.5 us (6%)
  matrix products  13.1 us (6%)
  local copies, waits for them, and re-layouts  3.58 us (2%)
    all_gather x1, waiting for transfers between devices, local(): everyone = lax.all_gather(stacked, 'dp', axis=1, tiled=True)  104 us
    reduce_scatter x1, waiting for transfers between devices, local(): lax.psum_scatter(jnp.dot(all_values, output_weight, preferred_element_typ...  58.3 us
    all_to_all x1, blocking collectives, local(): lax.all_to_all(rounded, 'dp', split_axis=0, concat_axis=1, tiled=True)  18.4 us
    all_to_all x1, blocking collectives, local(): lax.all_to_all(latent, 'tp', split_axis=1, concat_axis=0, tiled=True)  18.2 us
    dot_general x1, matrix products, local(): jnp.einsum('gqhd,hde->gqhe', everyone, value_weight, preferred_element_ty...  8.21 us
  transfers between devices with their start and end apart: 2, of which 2 were waited for; matrix products, arithmetic and copies ran while one was open for 0% of the time, Pallas kernels for 0%

commit v1 on v0

--- a/solution.py
+++ b/solution.py
@@ -23,14 +23,10 @@
     mixture = jnp.einsum("rhj,rje->rhe", weights, latent_cache, preferred_element_type=jnp.float32)
     latent = mixture[:, :, :latent_width].astype(jnp.bfloat16)
     swapped = lax.all_to_all(latent, "tp", split_axis=1, concat_axis=0, tiled=True)
-    local_heads = swapped.shape[1]
-    stacked = swapped.reshape(groups, requests, local_heads, latent_width)
-    everyone = lax.all_gather(stacked, "dp", axis=1, tiled=True)
-    values = jnp.einsum(
-        "gqhd,hde->gqhe", everyone, value_weight, preferred_element_type=jnp.float32
-    )
-    values = values.astype(jnp.bfloat16)
-    all_values = values.reshape(groups * columns * requests, -1)
+    values = jnp.einsum("qhd,hde->qhe", swapped, value_weight, preferred_element_type=jnp.float32)
+    values = values.astype(jnp.bfloat16).reshape(groups, requests, -1)
+    everyone = lax.all_gather(values, "dp", axis=1, tiled=True)
+    all_values = everyone.reshape(groups * columns * requests, -1)
     summed = lax.psum_scatter(
         jnp.dot(all_values, output_weight, preferred_element_type=jnp.float32),
         "tp",

time: 231 us -> 204 us (0.88)
  waiting for transfers between devices: 162 us -> 142 us
  matrix products: 13.1 us -> 5.14 us
    all_gather x1, waiting for transfers between devices: 104 us -> 83.9 us  [local(): everyone = lax.all_gather(values, 'dp', axis=1, tiled=True)]
    dot_general x1, matrix products: 8.21 us -> 0.27 us  [local(): jnp.einsum('qhd,hde->qhe', swapped, value_weight, preferred_element_type=...]
    all_gather x0 -> x1, local copies, waits for them, and re-layouts: none -> 2.74 us  [local(): everyone = lax.all_gather(values, 'dp', axis=1, tiled=True)]
where the time goes in v1:
time: 204 us; the launch traced here: 203 us
  waiting for transfers between devices  142 us (70%)
  blocking collectives  36.6 us (18%)
  between operations  13.5 us (7%)
  matrix products  5.14 us (3%)
  local copies, waits for them, and re-layouts  4.78 us (2%)
    all_gather x1, waiting for transfers between devices, local(): everyone = lax.all_gather(values, 'dp', axis=1, tiled=True)  83.9 us
    reduce_scatter x1, waiting for transfers between devices, local(): lax.psum_scatter(jnp.dot(all_values, output_weight, preferred_element_typ...  57.8 us
    all_to_all x1, blocking collectives, local(): lax.all_to_all(rounded, 'dp', split_axis=0, concat_axis=1, tiled=True)  18.4 us
    all_to_all x1, blocking collectives, local(): lax.all_to_all(latent, 'tp', split_axis=1, concat_axis=0, tiled=True)  18.2 us
  transfers between devices with their start and end apart: 2, of which 2 were waited for; matrix products, arithmetic and copies ran while one was open for 0% of the time, Pallas kernels for 0%

profile of v1, /device:TPU:6, one launch (start us, length us, event | category | flops | bytes accessed | tf_op | source)
XLA Modules:
  0.0 202.7 jit_solution(8184634764328297941)
XLA Ops:
  6.5 0.0 copy-start
  6.5 0.0 all-gather.2.cloned.1.call-start
  6.5 1.5 fusion.3
  8.1 0.2 fusion.8
  8.3 1.6 fusion.5
  9.9 0.3 copy.16
  10.2 18.2 %all_to_all.37 = bf16[2,128,512]{2,0,1:T(2,128)(2,1)S(1)} all-to-all(bf16[2,128,512]{2,0,1:T(2,128)(2,1)S(1)} %copy.16), channel_id=1, replica_groups=mesh['dp'=32,'tp'=16] {'tp'}, dimensions={1} | all-to-all | bytes 524288 | tf_op jit(solution)/shard_map/all_to_all | solution.py:25
  28.4 0.2 copy.23
  28.6 0.1 all_to_all.30
  28.7 0.0 copy-done
  28.7 0.3 fusion.4
  29.0 0.6 copy.19
  29.7 0.0 all-gather.2.cloned.1.call-update
  29.7 0.0 copy-start.1
  29.7 0.0 reduce-scatter.2.cloned.1.call-start
  29.7 83.9 %all-gather.2.cloned.1.call-done = bf16[16,64,1024]{2,0,1:T(8,128)(2,1)} async-done(((bf16[16,2,1024]{2,0,1:T(8,128)(2,1)}), bf16[16,64,1024]{2,0,1:T(8,128)(2,1)}) %all-gather.2.cloned.1.call-update) | async-done | bytes 2097168 | tf_op jit(solution)/shard_map/all_gather | solution.py:28
  113.6 2.7 %copy.20 = bf16[16,64,1024]{2,1,0:T(8,128)(2,1)S(1)} copy(bf16[16,64,1024]{2,0,1:T(8,128)(2,1)} %all-gather.2.cloned.1.call-done) | data formatting | bytes 4194304 | tf_op jit(solution)/shard_map/all_gather | solution.py:28
  116.4 0.0 copy-done.1
  116.4 1.7 fusion.9
  118.1 0.0 reduce-scatter.2.cloned.1.call-update
  118.1 57.8 %reduce-scatter.2.cloned.1.call-done = f32[64,224]{1,0:T(8,128)} async-done(((f32[1024,224]{1,0:T(8,128)}), f32[64,224]{1,0:T(8,128)}) %reduce-scatter.2.cloned.1.call-update) | async-done | bytes 57360 | tf_op jit(solution)/shard_map/reduce_scatter | solution.py:30
  175.9 0.8 convert_element_type.16
  176.8 18.4 %all_to_all.38 = bf16[32,2,224]{2,1,0:T(2,128)(2,1)S(1)} all-to-all(bf16[32,2,224]{2,1,0:T(2,128)(2,1)S(1)} %all_to_all.31), channel_id=1, replica_groups=mesh['dp'=32,'tp'=16] {'dp'}, dimensions={0} | all-to-all | bytes 57344 | tf_op jit(solution)/shard_map/all_to_all | solution.py:37
  195.2 0.7 all_to_all.34
  (5 shorter events, 0.1 us)
Async XLA Ops:
  6.5 22.1 %copy-start = (bf16[8,512,128]{2,1,0:T(8,128)(2,1)S(1)}, bf16[8,512,128]{2,1,0:T(8,128)(2,1)}, u32[]{:S(2)}) copy-start(bf16[8,512,128]{2,1,0:T(8,128)(2,1)} %param.8) | copy-start | bytes 3145732
  6.5 107.1 %all-gather.2.cloned.1.call-start = ((), (), s32[]{:S(2)}) async-start(), calls=%async_computation.3 | async-start | bytes 2162688 | tf_op jit(solution)/shard_map/all_gather | solution.py:28
  29.7 86.7 %copy-start.1 = (bf16[1024,224]{0,1:T(8,128)(2,1)S(1)}, bf16[1024,224]{0,1:T(8,128)(2,1)}, u32[]{:S(2)}) copy-start(bf16[1024,224]{0,1:T(8,128)(2,1)} %param.9) | copy-start | bytes 1376260
  29.7 146.2 %reduce-scatter.2.cloned.1.call-start = ((), (), s32[]{:S(2)}) async-start(), calls=%async_computation.4 | async-start | bytes 1114112 | tf_op jit(solution)/shard_map/reduce_scatter | solution.py:30
Sparse Core Ops, SparseCore 0:
  29.8 83.7 all-gather.1
  118.2 57.6 reduce-scatter.1

commit v2 on v1

v2 whole, which is shorter than its diff:
```python
import jax
import jax.numpy as jnp
from jax import lax
from jax.sharding import Mesh
from jax.sharding import PartitionSpec as P

score_scale = 192.0 ** (-0.5)
f32 = jnp.float32
bf16 = jnp.bfloat16


def attend(queries, latent_cache, lengths, latent_width):
    scores = (
        jnp.einsum("rhe,rje->rhj", queries, latent_cache, preferred_element_type=f32)
        * score_scale
    )
    alive_mask = lax.broadcasted_iota(jnp.int32, scores.shape, 2) < lengths[:, None, None]
    scores = jnp.where(alive_mask, scores, -1e30)
    row_max = jnp.max(scores, axis=2, keepdims=True)
    powers = jnp.exp(scores - row_max)
    weights = (powers / jnp.sum(powers, axis=2, keepdims=True)).astype(bf16)
    mixture = jnp.einsum("rhj,rje->rhe", weights, latent_cache, preferred_element_type=f32)
    return mixture[:, :, :latent_width].astype(bf16)


def local(queries, latent_cache, lengths, value_weight, output_weight):
    nx, nz, ny, nc = (lax.axis_size(a) for a in ("x", "z", "y", "c"))
    x, c = lax.axis_index("x"), lax.axis_index("c")
    requests = queries.shape[0]
    blocks = [output_weight] + [
        lax.ppermute(output_weight, "x", [(i, (i + k) % nx) for i in range(nx)])
        for k in range(1, nx)
    ]
    latent = attend(queries, latent_cache, lengths, value_weight.shape[1])
    swapped = lax.all_to_all(latent, ("y", "c"), split_axis=1, concat_axis=0, tiled=True)
    values = jnp.einsum("qhd,hde->qhe", swapped, value_weight, preferred_element_type=f32)
    values = values.astype(bf16).reshape(ny, nc, requests, -1)
    values = values.transpose(1, 0, 2, 3).reshape(nc, ny * requests, -1)
    everyone = lax.all_to_all(
        jnp.broadcast_to(values[None], (nz, *values.shape)), "z", split_axis=0, concat_axis=0, tiled=True
    )

    def product(core):
        rows = lax.dynamic_index_in_dim(everyone, core, 1, keepdims=False)
        rows = rows.reshape(nz * ny * requests, -1)
        return jnp.concatenate(
            [jnp.dot(rows, w, preferred_element_type=f32) for w in blocks], axis=1
        )

    theirs = product(1 - c)
    received = lax.ppermute(theirs, "c", [(i, (i + 1) % nc) for i in range(nc)])
    summed = (product(c) + received).astype(bf16).reshape(nz * ny, requests, -1)
    parts = lax.all_to_all(summed, ("z", "y"), split_axis=0, concat_axis=0, tiled=True)
    parts = parts.reshape(nz, ny, requests, nx, -1).astype(f32)
    total = jnp.sum(parts, axis=1).astype(bf16)
    order = jnp.mod(x - jnp.arange(nx), nx)
    total = jnp.take(total, order, axis=2)
    return total.transpose(1, 2, 0, 3).reshape(requests, -1)


def solution(mesh):
    grid = Mesh(mesh.devices.reshape(4, 8, 8, 2), ("x", "z", "y", "c"))
    everything = ("x", "z", "y", "c")
    return jax.shard_map(
        local,
        mesh=grid,
        in_specs=(
            P(everything, None, None),
            P(everything, None, None),
            P(everything),
            P(("y", "c"), None, None),
            P(("y", "c"), ("x", "z")),
        ),
        out_specs=P(everything, None),
        check_vma=False,
    )
```

time: 204 us -> 90.1 us (0.44)
  waiting for transfers between devices: 142 us -> 31.2 us
  starting transfers between devices: 0.04 us -> 30.2 us
  blocking collectives: 36.6 us -> 18.2 us
  between operations: 13.5 us -> 0.28 us
    all_gather x1 -> x0, waiting for transfers between devices: 83.9 us -> none  [local(): everyone = lax.all_gather(values, 'dp', axis=1, tiled=True)]
    reduce_scatter x1 -> x0, waiting for transfers between devices: 57.8 us -> none  [local(): lax.psum_scatter(jnp.dot(all_values, output_weight, preferred_element_typ...]
    all_to_all x0 -> x2, waiting for transfers between devices: none -> 23.9 us  [the longest x1 14.6 us: local(): lax.all_to_all(summed, ('z', 'y'), split_axis=0, concat_axis=0, tiled=True)]
    all_to_all x0 -> x2, starting transfers between devices: none -> 19 us  [the longest x1 10.4 us: local(): lax.all_to_all(jnp.broadcast_to(values[None], (nz, *values.shape)), 'z',...]
    all_to_all x2 -> x1, blocking collectives: 36.6 us -> 18.2 us  [local(): lax.all_to_all(latent, ('y', 'c'), split_axis=1, concat_axis=0, tiled=True)]
    ppermute x0 -> x4, starting transfers between devices: none -> 11.2 us  [the longest x3 9.26 us: local(): lax.ppermute(output_weight, 'x', [(i, (i + k) % nx) for i in range(nx)])]
    ppermute x0 -> x4, waiting for transfers between devices: none -> 7.3 us  [the longest x3 6.41 us: local(): lax.ppermute(output_weight, 'x', [(i, (i + k) % nx) for i in range(nx)])]
    all_gather x1 -> x0, local copies, waits for them, and re-layouts: 2.74 us -> none  [local(): everyone = lax.all_gather(values, 'dp', axis=1, tiled=True)]
  transfers between devices with their start and end apart: 2 -> 6, of which waited for: 2 -> 5; matrix products, arithmetic and copies ran while one was open for 0% -> 2% of each run, Pallas kernels for 0% -> 0%
where the time goes in v2:
time: 90.1 us; the launch traced here: 89.3 us
  waiting for transfers between devices  31.2 us (35%)
  starting transfers between devices  30.2 us (34%)
  blocking collectives  18.2 us (20%)
  matrix products  4.7 us (5%)
  local copies, waits for them, and re-layouts  4.13 us (5%)
    all_to_all x1, blocking collectives, local(): lax.all_to_all(latent, ('y', 'c'), split_axis=1, concat_axis=0, tiled=True)  18.2 us
    all_to_all x1, waiting for transfers between devices, local(): lax.all_to_all(summed, ('z', 'y'), split_axis=0, concat_axis=0, tiled=True)  14.6 us
    all_to_all x1, starting transfers between devices, local(): lax.all_to_all(jnp.broadcast_to(values[None], (nz, *values.shape)), 'z',...  10.4 us
    all_to_all x1, waiting for transfers between devices, local(): lax.all_to_all(jnp.broadcast_to(values[None], (nz, *values.shape)), 'z',...  9.35 us
    ppermute x3, starting transfers between devices, local(): lax.ppermute(output_weight, 'x', [(i, (i + k) % nx) for i in range(nx)])  9.26 us
    all_to_all x1, starting transfers between devices, local(): lax.all_to_all(summed, ('z', 'y'), split_axis=0, concat_axis=0, tiled=True)  8.57 us
    ppermute x3, waiting for transfers between devices, local(): lax.ppermute(output_weight, 'x', [(i, (i + k) % nx) for i in range(nx)])  6.41 us
    dot_general x8, matrix products, product(): jnp.dot(rows, w, preferred_element_type=f32)  2.32 us
  transfers between devices with their start and end apart: 6, of which 5 were waited for; matrix products, arithmetic and copies ran while one was open for 2% of the time, Pallas kernels for 0%

profile of v2, /device:TPU:6, one launch (start us, length us, event | category | flops | bytes accessed | tf_op | source)
XLA Modules:
  0.0 89.3 jit_solution(14684094058534781210)
XLA Ops:
  0.0 0.0 copy-start
  0.0 0.0 copy-start.2
  0.0 1.6 %fusion.3 = f32[2,128,256]{2,1,0:T(8,128)S(1)} fusion(bf16[2,128,576]{1,2,0:T(8,128)(2,1)} %param.5, bf16[2,256,576]{1,2,0:T(8,128)(2,1)} %param.6, s32[2]{0:T(128)} %param.7), kind=kOutput, calls=%fused_computation.5 | convolution fusion | flops 75694080 | bytes 1146888 | tf_op jit(solution)/shard_map/rhe,rje->rhj/dot_general | solution.py:14
  1.6 0.2 fusion.12
  1.8 0.0 copy-done.2
  1.8 0.5 fusion.6
  2.4 0.3 copy.18
  2.6 18.2 %all_to_all.28 = bf16[2,128,512]{2,0,1:T(2,128)(2,1)S(1)} all-to-all(bf16[2,128,512]{2,0,1:T(2,128)(2,1)S(1)} %copy.18), channel_id=1, replica_groups=mesh['x'=4,'z'=8,'y'=8,'c'=2] {'y','c'}, dimensions={1} | all-to-all | bytes 524288 | tf_op jit(solution)/shard_map/all_to_all | solution.py:35
  20.8 0.2 copy.27
  21.0 0.1 all_to_all.22
  21.1 0.0 copy-done
  21.1 0.3 fusion.4
  21.5 0.1 copy.21
  21.6 0.8 broadcast_in_dim.27
  22.4 0.0 copy-start.1
  22.4 10.4 %all-to-all-start.1 = ((bf16[8,2,16,1024]{3,2,1,0:T(8,128)(2,1)}), bf16[8,2,16,1024]{3,2,1,0:T(8,128)(2,1)S(1)}, u32[]{:S(2)}, u32[]{:S(2)}) async-start(bf16[8,2,16,1024]{3,2,1,0:T(8,128)(2,1)} %broadcast_in_dim.27), calls=%async_computation.1 | async-start | bytes 1048576 | tf_op jit(solution)/shard_map/all_to_all | solution.py:39
  32.8 0.0 copy-done.1
  32.9 3.3 %collective-permute-start.1 = (bf16[1024,224]{0,1:T(8,128)(2,1)S(1)}, bf16[1024,224]{0,1:T(8,128)(2,1)S(1)}, u32[]{:S(2)}, u32[]{:S(2)}) collective-permute-start(bf16[1024,224]{0,1:T(8,128)(2,1)S(1)} %copy-done.1), channel_id=1, source_target_pairs={{0,256},{128,384},{256,0},{384,128},{1,257},{129,385},{257,1},{385... | collective-permute-start | bytes 1376264 | tf_op jit(solution)/shard_map/ppermute | solution.py:31
  36.2 4.0 %collective-permute-start = (bf16[1024,224]{0,1:T(8,128)(2,1)S(1)}, bf16[1024,224]{0,1:T(8,128)(2,1)S(1)}, u32[]{:S(2)}, u32[]{:S(2)}) collective-permute-start(bf16[1024,224]{0,1:T(8,128)(2,1)S(1)} %copy-done.1), channel_id=1, source_target_pairs={{0,128},{128,256},{256,384},{384,0},{1,129},{129,257},{257,385},{3... | collective-permute-start | bytes 1376264 | tf_op jit(solution)/shard_map/ppermute | solution.py:31
  40.2 1.9 %collective-permute-start.2 = (bf16[1024,224]{0,1:T(8,128)(2,1)S(1)}, bf16[1024,224]{0,1:T(8,128)(2,1)S(1)}, u32[]{:S(2)}, u32[]{:S(2)}) collective-permute-start(bf16[1024,224]{0,1:T(8,128)(2,1)S(1)} %copy-done.1), channel_id=1, source_target_pairs={{0,384},{128,0},{256,128},{384,256},{1,385},{129,1},{257,129},{385... | collective-permute-start | bytes 1376264 | tf_op jit(solution)/shard_map/ppermute | solution.py:31
  42.1 9.4 %all-to-all-done.1 = bf16[8,2,16,1024]{3,2,1,0:T(8,128)(2,1)S(1)} async-done(((bf16[8,2,16,1024]{3,2,1,0:T(8,128)(2,1)}), bf16[8,2,16,1024]{3,2,1,0:T(8,128)(2,1)S(1)}, u32[]{:S(2)}, u32[]{:S(2)}) %all-to-all-start.1) | async-done | bytes 524320 | tf_op jit(solution)/shard_map/all_to_all | solution.py:39
  51.5 0.3 fusion.17
  51.8 0.3 fusion.13
  52.1 0.0 collective-permute-done.1
  52.1 0.3 fusion.19
  52.5 4.6 %collective-permute-done = bf16[1024,224]{0,1:T(8,128)(2,1)S(1)} collective-permute-done((bf16[1024,224]{0,1:T(8,128)(2,1)S(1)}, bf16[1024,224]{0,1:T(8,128)(2,1)S(1)}, u32[]{:S(2)}, u32[]{:S(2)}) %collective-permute-start) | collective-permute-done | bytes 458784 | tf_op jit(solution)/shard_map/ppermute | solution.py:31
  57.0 0.3 fusion.18
  57.3 1.8 %collective-permute-done.2 = bf16[1024,224]{0,1:T(8,128)(2,1)S(1)} collective-permute-done((bf16[1024,224]{0,1:T(8,128)(2,1)S(1)}, bf16[1024,224]{0,1:T(8,128)(2,1)S(1)}, u32[]{:S(2)}, u32[]{:S(2)}) %collective-permute-start.2) | collective-permute-done | bytes 458784 | tf_op jit(solution)/shard_map/ppermute | solution.py:31
  59.2 0.3 fusion.20
  59.5 1.9 %collective-permute-start.3 = (f32[128,896]{0,1:T(8,128)S(1)}, f32[128,896]{0,1:T(8,128)S(1)}, u32[]{:S(2)}, u32[]{:S(2)}) collective-permute-start(f32[128,896]{0,1:T(8,128)S(1)} %pad_maximum_fusion), channel_id=1, source_target_pairs={{0,1},{1,0},{2,3},{3,2},{4,5},{5,4},{6,7},{7,6},{8,9},{9,8},{10,11... | collective-permute-start | bytes 1376264 | tf_op jit(solution)/shard_map/ppermute | solution.py:51
  61.4 0.3 fusion.15
  61.7 0.3 fusion.14
  62.0 0.3 fusion.16
  62.3 0.9 collective-permute-done.3
  63.3 0.2 copy.23
  63.4 0.8 reshape.81
  64.2 8.6 %all-to-all-start.2 = ((bf16[64,2,896]{2,1,0:T(2,128)(2,1)}), bf16[64,2,896]{2,1,0:T(2,128)(2,1)S(1)}, u32[]{:S(2)}, u32[]{:S(2)}) async-start(bf16[64,2,896]{2,1,0:T(2,128)(2,1)} %reshape.81), calls=%async_computation.2 | async-start | bytes 458752 | tf_op jit(solution)/shard_map/all_to_all | solution.py:53
  72.8 14.6 %all-to-all-done.2 = bf16[64,2,896]{2,1,0:T(2,128)(2,1)S(1)} async-done(((bf16[64,2,896]{2,1,0:T(2,128)(2,1)}), bf16[64,2,896]{2,1,0:T(2,128)(2,1)S(1)}, u32[]{:S(2)}, u32[]{:S(2)}) %all-to-all-start.2) | async-done | bytes 229408 | tf_op jit(solution)/shard_map/all_to_all | solution.py:53
  87.4 0.3 reshape.82
  87.7 0.1 reduce_sum.22
  87.9 0.6 gather_fusion
  88.4 0.1 select_bitcast_fusion
  88.5 0.7 reshape.83
  (12 shorter events, 0.3 us)
Async XLA Ops:
  0.0 21.1 %copy-start = (bf16[8,512,128]{2,1,0:T(8,128)(2,1)S(1)}, bf16[8,512,128]{2,1,0:T(8,128)(2,1)}, u32[]{:S(2)}) copy-start(bf16[8,512,128]{2,1,0:T(8,128)(2,1)} %param.8) | copy-start | bytes 3145732
  0.0 1.8 %copy-start.2 = (bf16[2,256,576]{1,2,0:T(8,128)(2,1)S(1)}, bf16[2,256,576]{1,2,0:T(8,128)(2,1)}, u32[]{:S(2)}) copy-start(bf16[2,256,576]{1,2,0:T(8,128)(2,1)} %param.6) | copy-start | bytes 1769476
  22.4 10.5 %copy-start.1 = (bf16[1024,224]{0,1:T(8,128)(2,1)S(1)}, bf16[1024,224]{0,1:T(8,128)(2,1)}, u32[]{:S(2)}) copy-start(bf16[1024,224]{0,1:T(8,128)(2,1)} %param.9) | copy-start | bytes 1376260
  22.4 29.1 %all-to-all-start.1 = ((bf16[8,2,16,1024]{3,2,1,0:T(8,128)(2,1)}), bf16[8,2,16,1024]{3,2,1,0:T(8,128)(2,1)S(1)}, u32[]{:S(2)}, u32[]{:S(2)}) async-start(bf16[8,2,16,1024]{3,2,1,0:T(8,128)(2,1)} %broadcast_in_dim.27), calls=%async_computation.1 | async-start | bytes 1048576 | tf_op jit(solution)/shard_map/all_to_all | solution.py:39
  32.9 19.3 %collective-permute-start.1 = (bf16[1024,224]{0,1:T(8,128)(2,1)S(1)}, bf16[1024,224]{0,1:T(8,128)(2,1)S(1)}, u32[]{:S(2)}, u32[]{:S(2)}) collective-permute-start(bf16[1024,224]{0,1:T(8,128)(2,1)S(1)} %copy-done.1), channel_id=1, source_target_pairs={{0,256},{128,384},{256,0},{384,128},{1,257},{129,385},{257,1},{385... | collective-permute-start | bytes 1376264 | tf_op jit(solution)/shard_map/ppermute | solution.py:31
  36.2 20.8 %collective-permute-start = (bf16[1024,224]{0,1:T(8,128)(2,1)S(1)}, bf16[1024,224]{0,1:T(8,128)(2,1)S(1)}, u32[]{:S(2)}, u32[]{:S(2)}) collective-permute-start(bf16[1024,224]{0,1:T(8,128)(2,1)S(1)} %copy-done.1), channel_id=1, source_target_pairs={{0,128},{128,256},{256,384},{384,0},{1,129},{129,257},{257,385},{3... | collective-permute-start | bytes 1376264 | tf_op jit(solution)/shard_map/ppermute | solution.py:31
  40.2 19.0 %collective-permute-start.2 = (bf16[1024,224]{0,1:T(8,128)(2,1)S(1)}, bf16[1024,224]{0,1:T(8,128)(2,1)S(1)}, u32[]{:S(2)}, u32[]{:S(2)}) collective-permute-start(bf16[1024,224]{0,1:T(8,128)(2,1)S(1)} %copy-done.1), channel_id=1, source_target_pairs={{0,384},{128,0},{256,128},{384,256},{1,385},{129,1},{257,129},{385... | collective-permute-start | bytes 1376264 | tf_op jit(solution)/shard_map/ppermute | solution.py:31
  59.5 3.7 %collective-permute-start.3 = (f32[128,896]{0,1:T(8,128)S(1)}, f32[128,896]{0,1:T(8,128)S(1)}, u32[]{:S(2)}, u32[]{:S(2)}) collective-permute-start(f32[128,896]{0,1:T(8,128)S(1)} %pad_maximum_fusion), channel_id=1, source_target_pairs={{0,1},{1,0},{2,3},{3,2},{4,5},{5,4},{6,7},{7,6},{8,9},{9,8},{10,11... | collective-permute-start | bytes 1376264 | tf_op jit(solution)/shard_map/ppermute | solution.py:51
  64.2 23.2 %all-to-all-start.2 = ((bf16[64,2,896]{2,1,0:T(2,128)(2,1)}), bf16[64,2,896]{2,1,0:T(2,128)(2,1)S(1)}, u32[]{:S(2)}, u32[]{:S(2)}) async-start(bf16[64,2,896]{2,1,0:T(2,128)(2,1)} %reshape.81), calls=%async_computation.2 | async-start | bytes 458752 | tf_op jit(solution)/shard_map/all_to_all | solution.py:53

commit v3 on v2

--- a/solution.py
+++ b/solution.py
@@ -27,15 +27,20 @@
     nx, nz, ny, nc = (lax.axis_size(a) for a in ("x", "z", "y", "c"))
     x, c = lax.axis_index("x"), lax.axis_index("c")
     requests = queries.shape[0]
-    blocks = [output_weight] + [
-        lax.ppermute(output_weight, "x", [(i, (i + k) % nx) for i in range(nx)])
-        for k in range(1, nx)
-    ]
+    ahead = [(i, (i + 1) % nx) for i in range(nx)]
+    back = [(i, (i - 1) % nx) for i in range(nx)]
+    half = output_weight.shape[1] // 2
+    previous = lax.ppermute(output_weight, "x", ahead)
+    following = lax.ppermute(output_weight, "x", back)
     latent = attend(queries, latent_cache, lengths, value_weight.shape[1])
     swapped = lax.all_to_all(latent, ("y", "c"), split_axis=1, concat_axis=0, tiled=True)
     values = jnp.einsum("qhd,hde->qhe", swapped, value_weight, preferred_element_type=f32)
     values = values.astype(bf16).reshape(ny, nc, requests, -1)
     values = values.transpose(1, 0, 2, 3).reshape(nc, ny * requests, -1)
+    values, previous, following = lax.optimization_barrier((values, previous, following))
+    low = lax.ppermute(previous[:, :half], "x", ahead)
+    high = lax.ppermute(following[:, half:], "x", back)
+    blocks = [output_weight, previous, low, high, following]
     everyone = lax.all_to_all(
         jnp.broadcast_to(values[None], (nz, *values.shape)), "z", split_axis=0, concat_axis=0, tiled=True
     )

time: 90.1 us -> 88.2 us (0.979)
  blocking collectives: 18.2 us -> 0 us
  starting transfers between devices: 30.2 us -> 37.9 us
  waiting for transfers between devices: 31.2 us -> 37.6 us
  local copies, waits for them, and re-layouts: 4.13 us -> 6.24 us
    all_to_all x1 -> x0, blocking collectives: 18.2 us -> none  [local(): lax.all_to_all(latent, ('y', 'c'), split_axis=1, concat_axis=0, tiled=True)]
    all_to_all x0 -> x1, starting transfers between devices: none -> 7.21 us  [local(): lax.all_to_all(latent, ('y', 'c'), split_axis=1, concat_axis=0, tiled=True)]
    all_to_all x0 -> x1, waiting for transfers between devices: none -> 5.15 us  [local(): lax.all_to_all(latent, ('y', 'c'), split_axis=1, concat_axis=0, tiled=True)]
    ppermute x3 -> x4, starting transfers between devices: 9.26 us -> 11.8 us  [the longest x1 4.08 us: local(): previous = lax.ppermute(output_weight, 'x', ahead)]
    all_to_all x1, starting transfers between devices: 10.4 us -> 8.76 us  [local(): lax.all_to_all(jnp.broadcast_to(values[None], (nz, *values.shape)), 'z',...]
    slice x0 -> x2, local copies, waits for them, and re-layouts: none -> 1.41 us  [the longest x1 0.72 us: local(): high = lax.ppermute(following[:, half:], 'x', back)]
    ppermute x3 -> x4, waiting for transfers between devices: 6.41 us -> 7.76 us  [the longest x1 4.88 us: local(): following = lax.ppermute(output_weight, 'x', back)]
    dot_general x8 -> x10, matrix products: 2.32 us -> 2.67 us  [product(): jnp.dot(rows, w, preferred_element_type=f32)]
  transfers between devices with their start and end apart: 6 -> 8, of which waited for: 5 -> 6; matrix products, arithmetic and copies ran while one was open for 2% -> 5% of each run, Pallas kernels for 0% -> 0%
where the time goes in v3:
time: 88.2 us; the launch traced here: 87.7 us
  starting transfers between devices  37.9 us (43%)
  waiting for transfers between devices  37.6 us (43%)
  local copies, waits for them, and re-layouts  6.24 us (7%)
  matrix products  5.05 us (6%)
    all_to_all x1, waiting for transfers between devices, local(): lax.all_to_all(summed, ('z', 'y'), split_axis=0, concat_axis=0, tiled=True)  14.6 us
    all_to_all x1, waiting for transfers between devices, local(): lax.all_to_all(jnp.broadcast_to(values[None], (nz, *values.shape)), 'z',...  9.74 us
    all_to_all x1, starting transfers between devices, local(): lax.all_to_all(jnp.broadcast_to(values[None], (nz, *values.shape)), 'z',...  8.76 us
    all_to_all x1, starting transfers between devices, local(): lax.all_to_all(summed, ('z', 'y'), split_axis=0, concat_axis=0, tiled=True)  8.23 us
    all_to_all x1, starting transfers between devices, local(): lax.all_to_all(latent, ('y', 'c'), split_axis=1, concat_axis=0, tiled=True)  7.21 us
    all_to_all x1, waiting for transfers between devices, local(): lax.all_to_all(latent, ('y', 'c'), split_axis=1, concat_axis=0, tiled=True)  5.15 us
    ppermute x1, waiting for transfers between devices, local(): following = lax.ppermute(output_weight, 'x', back)  4.88 us
    ppermute x1, starting transfers between devices, local(): previous = lax.ppermute(output_weight, 'x', ahead)  4.08 us
  transfers between devices with their start and end apart: 8, of which 6 were waited for; matrix products, arithmetic and copies ran while one was open for 5% of the time, Pallas kernels for 0%

profile of v3, /device:TPU:6, one launch (start us, length us, event | category | flops | bytes accessed | tf_op | source)
XLA Modules:
  0.0 87.7 jit_solution(9948710582480752948)
XLA Ops:
  0.0 0.0 copy-start
  0.0 0.0 copy-start.2
  0.0 1.6 %fusion.3 = f32[2,128,256]{2,1,0:T(8,128)S(1)} fusion(bf16[2,128,576]{1,2,0:T(8,128)(2,1)} %param.5, bf16[2,256,576]{1,2,0:T(8,128)(2,1)} %param.6, s32[2]{0:T(128)} %param.7), kind=kOutput, calls=%fused_computation.5 | convolution fusion | flops 75694080 | bytes 1146888 | tf_op jit(solution)/shard_map/rhe,rje->rhj/dot_general | solution.py:14
  1.6 0.2 fusion.11
  1.8 0.0 copy-done.2
  1.8 0.5 fusion.5
  2.4 0.0 copy-start.1
  2.4 1.0 %copy.18 = bf16[2,128,512]{2,0,1:T(2,128)(2,1)} copy(bf16[2,128,512]{2,1,0:T(8,128)(2,1)S(1)} %slice.17) | data formatting | bytes 524288 | tf_op jit(solution)/shard_map/slice | solution.py:23
  3.3 7.2 %all-to-all-start = ((bf16[2,128,512]{2,0,1:T(2,128)(2,1)}), bf16[2,128,512]{2,0,1:T(2,128)(2,1)S(1)}, u32[]{:S(2)}, u32[]{:S(2)}) async-start(bf16[2,128,512]{2,0,1:T(2,128)(2,1)} %copy.18), calls=%async_computation | async-start | bytes 524288 | tf_op jit(solution)/shard_map/all_to_all | solution.py:36
  10.5 0.0 copy-done.1
  10.6 4.1 %collective-permute-start = (bf16[1024,224]{0,1:T(8,128)(2,1)S(1)}, bf16[1024,224]{0,1:T(8,128)(2,1)S(1)}, u32[]{:S(2)}, u32[]{:S(2)}) collective-permute-start(bf16[1024,224]{0,1:T(8,128)(2,1)S(1)} %copy-done.1), channel_id=1, source_target_pairs={{0,128},{128,256},{256,384},{384,0},{1,129},{129,257},{257,385},{3... | collective-permute-start | bytes 1376264 | tf_op jit(solution)/shard_map/ppermute | solution.py:33
  14.6 1.9 %collective-permute-start.1 = (bf16[1024,224]{0,1:T(8,128)(2,1)S(1)}, bf16[1024,224]{0,1:T(8,128)(2,1)S(1)}, u32[]{:S(2)}, u32[]{:S(2)}) collective-permute-start(bf16[1024,224]{0,1:T(8,128)(2,1)S(1)} %copy-done.1), channel_id=1, source_target_pairs={{0,384},{128,0},{256,128},{384,256},{1,385},{129,1},{257,129},{385... | collective-permute-start | bytes 1376264 | tf_op jit(solution)/shard_map/ppermute | solution.py:34
  16.6 5.1 %all-to-all-done = bf16[2,128,512]{2,0,1:T(2,128)(2,1)S(1)} async-done(((bf16[2,128,512]{2,0,1:T(2,128)(2,1)}), bf16[2,128,512]{2,0,1:T(2,128)(2,1)S(1)}, u32[]{:S(2)}, u32[]{:S(2)}) %all-to-all-start) | async-done | bytes 262176 | tf_op jit(solution)/shard_map/all_to_all | solution.py:36
  21.7 0.2 copy.27
  21.9 0.1 all_to_all.22
  22.0 0.0 copy-done
  22.0 0.3 fusion.4
  22.4 0.1 copy.21
  22.4 2.9 %collective-permute-done = bf16[1024,224]{0,1:T(8,128)(2,1)S(1)} collective-permute-done((bf16[1024,224]{0,1:T(8,128)(2,1)S(1)}, bf16[1024,224]{0,1:T(8,128)(2,1)S(1)}, u32[]{:S(2)}, u32[]{:S(2)}) %collective-permute-start) | collective-permute-done | bytes 458784 | tf_op jit(solution)/shard_map/ppermute | solution.py:33
  25.3 4.9 %collective-permute-done.1 = bf16[1024,224]{0,1:T(8,128)(2,1)S(1)} collective-permute-done((bf16[1024,224]{0,1:T(8,128)(2,1)S(1)}, bf16[1024,224]{0,1:T(8,128)(2,1)S(1)}, u32[]{:S(2)}, u32[]{:S(2)}) %collective-permute-start.1) | collective-permute-done | bytes 458784 | tf_op jit(solution)/shard_map/ppermute | solution.py:34
  30.2 0.8 broadcast_in_dim.25
  31.1 8.8 %all-to-all-start.1 = ((bf16[8,2,16,1024]{3,2,1,0:T(8,128)(2,1)}), bf16[8,2,16,1024]{3,2,1,0:T(8,128)(2,1)S(1)}, u32[]{:S(2)}, u32[]{:S(2)}) async-start(bf16[8,2,16,1024]{3,2,1,0:T(8,128)(2,1)} %broadcast_in_dim.25), calls=%async_computation.1 | async-start | bytes 1048576 | tf_op jit(solution)/shard_map/all_to_all | solution.py:44
  39.8 0.7 slice.11
  40.5 2.2 %collective-permute-start.2 = (bf16[1024,112]{0,1:T(8,128)(2,1)}, bf16[1024,112]{0,1:T(8,128)(2,1)S(1)}, u32[]{:S(2)}, u32[]{:S(2)}) collective-permute-start(bf16[1024,112]{0,1:T(8,128)(2,1)} %slice.11), channel_id=1, source_target_pairs={{0,128},{128,256},{256,384},{384,0},{1,129},{129,257},{257,385},{3... | collective-permute-start | bytes 688136 | tf_op jit(solution)/shard_map/ppermute | solution.py:41
  42.7 0.7 slice.12
  43.4 3.6 %collective-permute-start.3 = (bf16[1024,112]{0,1:T(8,128)(2,1)}, bf16[1024,112]{0,1:T(8,128)(2,1)S(1)}, u32[]{:S(2)}, u32[]{:S(2)}) collective-permute-start(bf16[1024,112]{0,1:T(8,128)(2,1)} %slice.12), channel_id=1, source_target_pairs={{0,384},{128,0},{256,128},{384,256},{1,385},{129,1},{257,129},{385... | collective-permute-start | bytes 688136 | tf_op jit(solution)/shard_map/ppermute | solution.py:42
  47.1 9.7 %all-to-all-done.1 = bf16[8,2,16,1024]{3,2,1,0:T(8,128)(2,1)S(1)} async-done(((bf16[8,2,16,1024]{3,2,1,0:T(8,128)(2,1)}), bf16[8,2,16,1024]{3,2,1,0:T(8,128)(2,1)S(1)}, u32[]{:S(2)}, u32[]{:S(2)}) %all-to-all-start.1) | async-done | bytes 524320 | tf_op jit(solution)/shard_map/all_to_all | solution.py:44
  56.8 0.3 convolution_dynamic-update-slice_fusion.2
  57.1 0.3 convolution_dynamic-update-slice_fusion.1
  57.4 0.0 collective-permute-done.2
  57.5 0.2 convolution_dynamic-update-slice_fusion.7
  57.7 0.0 collective-permute-done.3
  57.7 0.2 convolution_dynamic-update-slice_fusion.6
  57.9 0.3 convolution_dynamic-update-slice_fusion
  58.2 1.9 %collective-permute-start.4 = (f32[128,896]{0,1:T(8,128)S(1)}, f32[128,896]{0,1:T(8,128)S(1)}, u32[]{:S(2)}, u32[]{:S(2)}) collective-permute-start(f32[128,896]{0,1:T(8,128)S(1)} %convolution_dynamic-update-slice_fusion), channel_id=1, source_target_pairs={{0,1},{1,0},{2,3},{3,2},{4,5},{5,4},{6,7},{7,6},{8,9},{9,8},{10,11... | collective-permute-start | bytes 1376264 | tf_op jit(solution)/shard_map/ppermute | solution.py:56
  60.2 0.3 convolution_dynamic-update-slice_fusion.5
  60.5 0.3 convolution_dynamic-update-slice_fusion.4
  60.8 0.2 convolution_dynamic-update-slice_fusion.9
  61.0 0.2 convolution_dynamic-update-slice_fusion.8
  61.2 0.3 convolution_dynamic-update-slice_fusion.3
  61.5 0.4 collective-permute-done.4
  61.9 0.1 add_convert_fusion
  62.0 0.2 copy.23
  62.2 0.8 reshape.85
  63.0 8.2 %all-to-all-start.2 = ((bf16[64,2,896]{2,1,0:T(2,128)(2,1)}), bf16[64,2,896]{2,1,0:T(2,128)(2,1)S(1)}, u32[]{:S(2)}, u32[]{:S(2)}) async-start(bf16[64,2,896]{2,1,0:T(2,128)(2,1)} %reshape.85), calls=%async_computation.2 | async-start | bytes 458752 | tf_op jit(solution)/shard_map/all_to_all | solution.py:58
  71.3 14.6 %all-to-all-done.2 = bf16[64,2,896]{2,1,0:T(2,128)(2,1)S(1)} async-done(((bf16[64,2,896]{2,1,0:T(2,128)(2,1)}), bf16[64,2,896]{2,1,0:T(2,128)(2,1)S(1)}, u32[]{:S(2)}, u32[]{:S(2)}) %all-to-all-start.2) | async-done | bytes 229408 | tf_op jit(solution)/shard_map/all_to_all | solution.py:58
  85.8 0.3 reshape.86
  86.1 0.1 reduce_sum.22
  86.3 0.6 gather_fusion
  86.9 0.1 select_bitcast_fusion
  86.9 0.7 reshape.87
  (10 shorter events, 0.2 us)
Async XLA Ops:
  0.0 22.0 %copy-start = (bf16[8,512,128]{2,1,0:T(8,128)(2,1)S(1)}, bf16[8,512,128]{2,1,0:T(8,128)(2,1)}, u32[]{:S(2)}) copy-start(bf16[8,512,128]{2,1,0:T(8,128)(2,1)} %param.8) | copy-start | bytes 3145732
  0.0 1.8 %copy-start.2 = (bf16[2,256,576]{1,2,0:T(8,128)(2,1)S(1)}, bf16[2,256,576]{1,2,0:T(8,128)(2,1)}, u32[]{:S(2)}) copy-start(bf16[2,256,576]{1,2,0:T(8,128)(2,1)} %param.6) | copy-start | bytes 1769476
  2.4 8.2 %copy-start.1 = (bf16[1024,224]{0,1:T(8,128)(2,1)S(1)}, bf16[1024,224]{0,1:T(8,128)(2,1)}, u32[]{:S(2)}) copy-start(bf16[1024,224]{0,1:T(8,128)(2,1)} %param.9) | copy-start | bytes 1376260
  3.3 18.4 %all-to-all-start = ((bf16[2,128,512]{2,0,1:T(2,128)(2,1)}), bf16[2,128,512]{2,0,1:T(2,128)(2,1)S(1)}, u32[]{:S(2)}, u32[]{:S(2)}) async-start(bf16[2,128,512]{2,0,1:T(2,128)(2,1)} %copy.18), calls=%async_computation | async-start | bytes 524288 | tf_op jit(solution)/shard_map/all_to_all | solution.py:36
  10.6 14.7 %collective-permute-start = (bf16[1024,224]{0,1:T(8,128)(2,1)S(1)}, bf16[1024,224]{0,1:T(8,128)(2,1)S(1)}, u32[]{:S(2)}, u32[]{:S(2)}) collective-permute-start(bf16[1024,224]{0,1:T(8,128)(2,1)S(1)} %copy-done.1), channel_id=1, source_target_pairs={{0,128},{128,256},{256,384},{384,0},{1,129},{129,257},{257,385},{3... | collective-permute-start | bytes 1376264 | tf_op jit(solution)/shard_map/ppermute | solution.py:33
  14.6 15.5 %collective-permute-start.1 = (bf16[1024,224]{0,1:T(8,128)(2,1)S(1)}, bf16[1024,224]{0,1:T(8,128)(2,1)S(1)}, u32[]{:S(2)}, u32[]{:S(2)}) collective-permute-start(bf16[1024,224]{0,1:T(8,128)(2,1)S(1)} %copy-done.1), channel_id=1, source_target_pairs={{0,384},{128,0},{256,128},{384,256},{1,385},{129,1},{257,129},{385... | collective-permute-start | bytes 1376264 | tf_op jit(solution)/shard_map/ppermute | solution.py:34
  31.1 25.7 %all-to-all-start.1 = ((bf16[8,2,16,1024]{3,2,1,0:T(8,128)(2,1)}), bf16[8,2,16,1024]{3,2,1,0:T(8,128)(2,1)S(1)}, u32[]{:S(2)}, u32[]{:S(2)}) async-start(bf16[8,2,16,1024]{3,2,1,0:T(8,128)(2,1)} %broadcast_in_dim.25), calls=%async_computation.1 | async-start | bytes 1048576 | tf_op jit(solution)/shard_map/all_to_all | solution.py:44
  40.5 16.9 %collective-permute-start.2 = (bf16[1024,112]{0,1:T(8,128)(2,1)}, bf16[1024,112]{0,1:T(8,128)(2,1)S(1)}, u32[]{:S(2)}, u32[]{:S(2)}) collective-permute-start(bf16[1024,112]{0,1:T(8,128)(2,1)} %slice.11), channel_id=1, source_target_pairs={{0,128},{128,256},{256,384},{384,0},{1,129},{129,257},{257,385},{3... | collective-permute-start | bytes 688136 | tf_op jit(solution)/shard_map/ppermute | solution.py:41
  43.4 14.3 %collective-permute-start.3 = (bf16[1024,112]{0,1:T(8,128)(2,1)}, bf16[1024,112]{0,1:T(8,128)(2,1)S(1)}, u32[]{:S(2)}, u32[]{:S(2)}) collective-permute-start(bf16[1024,112]{0,1:T(8,128)(2,1)} %slice.12), channel_id=1, source_target_pairs={{0,384},{128,0},{256,128},{384,256},{1,385},{129,1},{257,129},{385... | collective-permute-start | bytes 688136 | tf_op jit(solution)/shard_map/ppermute | solution.py:42
  58.2 3.7 %collective-permute-start.4 = (f32[128,896]{0,1:T(8,128)S(1)}, f32[128,896]{0,1:T(8,128)S(1)}, u32[]{:S(2)}, u32[]{:S(2)}) collective-permute-start(f32[128,896]{0,1:T(8,128)S(1)} %convolution_dynamic-update-slice_fusion), channel_id=1, source_target_pairs={{0,1},{1,0},{2,3},{3,2},{4,5},{5,4},{6,7},{7,6},{8,9},{9,8},{10,11... | collective-permute-start | bytes 1376264 | tf_op jit(solution)/shard_map/ppermute | solution.py:56
  63.0 22.9 %all-to-all-start.2 = ((bf16[64,2,896]{2,1,0:T(2,128)(2,1)}), bf16[64,2,896]{2,1,0:T(2,128)(2,1)S(1)}, u32[]{:S(2)}, u32[]{:S(2)}) async-start(bf16[64,2,896]{2,1,0:T(2,128)(2,1)} %reshape.85), calls=%async_computation.2 | async-start | bytes 458752 | tf_op jit(solution)/shard_map/all_to_all | solution.py:58

commit v4 on v3

--- a/solution.py
+++ b/solution.py
@@ -27,20 +27,23 @@
     nx, nz, ny, nc = (lax.axis_size(a) for a in ("x", "z", "y", "c"))
     x, c = lax.axis_index("x"), lax.axis_index("c")
     requests = queries.shape[0]
+    weight = output_weight.T
     ahead = [(i, (i + 1) % nx) for i in range(nx)]
     back = [(i, (i - 1) % nx) for i in range(nx)]
-    half = output_weight.shape[1] // 2
-    previous = lax.ppermute(output_weight, "x", ahead)
-    following = lax.ppermute(output_weight, "x", back)
+    n = weight.shape[0]
+    half, rest = n // 2, 2 * n // 7
+    first = n - rest
+    previous = lax.ppermute(weight[:first], "x", ahead)
+    following = lax.ppermute(weight[rest:], "x", back)
     latent = attend(queries, latent_cache, lengths, value_weight.shape[1])
     swapped = lax.all_to_all(latent, ("y", "c"), split_axis=1, concat_axis=0, tiled=True)
     values = jnp.einsum("qhd,hde->qhe", swapped, value_weight, preferred_element_type=f32)
     values = values.astype(bf16).reshape(ny, nc, requests, -1)
     values = values.transpose(1, 0, 2, 3).reshape(nc, ny * requests, -1)
     values, previous, following = lax.optimization_barrier((values, previous, following))
-    low = lax.ppermute(previous[:, :half], "x", ahead)
-    high = lax.ppermute(following[:, half:], "x", back)
-    blocks = [output_weight, previous, low, high, following]
+    low = lax.ppermute(jnp.concatenate([weight[first:], previous[:half]]), "x", ahead)
+    high = lax.ppermute(jnp.concatenate([following[half - rest :], weight[:rest]]), "x", back)
+    blocks = [weight, previous, low, high, following]
     everyone = lax.all_to_all(
         jnp.broadcast_to(values[None], (nz, *values.shape)), "z", split_axis=0, concat_axis=0, tiled=True
     )
@@ -49,7 +52,7 @@
         rows = lax.dynamic_index_in_dim(everyone, core, 1, keepdims=False)
         rows = rows.reshape(nz * ny * requests, -1)
         return jnp.concatenate(
-            [jnp.dot(rows, w, preferred_element_type=f32) for w in blocks], axis=1
+            [jnp.einsum("rk,nk->rn", rows, w, preferred_element_type=f32) for w in blocks], axis=1
         )
 
     theirs = product(1 - c)
@@ -57,10 +60,14 @@
     summed = (product(c) + received).astype(bf16).reshape(nz * ny, requests, -1)
     parts = lax.all_to_all(summed, ("z", "y"), split_axis=0, concat_axis=0, tiled=True)
     parts = parts.reshape(nz, ny, requests, nx, -1).astype(f32)
-    total = jnp.sum(parts, axis=1).astype(bf16)
-    order = jnp.mod(x - jnp.arange(nx), nx)
-    total = jnp.take(total, order, axis=2)
-    return total.transpose(1, 2, 0, 3).reshape(requests, -1)
+    total = parts[:, 0]
+    for i in range(1, ny):
+        total = total + parts[:, i]
+    total = total.astype(bf16).transpose(2, 1, 0, 3)
+    total = jnp.concatenate([total[:1], total[:0:-1]])
+    total = jnp.concatenate([total, total])
+    total = lax.dynamic_slice_in_dim(total, jnp.mod(-x, nx), nx, 0)
+    return total.transpose(1, 0, 2, 3).reshape(requests, -1)
 
 
 def solution(mesh):

time: 88.2 us -> 90 us (1.020)
  the two profiles are of different devices: /device:TPU:6 before, /device:TPU:8 now
where the time goes in v4:
time: 90 us; the launch traced here: 89.5 us
  starting transfers between devices  43.2 us (48%)
  waiting for transfers between devices  33.3 us (37%)
  local copies, waits for them, and re-layouts  5.5 us (6%)
  matrix products  5.03 us (6%)
  other arithmetic  2.03 us (2%)
    all_to_all x1, waiting for transfers between devices, local(): lax.all_to_all(summed, ('z', 'y'), split_axis=0, concat_axis=0, tiled=True)  14 us
    all_to_all x1, starting transfers between devices, local(): lax.all_to_all(jnp.broadcast_to(values[None], (nz, *values.shape)), 'z',...  10.3 us
    all_to_all x1, starting transfers between devices, local(): lax.all_to_all(summed, ('z', 'y'), split_axis=0, concat_axis=0, tiled=True)  10.2 us
    all_to_all x1, waiting for transfers between devices, local(): lax.all_to_all(jnp.broadcast_to(values[None], (nz, *values.shape)), 'z',...  9.23 us
    all_to_all x1, starting transfers between devices, local(): lax.all_to_all(latent, ('y', 'c'), split_axis=1, concat_axis=0, tiled=True)  9.15 us
    ppermute x1, waiting for transfers between devices, local(): previous = lax.ppermute(weight[:first], 'x', ahead)  4.02 us
    ppermute x1, starting transfers between devices, local(): lax.ppermute(jnp.concatenate([weight[first:], previous[:half]]), 'x', ahead)  3.91 us
    all_to_all x1, waiting for transfers between devices, local(): lax.all_to_all(latent, ('y', 'c'), split_axis=1, concat_axis=0, tiled=True)  3.77 us
  transfers between devices with their start and end apart: 8, of which 6 were waited for; matrix products, arithmetic and copies ran while one was open for 5% of the time, Pallas kernels for 0%

profile of v4, /device:TPU:8, one launch (start us, length us, event | category | flops | bytes accessed | tf_op | source)
XLA Modules:
  0.0 89.5 jit_solution(18091434306818967291)
XLA Ops:
  0.0 0.0 copy-start
  0.0 0.0 copy-start.4
  0.0 1.6 %fusion.3 = f32[2,128,256]{2,1,0:T(8,128)S(1)} fusion(bf16[2,128,576]{1,2,0:T(8,128)(2,1)} %param.5, bf16[2,256,576]{1,2,0:T(8,128)(2,1)} %param.6, s32[2]{0:T(128)} %param.7), kind=kOutput, calls=%fused_computation.4 | convolution fusion | flops 75694080 | bytes 1146888 | tf_op jit(solution)/shard_map/rhe,rje->rhj/dot_general | solution.py:14
  1.6 0.2 fusion.16
  1.8 0.0 copy-done.4
  1.8 0.5 fusion.5
  2.4 0.0 copy-start.1
  2.4 1.0 %copy.21 = bf16[2,128,512]{2,0,1:T(2,128)(2,1)} copy(bf16[2,128,512]{2,1,0:T(8,128)(2,1)S(1)} %slice.123) | data formatting | bytes 524288 | tf_op jit(solution)/shard_map/slice | solution.py:23
  3.3 9.1 %all-to-all-start = ((bf16[2,128,512]{2,0,1:T(2,128)(2,1)}), bf16[2,128,512]{2,0,1:T(2,128)(2,1)S(1)}, u32[]{:S(2)}, u32[]{:S(2)}) async-start(bf16[2,128,512]{2,0,1:T(2,128)(2,1)} %copy.21), calls=%async_computation | async-start | bytes 524288 | tf_op jit(solution)/shard_map/all_to_all | solution.py:39
  12.5 0.0 copy-done.1
  12.5 0.1 fusion.15
  12.6 3.1 %collective-permute-start.1 = (bf16[160,1024]{1,0:T(8,128)(2,1)S(1)}, bf16[160,1024]{1,0:T(8,128)(2,1)S(1)}, u32[]{:S(2)}, u32[]{:S(2)}) collective-permute-start(bf16[160,1024]{1,0:T(8,128)(2,1)S(1)} %get-tuple-element.15), channel_id=1, source_target_pairs={{0,384},{128,0},{256,128},{384,256},{1,385},{129,1},{257,129},{385... | collective-permute-start | bytes 983048 | tf_op jit(solution)/shard_map/ppermute | solution.py:37
  15.7 2.8 %collective-permute-start = (bf16[160,1024]{1,0:T(8,128)(2,1)S(1)}, bf16[160,1024]{1,0:T(8,128)(2,1)S(1)}, u32[]{:S(2)}, u32[]{:S(2)}) collective-permute-start(bf16[160,1024]{1,0:T(8,128)(2,1)S(1)} %get-tuple-element.16), channel_id=1, source_target_pairs={{0,128},{128,256},{256,384},{384,0},{1,129},{129,257},{257,385},{3... | collective-permute-start | bytes 983048 | tf_op jit(solution)/shard_map/ppermute | solution.py:36
  18.4 3.8 %all-to-all-done = bf16[2,128,512]{2,0,1:T(2,128)(2,1)S(1)} async-done(((bf16[2,128,512]{2,0,1:T(2,128)(2,1)}), bf16[2,128,512]{2,0,1:T(2,128)(2,1)S(1)}, u32[]{:S(2)}, u32[]{:S(2)}) %all-to-all-start) | async-done | bytes 262176 | tf_op jit(solution)/shard_map/all_to_all | solution.py:39
  22.2 0.2 copy.29
  22.4 0.1 all_to_all.22
  22.5 0.0 copy-done
  22.5 0.3 fusion.4
  22.9 0.1 copy.24
  22.9 1.3 %collective-permute-done.1 = bf16[160,1024]{1,0:T(8,128)(2,1)S(1)} collective-permute-done((bf16[160,1024]{1,0:T(8,128)(2,1)S(1)}, bf16[160,1024]{1,0:T(8,128)(2,1)S(1)}, u32[]{:S(2)}, u32[]{:S(2)}) %collective-permute-start.1) | collective-permute-done | bytes 327712 | tf_op jit(solution)/shard_map/ppermute | solution.py:37
  24.2 4.0 %collective-permute-done = bf16[160,1024]{1,0:T(8,128)(2,1)S(1)} collective-permute-done((bf16[160,1024]{1,0:T(8,128)(2,1)S(1)}, bf16[160,1024]{1,0:T(8,128)(2,1)S(1)}, u32[]{:S(2)}, u32[]{:S(2)}) %collective-permute-start) | collective-permute-done | bytes 327712 | tf_op jit(solution)/shard_map/ppermute | solution.py:36
  28.3 0.0 copy-start.2
  28.3 0.9 %broadcast_in_dim.7 = bf16[8,2,16,1024]{3,2,1,0:T(8,128)(2,1)} broadcast(bf16[2,16,1024]{2,1,0:T(8,128)(2,1)S(1)} %copy.25), dimensions={1,2,3} | broadcast | bytes 589824 | tf_op jit(solution)/shard_map/broadcast_in_dim | solution.py:48
  29.2 10.3 %all-to-all-start.1 = ((bf16[8,2,16,1024]{3,2,1,0:T(8,128)(2,1)}), bf16[8,2,16,1024]{3,2,1,0:T(8,128)(2,1)S(1)}, u32[]{:S(2)}, u32[]{:S(2)}) async-start(bf16[8,2,16,1024]{3,2,1,0:T(8,128)(2,1)} %broadcast_in_dim.7), calls=%async_computation.1 | async-start | bytes 1048576 | tf_op jit(solution)/shard_map/all_to_all | solution.py:47
  39.5 0.0 copy-done.2
  39.5 0.0 slice-start
  39.6 0.8 pad_maximum_fusion.1
  40.3 1.9 %collective-permute-start.3 = (bf16[176,1024]{1,0:T(8,128)(2,1)}, bf16[176,1024]{1,0:T(8,128)(2,1)S(1)}, u32[]{:S(2)}, u32[]{:S(2)}) collective-permute-start(bf16[176,1024]{1,0:T(8,128)(2,1)} %pad_maximum_fusion.1), channel_id=1, source_target_pairs={{0,384},{128,0},{256,128},{384,256},{1,385},{129,1},{257,129},{385... | collective-permute-start | bytes 1081352 | tf_op jit(solution)/shard_map/ppermute | solution.py:45
  42.2 0.0 slice-done
  42.2 0.8 pad_maximum_fusion
  43.0 3.9 %collective-permute-start.2 = (bf16[176,1024]{1,0:T(8,128)(2,1)}, bf16[176,1024]{1,0:T(8,128)(2,1)S(1)}, u32[]{:S(2)}, u32[]{:S(2)}) collective-permute-start(bf16[176,1024]{1,0:T(8,128)(2,1)} %pad_maximum_fusion), channel_id=1, source_target_pairs={{0,128},{128,256},{256,384},{384,0},{1,129},{129,257},{257,385},{3... | collective-permute-start | bytes 1081352 | tf_op jit(solution)/shard_map/ppermute | solution.py:44
  46.9 9.2 %all-to-all-done.1 = bf16[8,2,16,1024]{3,2,1,0:T(8,128)(2,1)S(1)} async-done(((bf16[8,2,16,1024]{3,2,1,0:T(8,128)(2,1)}), bf16[8,2,16,1024]{3,2,1,0:T(8,128)(2,1)S(1)}, u32[]{:S(2)}, u32[]{:S(2)}) %all-to-all-start.1) | async-done | bytes 524320 | tf_op jit(solution)/shard_map/all_to_all | solution.py:47
  56.2 0.3 convolution_dynamic-update-slice_fusion.1
  56.5 0.0 copy-start.3
  56.5 0.3 convolution_dynamic-update-slice_fusion
  56.8 0.7 copy-done.3
  57.5 0.2 convolution_dynamic-update-slice_fusion.9
  57.7 0.2 convolution_dynamic-update-slice_fusion.7
  58.0 0.0 collective-permute-done.2
  58.0 0.3 convolution_dynamic-update-slice_fusion.3
  58.3 0.0 collective-permute-done.3
  58.3 0.3 convolution_dynamic-update-slice_fusion.2
  58.6 0.3 convolution_dynamic-update-slice_fusion.6
  58.8 1.9 %collective-permute-start.4 = (f32[128,896]{0,1:T(8,128)S(1)}, f32[128,896]{0,1:T(8,128)S(1)}, u32[]{:S(2)}, u32[]{:S(2)}) collective-permute-start(f32[128,896]{0,1:T(8,128)S(1)} %convolution_dynamic-update-slice_fusion.6), channel_id=1, source_target_pairs={{0,1},{1,0},{2,3},{3,2},{4,5},{5,4},{6,7},{7,6},{8,9},{9,8},{10,11... | collective-permute-start | bytes 1376264 | tf_op jit(solution)/shard_map/ppermute | solution.py:59
  60.7 0.3 convolution_dynamic-update-slice_fusion.5
  61.0 0.3 convolution_dynamic-update-slice_fusion.4
  61.3 0.3 convolution_dynamic-update-slice_fusion.8
  61.5 1.0 %collective-permute-done.4 = f32[128,896]{0,1:T(8,128)S(1)} collective-permute-done((f32[128,896]{0,1:T(8,128)S(1)}, f32[128,896]{0,1:T(8,128)S(1)}, u32[]{:S(2)}, u32[]{:S(2)}) %collective-permute-start.4) | collective-permute-done | bytes 458784 | tf_op jit(solution)/shard_map/ppermute | solution.py:59
  62.5 0.1 add_convert_fusion
  62.6 0.2 copy.26
  62.8 0.8 reshape.35
  63.6 10.2 %all-to-all-start.2 = ((bf16[64,2,896]{2,1,0:T(2,128)(2,1)}), bf16[64,2,896]{2,1,0:T(2,128)(2,1)S(1)}, u32[]{:S(2)}, u32[]{:S(2)}) async-start(bf16[64,2,896]{2,1,0:T(2,128)(2,1)} %reshape.35), calls=%async_computation.2 | async-start | bytes 458752 | tf_op jit(solution)/shard_map/all_to_all | solution.py:61
  73.8 14.0 %all-to-all-done.2 = bf16[64,2,896]{2,1,0:T(2,128)(2,1)S(1)} async-done(((bf16[64,2,896]{2,1,0:T(2,128)(2,1)}), bf16[64,2,896]{2,1,0:T(2,128)(2,1)S(1)}, u32[]{:S(2)}, u32[]{:S(2)}) %all-to-all-start.2) | async-done | bytes 229408 | tf_op jit(solution)/shard_map/all_to_all | solution.py:61
  87.8 0.5 reshape.37
  88.3 0.1 fusion.12
  88.4 0.1 rev.3
  88.6 0.2 fusion.11
  88.8 0.7 reshape.36
  (10 shorter events, 0.2 us)
Async XLA Ops:
  0.0 22.5 %copy-start = (bf16[8,512,128]{2,1,0:T(8,128)(2,1)S(1)}, bf16[8,512,128]{2,1,0:T(8,128)(2,1)}, u32[]{:S(2)}) copy-start(bf16[8,512,128]{2,1,0:T(8,128)(2,1)} %param.8) | copy-start | bytes 3145732
  0.0 1.8 %copy-start.4 = (bf16[2,256,576]{1,2,0:T(8,128)(2,1)S(1)}, bf16[2,256,576]{1,2,0:T(8,128)(2,1)}, u32[]{:S(2)}) copy-start(bf16[2,256,576]{1,2,0:T(8,128)(2,1)} %param.6) | copy-start | bytes 1769476
  2.4 10.1 %copy-start.1 = (bf16[1024,224]{0,1:T(8,128)(2,1)S(1)}, bf16[1024,224]{0,1:T(8,128)(2,1)}, u32[]{:S(2)}) copy-start(bf16[1024,224]{0,1:T(8,128)(2,1)} %param.9) | copy-start | bytes 1376260
  3.3 18.9 %all-to-all-start = ((bf16[2,128,512]{2,0,1:T(2,128)(2,1)}), bf16[2,128,512]{2,0,1:T(2,128)(2,1)S(1)}, u32[]{:S(2)}, u32[]{:S(2)}) async-start(bf16[2,128,512]{2,0,1:T(2,128)(2,1)} %copy.21), calls=%async_computation | async-start | bytes 524288 | tf_op jit(solution)/shard_map/all_to_all | solution.py:39
  12.6 11.7 %collective-permute-start.1 = (bf16[160,1024]{1,0:T(8,128)(2,1)S(1)}, bf16[160,1024]{1,0:T(8,128)(2,1)S(1)}, u32[]{:S(2)}, u32[]{:S(2)}) collective-permute-start(bf16[160,1024]{1,0:T(8,128)(2,1)S(1)} %get-tuple-element.15), channel_id=1, source_target_pairs={{0,384},{128,0},{256,128},{384,256},{1,385},{129,1},{257,129},{385... | collective-permute-start | bytes 983048 | tf_op jit(solution)/shard_map/ppermute | solution.py:37
  15.7 12.6 %collective-permute-start = (bf16[160,1024]{1,0:T(8,128)(2,1)S(1)}, bf16[160,1024]{1,0:T(8,128)(2,1)S(1)}, u32[]{:S(2)}, u32[]{:S(2)}) collective-permute-start(bf16[160,1024]{1,0:T(8,128)(2,1)S(1)} %get-tuple-element.16), channel_id=1, source_target_pairs={{0,128},{128,256},{256,384},{384,0},{1,129},{129,257},{257,385},{3... | collective-permute-start | bytes 983048 | tf_op jit(solution)/shard_map/ppermute | solution.py:36
  28.3 11.3 %copy-start.2 = (bf16[160,1024]{1,0:T(8,128)(2,1)}, bf16[160,1024]{1,0:T(8,128)(2,1)S(1)}, u32[]{:S(2)}) copy-start(bf16[160,1024]{1,0:T(8,128)(2,1)S(1)} %collective-permute-done) | copy-start | bytes 983044
  29.2 27.0 %all-to-all-start.1 = ((bf16[8,2,16,1024]{3,2,1,0:T(8,128)(2,1)}), bf16[8,2,16,1024]{3,2,1,0:T(8,128)(2,1)S(1)}, u32[]{:S(2)}, u32[]{:S(2)}) async-start(bf16[8,2,16,1024]{3,2,1,0:T(8,128)(2,1)} %broadcast_in_dim.7), calls=%async_computation.1 | async-start | bytes 1048576 | tf_op jit(solution)/shard_map/all_to_all | solution.py:47
  39.5 2.7 %slice-start = ((bf16[160,1024]{1,0:T(8,128)(2,1)}), bf16[112,1024]{1,0:T(8,128)(2,1)S(1)}, s32[]{:S(2)}) async-start(bf16[160,1024]{1,0:T(8,128)(2,1)} %copy-done.2), calls=%async_computation.3 | async-start | bytes 458752 | tf_op jit(solution)/shard_map/slice | solution.py:44
  40.3 18.0 %collective-permute-start.3 = (bf16[176,1024]{1,0:T(8,128)(2,1)}, bf16[176,1024]{1,0:T(8,128)(2,1)S(1)}, u32[]{:S(2)}, u32[]{:S(2)}) collective-permute-start(bf16[176,1024]{1,0:T(8,128)(2,1)} %pad_maximum_fusion.1), channel_id=1, source_target_pairs={{0,384},{128,0},{256,128},{384,256},{1,385},{129,1},{257,129},{385... | collective-permute-start | bytes 1081352 | tf_op jit(solution)/shard_map/ppermute | solution.py:45
  43.0 15.0 %collective-permute-start.2 = (bf16[176,1024]{1,0:T(8,128)(2,1)}, bf16[176,1024]{1,0:T(8,128)(2,1)S(1)}, u32[]{:S(2)}, u32[]{:S(2)}) collective-permute-start(bf16[176,1024]{1,0:T(8,128)(2,1)} %pad_maximum_fusion), channel_id=1, source_target_pairs={{0,128},{128,256},{256,384},{384,0},{1,129},{129,257},{257,385},{3... | collective-permute-start | bytes 1081352 | tf_op jit(solution)/shard_map/ppermute | solution.py:44
  56.5 1.0 %copy-start.3 = (bf16[160,1024]{1,0:T(8,128)(2,1)S(1)}, bf16[160,1024]{1,0:T(8,128)(2,1)}, u32[]{:S(2)}) copy-start(bf16[160,1024]{1,0:T(8,128)(2,1)} %copy-done.2) | copy-start | bytes 983044
  58.8 3.7 %collective-permute-start.4 = (f32[128,896]{0,1:T(8,128)S(1)}, f32[128,896]{0,1:T(8,128)S(1)}, u32[]{:S(2)}, u32[]{:S(2)}) collective-permute-start(f32[128,896]{0,1:T(8,128)S(1)} %convolution_dynamic-update-slice_fusion.6), channel_id=1, source_target_pairs={{0,1},{1,0},{2,3},{3,2},{4,5},{5,4},{6,7},{7,6},{8,9},{9,8},{10,11... | collective-permute-start | bytes 1376264 | tf_op jit(solution)/shard_map/ppermute | solution.py:59
  63.6 24.2 %all-to-all-start.2 = ((bf16[64,2,896]{2,1,0:T(2,128)(2,1)}), bf16[64,2,896]{2,1,0:T(2,128)(2,1)S(1)}, u32[]{:S(2)}, u32[]{:S(2)}) async-start(bf16[64,2,896]{2,1,0:T(2,128)(2,1)} %reshape.35), calls=%async_computation.2 | async-start | bytes 458752 | tf_op jit(solution)/shard_map/all_to_all | solution.py:61

commit v5 on v4

--- a/solution.py
+++ b/solution.py
@@ -27,23 +27,22 @@
     nx, nz, ny, nc = (lax.axis_size(a) for a in ("x", "z", "y", "c"))
     x, c = lax.axis_index("x"), lax.axis_index("c")
     requests = queries.shape[0]
-    weight = output_weight.T
-    ahead = [(i, (i + 1) % nx) for i in range(nx)]
-    back = [(i, (i - 1) % nx) for i in range(nx)]
-    n = weight.shape[0]
-    half, rest = n // 2, 2 * n // 7
-    first = n - rest
-    previous = lax.ppermute(weight[:first], "x", ahead)
-    following = lax.ppermute(weight[rest:], "x", back)
-    latent = attend(queries, latent_cache, lengths, value_weight.shape[1])
-    swapped = lax.all_to_all(latent, ("y", "c"), split_axis=1, concat_axis=0, tiled=True)
-    values = jnp.einsum("qhd,hde->qhe", swapped, value_weight, preferred_element_type=f32)
-    values = values.astype(bf16).reshape(ny, nc, requests, -1)
-    values = values.transpose(1, 0, 2, 3).reshape(nc, ny * requests, -1)
-    values, previous, following = lax.optimization_barrier((values, previous, following))
-    low = lax.ppermute(jnp.concatenate([weight[first:], previous[:half]]), "x", ahead)
-    high = lax.ppermute(jnp.concatenate([following[half - rest :], weight[:rest]]), "x", back)
-    blocks = [weight, previous, low, high, following]
+    others = [
+        lax.ppermute(output_weight, "x", [(i, (i + k) % nx) for i in range(nx)]) for k in range(1, nx)
+    ]
+
+    def make_values():
+        latent = attend(queries, latent_cache, lengths, value_weight.shape[1])
+        swapped = lax.all_to_all(latent, ("y", "c"), split_axis=1, concat_axis=0, tiled=True)
+        values = jnp.einsum("qhd,hde->qhe", swapped, value_weight, preferred_element_type=f32)
+        values = values.astype(bf16).reshape(ny, nc, requests, -1)
+        return values.transpose(1, 0, 2, 3).reshape(nc, ny * requests, -1)
+
+    values = lax.cond(
+        lengths[0] >= 1, make_values, lambda: jnp.zeros((nc, ny * requests, value_weight.shape[0] * value_weight.shape[2]), bf16)
+    )
+    values, others = lax.optimization_barrier((values, others))
+    blocks = [output_weight, *others]
     everyone = lax.all_to_all(
         jnp.broadcast_to(values[None], (nz, *values.shape)), "z", split_axis=0, concat_axis=0, tiled=True
     )
@@ -52,7 +51,7 @@
         rows = lax.dynamic_index_in_dim(everyone, core, 1, keepdims=False)
         rows = rows.reshape(nz * ny * requests, -1)
         return jnp.concatenate(
-            [jnp.einsum("rk,nk->rn", rows, w, preferred_element_type=f32) for w in blocks], axis=1
+            [jnp.dot(rows, w, preferred_element_type=f32) for w in blocks], axis=1
         )
 
     theirs = product(1 - c)

time: 90 us -> 91.7 us (1.019)
  the two profiles are of different devices: /device:TPU:8 before, /device:TPU:6 now
where the time goes in v5:
time: 91.7 us; the launch traced here: 90.6 us
  waiting for transfers between devices  34.7 us (38%)
  starting transfers between devices  30 us (33%)
  blocking collectives  15 us (16%)
  local copies, waits for them, and re-layouts  5.33 us (6%)
  matrix products  4.63 us (5%)
    all_to_all x1, waiting for transfers between devices, local(): lax.all_to_all(jnp.broadcast_to(values[None], (nz, *values.shape)), 'z',...  18.6 us
    all_to_all x1, blocking collectives, make_values(): lax.all_to_all(latent, ('y', 'c'), split_axis=1, concat_axis=0, tiled=True)  15 us
    all_to_all x1, waiting for transfers between devices, local(): lax.all_to_all(summed, ('z', 'y'), split_axis=0, concat_axis=0, tiled=True)  14.9 us
    ppermute x3, starting transfers between devices, local(): lax.ppermute(output_weight, 'x', [(i, (i + k) % nx) for i in range(nx)])  13 us
    all_to_all x1, starting transfers between devices, local(): lax.all_to_all(jnp.broadcast_to(values[None], (nz, *values.shape)), 'z',...  10.3 us
    all_to_all x1, starting transfers between devices, local(): lax.all_to_all(summed, ('z', 'y'), split_axis=0, concat_axis=0, tiled=True)  4.62 us
    dot_general x8, matrix products, product(): jnp.dot(rows, w, preferred_element_type=f32)  2.3 us
    ppermute x1, starting transfers between devices, local(): received = lax.ppermute(theirs, 'c', [(i, (i + 1) % nc) for i in range(nc)])  2 us
  transfers between devices with their start and end apart: 6, of which 3 were waited for; matrix products, arithmetic and copies ran while one was open for 4% of the time, Pallas kernels for 0%

profile of v5, /device:TPU:6, one launch (start us, length us, event | category | flops | bytes accessed | tf_op | source)
XLA Modules:
  0.0 90.6 jit_solution(5674176696271356239)
XLA Ops:
  0.0 2.7 %collective-permute-start.2 = (bf16[1024,224]{0,1:T(8,128)(2,1)}, bf16[1024,224]{0,1:T(8,128)(2,1)S(1)}, u32[]{:S(2)}, u32[]{:S(2)}) collective-permute-start(bf16[1024,224]{0,1:T(8,128)(2,1)} %param.11), channel_id=1, source_target_pairs={{0,384},{128,0},{256,128},{384,256},{1,385},{129,1},{257,129},{385... | collective-permute-start | bytes 1376264 | tf_op jit(solution)/shard_map/ppermute | solution.py:31
  2.7 8.4 %collective-permute-start.1 = (bf16[1024,224]{0,1:T(8,128)(2,1)}, bf16[1024,224]{0,1:T(8,128)(2,1)S(1)}, u32[]{:S(2)}, u32[]{:S(2)}) collective-permute-start(bf16[1024,224]{0,1:T(8,128)(2,1)} %param.11), channel_id=1, source_target_pairs={{0,256},{128,384},{256,0},{384,128},{1,257},{129,385},{257,1},{385... | collective-permute-start | bytes 1376264 | tf_op jit(solution)/shard_map/ppermute | solution.py:31
  11.1 1.9 %collective-permute-start = (bf16[1024,224]{0,1:T(8,128)(2,1)}, bf16[1024,224]{0,1:T(8,128)(2,1)S(1)}, u32[]{:S(2)}, u32[]{:S(2)}) collective-permute-start(bf16[1024,224]{0,1:T(8,128)(2,1)} %param.11), channel_id=1, source_target_pairs={{0,128},{128,256},{256,384},{384,0},{1,129},{129,257},{257,385},{3... | collective-permute-start | bytes 1376264 | tf_op jit(solution)/shard_map/ppermute | solution.py:31
  13.1 0.0 copy-start.3
  13.1 0.6 copy-done.3
  13.8 18.4 %conditional.1 = (bf16[2,16,1024]{2,0,1:T(2,128)(2,1)S(1)}) conditional(s32[]{:T(128)} %bitcast.5, () %tuple.12, (s32[2]{0:T(128)S(1)}, bf16[2,128,576]{1,2,0:T(8,128)(2,1)}, bf16[2,256,576]{1,2,0:T(8,128)(2,1)}, bf16[8,512,128]{2,1,0:T(8,128)(2,1)}) %tuple.18), branch_computations={%region_0.0_spmd, %region_1.4_spmd} | conditional | flops 185107200 | bytes 13502536 | solution.py:41
  13.8 0.0 copy-start.2
  13.8 1.5 %fusion.3 = f32[2,128,256]{2,1,0:T(8,128)S(1)} fusion(bf16[2,128,576]{1,2,0:T(8,128)(2,1)} %get-tuple-element.31, bf16[2,256,576]{1,2,0:T(8,128)(2,1)} %get-tuple-element.32, s32[2]{0:T(128)S(1)} %get-tuple-element.16), kind=kOutput, calls=%fused_computation.4 | convolution fusion | flops 75694080 | bytes 1146888 | tf_op jit(solution)/shard_map/cond/branch_1_fun/rhe,rje->rhj/dot_general | solution.py:14
  15.3 0.2 fusion.15
  15.5 0.0 copy-done.2
  15.5 0.5 fusion.5
  16.1 0.0 copy-start.1
  16.1 0.3 copy.28
  16.4 15.0 %all_to_all.24 = bf16[2,128,512]{2,0,1:T(2,128)(2,1)S(1)} all-to-all(bf16[2,128,512]{2,0,1:T(2,128)(2,1)S(1)} %copy.28), channel_id=1, replica_groups=mesh['x'=4,'z'=8,'y'=8,'c'=2] {'y','c'}, dimensions={1} | all-to-all | bytes 524288 | tf_op jit(solution)/shard_map/cond/branch_1_fun/all_to_all | solution.py:36
  31.4 0.2 copy.36
  31.6 0.1 all_to_all.16
  31.7 0.0 copy-done.1
  31.7 0.3 fusion.4
  32.1 0.1 copy.31
  32.1 0.0 collective-permute-done.2
  32.1 0.0 collective-permute-done.1
  32.1 0.0 collective-permute-done
  32.2 0.9 broadcast_in_dim.9
  33.0 10.3 %all-to-all-start.1 = ((bf16[8,2,16,1024]{3,2,1,0:T(8,128)(2,1)}), bf16[8,2,16,1024]{3,2,1,0:T(8,128)(2,1)S(1)}, u32[]{:S(2)}, u32[]{:S(2)}) async-start(bf16[8,2,16,1024]{3,2,1,0:T(8,128)(2,1)} %broadcast_in_dim.9), calls=%async_computation.1 | async-start | bytes 1048576 | tf_op jit(solution)/shard_map/all_to_all | solution.py:46
  43.4 18.6 %all-to-all-done.1 = bf16[8,2,16,1024]{3,2,1,0:T(8,128)(2,1)S(1)} async-done(((bf16[8,2,16,1024]{3,2,1,0:T(8,128)(2,1)}), bf16[8,2,16,1024]{3,2,1,0:T(8,128)(2,1)S(1)}, u32[]{:S(2)}, u32[]{:S(2)}) %all-to-all-start.1) | async-done | bytes 524320 | tf_op jit(solution)/shard_map/all_to_all | solution.py:46
  62.0 0.3 fusion.23
  62.3 0.3 fusion.19
  62.6 0.3 fusion.22
  62.9 0.0 copy-start
  62.9 0.3 fusion.18
  63.2 0.7 copy-done
  64.0 0.3 fusion.20
  64.3 0.3 fusion.21
  64.6 2.0 %collective-permute-start.3 = (f32[128,896]{0,1:T(8,128)S(1)}, f32[128,896]{0,1:T(8,128)S(1)}, u32[]{:S(2)}, u32[]{:S(2)}) collective-permute-start(f32[128,896]{0,1:T(8,128)S(1)} %pad_maximum_fusion), channel_id=1, source_target_pairs={{0,1},{1,0},{2,3},{3,2},{4,5},{5,4},{6,7},{7,6},{8,9},{9,8},{10,11... | collective-permute-start | bytes 1376264 | tf_op jit(solution)/shard_map/ppermute | solution.py:58
  66.6 0.3 fusion.17
  66.9 0.3 fusion.16
  67.2 1.1 %collective-permute-done.3 = f32[128,896]{0,1:T(8,128)S(1)} collective-permute-done((f32[128,896]{0,1:T(8,128)S(1)}, f32[128,896]{0,1:T(8,128)S(1)}, u32[]{:S(2)}, u32[]{:S(2)}) %collective-permute-start.3) | collective-permute-done | bytes 458784 | tf_op jit(solution)/shard_map/ppermute | solution.py:58
  68.4 0.2 copy.33
  68.5 0.8 reshape.37
  69.3 4.6 %all-to-all-start.2 = ((bf16[64,2,896]{2,1,0:T(2,128)(2,1)}), bf16[64,2,896]{2,1,0:T(2,128)(2,1)S(1)}, u32[]{:S(2)}, u32[]{:S(2)}) async-start(bf16[64,2,896]{2,1,0:T(2,128)(2,1)} %reshape.37), calls=%async_computation.2 | async-start | bytes 458752 | tf_op jit(solution)/shard_map/all_to_all | solution.py:60
  74.0 14.9 %all-to-all-done.2 = bf16[64,2,896]{2,1,0:T(2,128)(2,1)S(1)} async-done(((bf16[64,2,896]{2,1,0:T(2,128)(2,1)}), bf16[64,2,896]{2,1,0:T(2,128)(2,1)S(1)}, u32[]{:S(2)}, u32[]{:S(2)}) %all-to-all-start.2) | async-done | bytes 229408 | tf_op jit(solution)/shard_map/all_to_all | solution.py:60
  88.9 0.5 reshape.40
  89.4 0.1 fusion.14
  89.5 0.1 rev.3
  89.6 0.2 fusion.13
  89.8 0.7 reshape.38
  (10 shorter events, 0.3 us)
Async XLA Ops:
  0.0 32.1 %collective-permute-start.2 = (bf16[1024,224]{0,1:T(8,128)(2,1)}, bf16[1024,224]{0,1:T(8,128)(2,1)S(1)}, u32[]{:S(2)}, u32[]{:S(2)}) collective-permute-start(bf16[1024,224]{0,1:T(8,128)(2,1)} %param.11), channel_id=1, source_target_pairs={{0,384},{128,0},{256,128},{384,256},{1,385},{129,1},{257,129},{385... | collective-permute-start | bytes 1376264 | tf_op jit(solution)/shard_map/ppermute | solution.py:31
  2.7 29.4 %collective-permute-start.1 = (bf16[1024,224]{0,1:T(8,128)(2,1)}, bf16[1024,224]{0,1:T(8,128)(2,1)S(1)}, u32[]{:S(2)}, u32[]{:S(2)}) collective-permute-start(bf16[1024,224]{0,1:T(8,128)(2,1)} %param.11), channel_id=1, source_target_pairs={{0,256},{128,384},{256,0},{384,128},{1,257},{129,385},{257,1},{385... | collective-permute-start | bytes 1376264 | tf_op jit(solution)/shard_map/ppermute | solution.py:31
  11.1 21.0 %collective-permute-start = (bf16[1024,224]{0,1:T(8,128)(2,1)}, bf16[1024,224]{0,1:T(8,128)(2,1)S(1)}, u32[]{:S(2)}, u32[]{:S(2)}) collective-permute-start(bf16[1024,224]{0,1:T(8,128)(2,1)} %param.11), channel_id=1, source_target_pairs={{0,128},{128,256},{256,384},{384,0},{1,129},{129,257},{257,385},{3... | collective-permute-start | bytes 1376264 | tf_op jit(solution)/shard_map/ppermute | solution.py:31
  13.1 0.7 copy-start.3
  13.8 1.7 %copy-start.2 = (bf16[2,256,576]{1,2,0:T(8,128)(2,1)S(1)}, bf16[2,256,576]{1,2,0:T(8,128)(2,1)}, u32[]{:S(2)}) copy-start(bf16[2,256,576]{1,2,0:T(8,128)(2,1)} %get-tuple-element.32) | copy-start | bytes 1769476 | tf_op jit(solution)/shard_map/cond
  16.1 15.6 %copy-start.1 = (bf16[8,512,128]{2,1,0:T(8,128)(2,1)S(1)}, bf16[8,512,128]{2,1,0:T(8,128)(2,1)}, u32[]{:S(2)}) copy-start(bf16[8,512,128]{2,1,0:T(8,128)(2,1)} %get-tuple-element.33) | copy-start | bytes 3145732 | tf_op jit(solution)/shard_map/cond
  33.0 29.0 %all-to-all-start.1 = ((bf16[8,2,16,1024]{3,2,1,0:T(8,128)(2,1)}), bf16[8,2,16,1024]{3,2,1,0:T(8,128)(2,1)S(1)}, u32[]{:S(2)}, u32[]{:S(2)}) async-start(bf16[8,2,16,1024]{3,2,1,0:T(8,128)(2,1)} %broadcast_in_dim.9), calls=%async_computation.1 | async-start | bytes 1048576 | tf_op jit(solution)/shard_map/all_to_all | solution.py:46
  62.9 1.0 %copy-start = (bf16[1024,224]{0,1:T(8,128)(2,1)S(1)}, bf16[1024,224]{0,1:T(8,128)(2,1)}, u32[]{:S(2)}) copy-start(bf16[1024,224]{0,1:T(8,128)(2,1)} %param.11) | copy-start | bytes 1376260
  64.6 3.7 %collective-permute-start.3 = (f32[128,896]{0,1:T(8,128)S(1)}, f32[128,896]{0,1:T(8,128)S(1)}, u32[]{:S(2)}, u32[]{:S(2)}) collective-permute-start(f32[128,896]{0,1:T(8,128)S(1)} %pad_maximum_fusion), channel_id=1, source_target_pairs={{0,1},{1,0},{2,3},{3,2},{4,5},{5,4},{6,7},{7,6},{8,9},{9,8},{10,11... | collective-permute-start | bytes 1376264 | tf_op jit(solution)/shard_map/ppermute | solution.py:58
  69.3 19.6 %all-to-all-start.2 = ((bf16[64,2,896]{2,1,0:T(2,128)(2,1)}), bf16[64,2,896]{2,1,0:T(2,128)(2,1)S(1)}, u32[]{:S(2)}, u32[]{:S(2)}) async-start(bf16[64,2,896]{2,1,0:T(2,128)(2,1)} %reshape.37), calls=%async_computation.2 | async-start | bytes 458752 | tf_op jit(solution)/shard_map/all_to_all | solution.py:60

commit v6 on v5

--- a/solution.py
+++ b/solution.py
@@ -30,22 +30,22 @@
     others = [
         lax.ppermute(output_weight, "x", [(i, (i + k) % nx) for i in range(nx)]) for k in range(1, nx)
     ]
+    latent = attend(queries, latent_cache, lengths, value_weight.shape[1])
+    swapped = lax.all_to_all(latent, ("y", "c"), split_axis=1, concat_axis=0, tiled=True)
 
-    def make_values():
-        latent = attend(queries, latent_cache, lengths, value_weight.shape[1])
-        swapped = lax.all_to_all(latent, ("y", "c"), split_axis=1, concat_axis=0, tiled=True)
+    def gather_values():
         values = jnp.einsum("qhd,hde->qhe", swapped, value_weight, preferred_element_type=f32)
         values = values.astype(bf16).reshape(ny, nc, requests, -1)
-        return values.transpose(1, 0, 2, 3).reshape(nc, ny * requests, -1)
+        values = values.transpose(1, 0, 2, 3).reshape(nc, ny * requests, -1)
+        values = jnp.broadcast_to(values[None], (nz, *values.shape))
+        return lax.all_to_all(values, "z", split_axis=0, concat_axis=0, tiled=True)
 
-    values = lax.cond(
-        lengths[0] >= 1, make_values, lambda: jnp.zeros((nc, ny * requests, value_weight.shape[0] * value_weight.shape[2]), bf16)
+    width = value_weight.shape[0] * value_weight.shape[2]
+    everyone = lax.cond(
+        lengths[0] >= 1, gather_values, lambda: jnp.zeros((nz, nc, ny * requests, width), bf16)
     )
-    values, others = lax.optimization_barrier((values, others))
+    everyone, others = lax.optimization_barrier((everyone, others))
     blocks = [output_weight, *others]
-    everyone = lax.all_to_all(
-        jnp.broadcast_to(values[None], (nz, *values.shape)), "z", split_axis=0, concat_axis=0, tiled=True
-    )
 
     def product(core):
         rows = lax.dynamic_index_in_dim(everyone, core, 1, keepdims=False)

time: 91.7 us -> 83.2 us (0.907)
  waiting for transfers between devices: 34.7 us -> 16.4 us
  blocking collectives: 15 us -> 28.7 us
  starting transfers between devices: 30 us -> 24.8 us
  matrix products: 4.63 us -> 5.63 us
    all_to_all x1, waiting for transfers between devices: 18.6 us -> 0.67 us  [local(): lax.all_to_all(latent, ('y', 'c'), split_axis=1, concat_axis=0, tiled=True)]
    all_to_all x1, blocking collectives: 15 us -> 28.7 us  [gather_values(): return lax.all_to_all(values, 'z', split_axis=0, concat_axis=0, tiled=True)]
    ppermute x3, starting transfers between devices: 13 us -> 9.76 us  [local(): lax.ppermute(output_weight, 'x', [(i, (i + k) % nx) for i in range(nx)])]
    all_to_all x1, starting transfers between devices: 10.3 us -> 7.21 us  [local(): lax.all_to_all(latent, ('y', 'c'), split_axis=1, concat_axis=0, tiled=True)]
    dot_general x1, matrix products: 0.27 us -> 1.49 us  [gather_values(): jnp.einsum('qhd,hde->qhe', swapped, value_weight, preferred_element_type=...]
    all_to_all x1, starting transfers between devices: 4.62 us -> 5.83 us  [local(): lax.all_to_all(summed, ('z', 'y'), split_axis=0, concat_axis=0, tiled=True)]
  transfers between devices with their start and end apart: 6 -> 6, of which waited for: 3 -> 3; matrix products, arithmetic and copies ran while one was open for 4% -> 3% of each run, Pallas kernels for 0% -> 0%
where the time goes in v6:
time: 83.2 us; the launch traced here: 82 us
  blocking collectives  28.7 us (34%)
  starting transfers between devices  24.8 us (30%)
  waiting for transfers between devices  16.4 us (20%)
  matrix products  5.63 us (7%)
  local copies, waits for them, and re-layouts  5.57 us (7%)
    all_to_all x1, blocking collectives, gather_values(): return lax.all_to_all(values, 'z', split_axis=0, concat_axis=0, tiled=True)  28.7 us
    all_to_all x1, waiting for transfers between devices, local(): lax.all_to_all(summed, ('z', 'y'), split_axis=0, concat_axis=0, tiled=True)  14.6 us
    ppermute x3, starting transfers between devices, local(): lax.ppermute(output_weight, 'x', [(i, (i + k) % nx) for i in range(nx)])  9.76 us
    all_to_all x1, starting transfers between devices, local(): lax.all_to_all(latent, ('y', 'c'), split_axis=1, concat_axis=0, tiled=True)  7.21 us
    all_to_all x1, starting transfers between devices, local(): lax.all_to_all(summed, ('z', 'y'), split_axis=0, concat_axis=0, tiled=True)  5.83 us
    dot_general x8, matrix products, product(): jnp.dot(rows, w, preferred_element_type=f32)  2.32 us
    ppermute x1, starting transfers between devices, local(): received = lax.ppermute(theirs, 'c', [(i, (i + 1) % nc) for i in range(nc)])  2 us
    unnamed x6, local copies, waits for them, and re-layouts  1.72 us
  transfers between devices with their start and end apart: 6, of which 3 were waited for; matrix products, arithmetic and copies ran while one was open for 3% of the time, Pallas kernels for 0%

profile of v6, /device:TPU:6, one launch (start us, length us, event | category | flops | bytes accessed | tf_op | source)
XLA Modules:
  0.0 82.0 jit_solution(11050829175982675636)
XLA Ops:
  0.0 0.0 copy-start
  0.0 1.1 %copy-done = bf16[2,256,576]{1,2,0:T(8,128)(2,1)S(1)} copy-done((bf16[2,256,576]{1,2,0:T(8,128)(2,1)S(1)}, bf16[2,256,576]{1,2,0:T(8,128)(2,1)}, u32[]{:S(2)}) %copy-start) | copy-done | bytes 589848
  1.1 1.3 %fusion.4 = f32[2,128,256]{2,1,0:T(8,128)S(1)} fusion(bf16[2,128,576]{1,2,0:T(8,128)(2,1)} %param.7, bf16[2,256,576]{1,2,0:T(8,128)(2,1)S(1)} %copy-done, s32[2]{0:T(128)} %param.9), kind=kOutput, calls=%fused_computation.6 | convolution fusion | flops 75694080 | bytes 1146888 | tf_op jit(solution)/shard_map/rhe,rje->rhj/dot_general | solution.py:14
  2.3 0.2 fusion.15
  2.5 0.5 fusion.6
  3.1 0.0 copy-start.1
  3.1 1.0 %copy.29 = bf16[2,128,512]{2,0,1:T(2,128)(2,1)} copy(bf16[2,128,512]{2,1,0:T(8,128)(2,1)S(1)} %slice.99) | data formatting | bytes 524288 | tf_op jit(solution)/shard_map/slice | solution.py:23
  4.1 7.2 %all-to-all-start.1 = ((bf16[2,128,512]{2,0,1:T(2,128)(2,1)}), bf16[2,128,512]{2,0,1:T(2,128)(2,1)S(1)}, u32[]{:S(2)}, u32[]{:S(2)}) async-start(bf16[2,128,512]{2,0,1:T(2,128)(2,1)} %copy.29), calls=%async_computation.1 | async-start | bytes 524288 | tf_op jit(solution)/shard_map/all_to_all | solution.py:34
  11.3 0.0 copy-done.1
  11.3 2.7 %collective-permute-start.2 = (bf16[1024,224]{0,1:T(8,128)(2,1)S(1)}, bf16[1024,224]{0,1:T(8,128)(2,1)S(1)}, u32[]{:S(2)}, u32[]{:S(2)}) collective-permute-start(bf16[1024,224]{0,1:T(8,128)(2,1)S(1)} %copy-done.1), channel_id=1, source_target_pairs={{0,384},{128,0},{256,128},{384,256},{1,385},{129,1},{257,129},{385... | collective-permute-start | bytes 1376264 | tf_op jit(solution)/shard_map/ppermute | solution.py:31
  14.1 4.7 %collective-permute-start.1 = (bf16[1024,224]{0,1:T(8,128)(2,1)S(1)}, bf16[1024,224]{0,1:T(8,128)(2,1)S(1)}, u32[]{:S(2)}, u32[]{:S(2)}) collective-permute-start(bf16[1024,224]{0,1:T(8,128)(2,1)S(1)} %copy-done.1), channel_id=1, source_target_pairs={{0,256},{128,384},{256,0},{384,128},{1,257},{129,385},{257,1},{385... | collective-permute-start | bytes 1376264 | tf_op jit(solution)/shard_map/ppermute | solution.py:31
  18.8 2.3 %collective-permute-start = (bf16[1024,224]{0,1:T(8,128)(2,1)S(1)}, bf16[1024,224]{0,1:T(8,128)(2,1)S(1)}, u32[]{:S(2)}, u32[]{:S(2)}) collective-permute-start(bf16[1024,224]{0,1:T(8,128)(2,1)S(1)} %copy-done.1), channel_id=1, source_target_pairs={{0,128},{128,256},{256,384},{384,0},{1,129},{129,257},{257,385},{3... | collective-permute-start | bytes 1376264 | tf_op jit(solution)/shard_map/ppermute | solution.py:31
  21.1 0.0 copy-start.2
  21.1 0.6 copy-done.2
  21.8 0.7 all-to-all-done.1
  22.5 0.2 copy.34
  22.7 30.6 %conditional.1 = (bf16[8,2,16,1024]{3,2,1,0:T(8,128)(2,1)S(1)}) conditional(s32[]{:T(128)} %bitcast.3, () %tuple.12, (bf16[8,512,128]{2,1,0:T(8,128)(2,1)}, bf16[16,2,8,512]{3,1,0,2:T(2,128)(2,1)S(1)}) %tuple.18), branch_computations={%region_2.3_spmd, %region_3.4_spmd} | conditional | flops 33587200 | bytes 4063240 | solution.py:44
  22.7 0.1 all_to_all.24
  22.8 1.5 %fusion = bf16[32,8,128]{2,0,1:T(8,128)(2,1)S(1)} fusion(bf16[32,8,512]{2,0,1:T(8,128)(2,1)S(1)} %all_to_all.24, bf16[8,512,128]{2,1,0:T(8,128)(2,1)} %get-tuple-element.24), kind=kOutput, calls=%fused_computation.1 | convolution fusion | flops 33587200 | bytes 1376256 | tf_op jit(solution)/shard_map/cond/branch_1_fun/qhd,hde->qhe/dot_general | solution.py:37
  24.4 0.1 copy.27
  24.5 0.1 broadcast_in_dim.6
  24.5 28.7 %all_to_all.28 = bf16[8,2,16,1024]{3,2,1,0:T(8,128)(2,1)S(1)} all-to-all(bf16[8,2,16,1024]{3,2,1,0:T(8,128)(2,1)S(1)} %broadcast_in_dim.6), channel_id=1, replica_groups=mesh['x'=4,'z'=8,'y'=8,'c'=2] {'z'}, dimensions={0} | all-to-all | bytes 1048576 | tf_op jit(solution)/shard_map/cond/branch_1_fun/all_to_all | solution.py:41
  53.2 0.0 collective-permute-done.2
  53.2 0.0 collective-permute-done.1
  53.2 0.0 collective-permute-done
  53.3 0.3 fusion.23
  53.6 0.3 fusion.19
  53.9 0.3 fusion.22
  54.2 0.3 fusion.18
  54.5 0.3 fusion.20
  54.8 0.3 fusion.21
  55.1 2.0 %collective-permute-start.3 = (f32[128,896]{0,1:T(8,128)S(1)}, f32[128,896]{0,1:T(8,128)S(1)}, u32[]{:S(2)}, u32[]{:S(2)}) collective-permute-start(f32[128,896]{0,1:T(8,128)S(1)} %pad_maximum_fusion), channel_id=1, source_target_pairs={{0,1},{1,0},{2,3},{3,2},{4,5},{5,4},{6,7},{7,6},{8,9},{9,8},{10,11... | collective-permute-start | bytes 1376264 | tf_op jit(solution)/shard_map/ppermute | solution.py:58
  57.1 0.3 fusion.17
  57.4 0.3 fusion.16
  57.7 1.1 %collective-permute-done.3 = f32[128,896]{0,1:T(8,128)S(1)} collective-permute-done((f32[128,896]{0,1:T(8,128)S(1)}, f32[128,896]{0,1:T(8,128)S(1)}, u32[]{:S(2)}, u32[]{:S(2)}) %collective-permute-start.3) | collective-permute-done | bytes 458784 | tf_op jit(solution)/shard_map/ppermute | solution.py:58
  58.9 0.2 copy.31
  59.1 0.8 reshape.35
  59.8 5.8 %all-to-all-start.2 = ((bf16[64,2,896]{2,1,0:T(2,128)(2,1)}), bf16[64,2,896]{2,1,0:T(2,128)(2,1)S(1)}, u32[]{:S(2)}, u32[]{:S(2)}) async-start(bf16[64,2,896]{2,1,0:T(2,128)(2,1)} %reshape.35), calls=%async_computation.2 | async-start | bytes 458752 | tf_op jit(solution)/shard_map/all_to_all | solution.py:60
  65.7 14.6 %all-to-all-done.2 = bf16[64,2,896]{2,1,0:T(2,128)(2,1)S(1)} async-done(((bf16[64,2,896]{2,1,0:T(2,128)(2,1)}), bf16[64,2,896]{2,1,0:T(2,128)(2,1)S(1)}, u32[]{:S(2)}, u32[]{:S(2)}) %all-to-all-start.2) | async-done | bytes 229408 | tf_op jit(solution)/shard_map/all_to_all | solution.py:60
  80.3 0.5 reshape.38
  80.8 0.1 fusion.13
  80.9 0.1 rev.3
  81.1 0.2 fusion.12
  81.3 0.7 reshape.36
  (10 shorter events, 0.3 us)
Async XLA Ops:
  0.0 1.1 %copy-start = (bf16[2,256,576]{1,2,0:T(8,128)(2,1)S(1)}, bf16[2,256,576]{1,2,0:T(8,128)(2,1)}, u32[]{:S(2)}) copy-start(bf16[2,256,576]{1,2,0:T(8,128)(2,1)} %param.8) | copy-start | bytes 1769476
  3.1 8.2 %copy-start.1 = (bf16[1024,224]{0,1:T(8,128)(2,1)S(1)}, bf16[1024,224]{0,1:T(8,128)(2,1)}, u32[]{:S(2)}) copy-start(bf16[1024,224]{0,1:T(8,128)(2,1)} %param.11) | copy-start | bytes 1376260
  4.1 18.4 %all-to-all-start.1 = ((bf16[2,128,512]{2,0,1:T(2,128)(2,1)}), bf16[2,128,512]{2,0,1:T(2,128)(2,1)S(1)}, u32[]{:S(2)}, u32[]{:S(2)}) async-start(bf16[2,128,512]{2,0,1:T(2,128)(2,1)} %copy.29), calls=%async_computation.1 | async-start | bytes 524288 | tf_op jit(solution)/shard_map/all_to_all | solution.py:34
  11.3 41.9 %collective-permute-start.2 = (bf16[1024,224]{0,1:T(8,128)(2,1)S(1)}, bf16[1024,224]{0,1:T(8,128)(2,1)S(1)}, u32[]{:S(2)}, u32[]{:S(2)}) collective-permute-start(bf16[1024,224]{0,1:T(8,128)(2,1)S(1)} %copy-done.1), channel_id=1, source_target_pairs={{0,384},{128,0},{256,128},{384,256},{1,385},{129,1},{257,129},{385... | collective-permute-start | bytes 1376264 | tf_op jit(solution)/shard_map/ppermute | solution.py:31
  14.1 39.2 %collective-permute-start.1 = (bf16[1024,224]{0,1:T(8,128)(2,1)S(1)}, bf16[1024,224]{0,1:T(8,128)(2,1)S(1)}, u32[]{:S(2)}, u32[]{:S(2)}) collective-permute-start(bf16[1024,224]{0,1:T(8,128)(2,1)S(1)} %copy-done.1), channel_id=1, source_target_pairs={{0,256},{128,384},{256,0},{384,128},{1,257},{129,385},{257,1},{385... | collective-permute-start | bytes 1376264 | tf_op jit(solution)/shard_map/ppermute | solution.py:31
  18.8 34.4 %collective-permute-start = (bf16[1024,224]{0,1:T(8,128)(2,1)S(1)}, bf16[1024,224]{0,1:T(8,128)(2,1)S(1)}, u32[]{:S(2)}, u32[]{:S(2)}) collective-permute-start(bf16[1024,224]{0,1:T(8,128)(2,1)S(1)} %copy-done.1), channel_id=1, source_target_pairs={{0,128},{128,256},{256,384},{384,0},{1,129},{129,257},{257,385},{3... | collective-permute-start | bytes 1376264 | tf_op jit(solution)/shard_map/ppermute | solution.py:31
  21.1 0.7 copy-start.2
  55.1 3.7 %collective-permute-start.3 = (f32[128,896]{0,1:T(8,128)S(1)}, f32[128,896]{0,1:T(8,128)S(1)}, u32[]{:S(2)}, u32[]{:S(2)}) collective-permute-start(f32[128,896]{0,1:T(8,128)S(1)} %pad_maximum_fusion), channel_id=1, source_target_pairs={{0,1},{1,0},{2,3},{3,2},{4,5},{5,4},{6,7},{7,6},{8,9},{9,8},{10,11... | collective-permute-start | bytes 1376264 | tf_op jit(solution)/shard_map/ppermute | solution.py:58
  59.8 20.5 %all-to-all-start.2 = ((bf16[64,2,896]{2,1,0:T(2,128)(2,1)}), bf16[64,2,896]{2,1,0:T(2,128)(2,1)S(1)}, u32[]{:S(2)}, u32[]{:S(2)}) async-start(bf16[64,2,896]{2,1,0:T(2,128)(2,1)} %reshape.35), calls=%async_computation.2 | async-start | bytes 458752 | tf_op jit(solution)/shard_map/all_to_all | solution.py:60

commit v7 on v2

v7 whole, which is shorter than its diff:
```python
import jax
import jax.numpy as jnp
from jax import lax
from jax.experimental import pallas as pl
from jax.experimental.pallas import tpu as pltpu
from jax.sharding import Mesh
from jax.sharding import PartitionSpec as P

score_scale = 192.0 ** (-0.5)
f32 = jnp.float32
bf16 = jnp.bfloat16


def attend_kernel(lengths, queries, cache, latent):
    live = lengths[pl.program_id(0)]
    keys = cache[0]
    scores = (
        lax.dot_general(queries[0], keys, (((0,), (0,)), ((), ())), preferred_element_type=f32)
        * score_scale
    )
    alive = lax.broadcasted_iota(jnp.int32, scores.shape, 1) < live
    scores = jnp.where(alive, scores, -1e30)
    powers = jnp.exp(scores - jnp.max(scores, axis=1, keepdims=True))
    weights = (powers / jnp.sum(powers, axis=1, keepdims=True)).astype(bf16)
    groups, _, heads, width = latent.shape
    mixture = lax.dot_general(
        weights, keys[:width], (((1,), (1,)), ((), ())), preferred_element_type=f32
    )
    latent[...] = mixture.reshape(groups, 1, heads, width).astype(bf16)


def attend(queries, cache, lengths, groups, width):
    requests, entries, heads = queries.shape
    slots = cache.shape[2]
    return pl.pallas_call(
        attend_kernel,
        grid_spec=pltpu.PrefetchScalarGridSpec(
            num_scalar_prefetch=1,
            grid=(requests,),
            in_specs=[
                pl.BlockSpec((1, entries, heads), lambda r, _: (r, 0, 0)),
                pl.BlockSpec((1, entries, slots), lambda r, _: (r, 0, 0)),
            ],
            out_specs=pl.BlockSpec((groups, 1, heads // groups, width), lambda r, _: (0, r, 0, 0)),
        ),
        out_shape=jax.ShapeDtypeStruct((groups, requests, heads // groups, width), bf16),
        cost_estimate=pl.CostEstimate(
            flops=2 * requests * heads * slots * (entries + width),
            transcendentals=requests * heads * slots,
            bytes_accessed=2 * requests * (entries * (heads + slots) + heads * width),
        ),
        name="attend",
    )(lengths, queries, cache)


def finish_kernel(place, parts, out):
    nz, nx = parts.shape[0], 4
    n = parts.shape[-1] // nx
    total = parts[:, 0].astype(f32)
    for i in range(1, parts.shape[1]):
        total = total + parts[:, i].astype(f32)
    columns = []
    for at in range(nx):
        k = lax.rem(place[0] + nx - at, nx)
        block = total[:, :, :n]
        for i in range(1, nx):
            block = jnp.where(k == i, total[:, :, i * n : (i + 1) * n], block)
        columns += [block[z] for z in range(nz)]
    out[...] = jnp.concatenate(columns, axis=1).astype(bf16)


def local(queries, latent_cache, lengths, value_weight, output_weight):
    nx, nz, ny, nc = (lax.axis_size(a) for a in ("x", "z", "y", "c"))
    x, c = lax.axis_index("x"), lax.axis_index("c")
    requests = queries.shape[0]
    others = [
        lax.ppermute(output_weight, "x", [(i, (i + k) % nx) for i in range(nx)]) for k in range(1, nx)
    ]
    latent = attend(
        queries.transpose(0, 2, 1), latent_cache.transpose(0, 2, 1), lengths, ny * nc, value_weight.shape[1]
    )
    swapped = lax.all_to_all(latent, ("y", "c"), split_axis=0, concat_axis=0, tiled=True)
    values = jnp.einsum("trhd,hde->trhe", swapped, value_weight, preferred_element_type=f32)
    values = values.astype(bf16).reshape(ny, nc, requests, -1)
    values = values.transpose(1, 0, 2, 3).reshape(nc, ny * requests, -1)

    def gather(values):
        values = jnp.broadcast_to(values[None], (nz, *values.shape))
        return lax.all_to_all(values, "z", split_axis=0, concat_axis=0, tiled=True)

    everyone = lax.cond(x < nx, gather, lambda v: jnp.zeros((nz, *v.shape), bf16), values)
    everyone, others = lax.optimization_barrier((everyone, others))
    blocks = [output_weight, *others]

    def product(core):
        rows = lax.dynamic_index_in_dim(everyone, core, 1, keepdims=False)
        rows = rows.reshape(nz * ny * requests, -1)
        return jnp.concatenate([jnp.dot(rows, w, preferred_element_type=f32) for w in blocks], axis=1)

    theirs = product(1 - c)
    received = lax.ppermute(theirs, "c", [(i, (i + 1) % nc) for i in range(nc)])
    summed = (product(c) + received).astype(bf16).reshape(nz * ny, requests, -1)
    summed, x = lax.optimization_barrier((summed, x))
    parts = lax.all_to_all(summed, ("z", "y"), split_axis=0, concat_axis=0, tiled=True)
    return pl.pallas_call(
        finish_kernel,
        grid_spec=pltpu.PrefetchScalarGridSpec(num_scalar_prefetch=1, grid=()),
        out_shape=jax.ShapeDtypeStruct((requests, nz * summed.shape[2]), bf16),
        name="finish",
    )(x.reshape(1), parts.reshape(nz, ny, requests, -1))


def solution(mesh):
    grid = Mesh(mesh.devices.reshape(4, 8, 8, 2), ("x", "z", "y", "c"))
    everything = ("x", "z", "y", "c")
    return jax.shard_map(
        local,
        mesh=grid,
        in_specs=(
            P(everything, None, None),
            P(everything, None, None),
            P(everything),
            P(("y", "c"), None, None),
            P(("y", "c"), ("x", "z")),
        ),
        out_specs=P(everything, None),
        check_vma=False,
    )
```

time: 90.1 us -> 80.2 us (0.89)
  blocking collectives: 18.2 us -> 48.4 us
  waiting for transfers between devices: 31.2 us -> 2.51 us
  starting transfers between devices: 30.2 us -> 19.1 us
  Pallas kernels: 0 us -> 5.63 us
  local copies, waits for them, and re-layouts: 4.13 us -> 0.49 us
  matrix products: 4.7 us -> 2.68 us
    all_to_all x1 -> x2, blocking collectives: 18.2 us -> 48.4 us  [the longest x1 28.7 us: gather(): return lax.all_to_all(values, 'z', split_axis=0, concat_axis=0, tiled=True)]
    all_to_all x2 -> x1, waiting for transfers between devices: 23.9 us -> 1.38 us  [local(): lax.all_to_all(latent, ('y', 'c'), split_axis=0, concat_axis=0, tiled=True)]
    all_to_all x2 -> x1, starting transfers between devices: 19 us -> 7.34 us  [local(): lax.all_to_all(latent, ('y', 'c'), split_axis=0, concat_axis=0, tiled=True)]
    ppermute x3, waiting for transfers between devices: 6.41 us -> 0.01 us  [local(): lax.ppermute(output_weight, 'x', [(i, (i + k) % nx) for i in range(nx)])]
    pallas_call x0 -> x2, Pallas kernels: none -> 5.63 us  [the longest x1 3.87 us: attend(): pl.pallas_call(attend_kernel, grid_spec=pltpu.PrefetchScalarGridSpec(num_...]
    dot_general x3 -> x1, matrix products: 2.38 us -> 0.36 us  [local(): jnp.einsum('trhd,hde->trhe', swapped, value_weight, preferred_element_typ...]
    reshape x2 -> x0, local copies, waits for them, and re-layouts: 1.03 us -> none  [the longest x1 0.73 us: local(): return total.transpose(1, 2, 0, 3).reshape(requests, -1)]
  transfers between devices with their start and end apart: 6 -> 5, of which waited for: 5 -> 2; matrix products, arithmetic and copies ran while one was open for 2% -> 1% of each run, Pallas kernels for 0% -> 0%
where the time goes in v7:
time: 80.2 us; the launch traced here: 79.1 us
  blocking collectives  48.4 us (60%)
  starting transfers between devices  19.1 us (24%)
  Pallas kernels  5.63 us (7%)
  matrix products  2.68 us (3%)
  waiting for transfers between devices  2.51 us (3%)
    all_to_all x1, blocking collectives, gather(): return lax.all_to_all(values, 'z', split_axis=0, concat_axis=0, tiled=True)  28.7 us
    all_to_all x1, blocking collectives, local(): lax.all_to_all(summed, ('z', 'y'), split_axis=0, concat_axis=0, tiled=True)  19.7 us
    ppermute x3, starting transfers between devices, local(): lax.ppermute(output_weight, 'x', [(i, (i + k) % nx) for i in range(nx)])  9.76 us
    all_to_all x1, starting transfers between devices, local(): lax.all_to_all(latent, ('y', 'c'), split_axis=0, concat_axis=0, tiled=True)  7.34 us
    pallas_call x1, Pallas kernels, attend(): pl.pallas_call(attend_kernel, grid_spec=pltpu.PrefetchScalarGridSpec(num_...  3.87 us
    dot_general x8, matrix products, product(): jnp.dot(rows, w, preferred_element_type=f32)  2.32 us
    ppermute x1, starting transfers between devices, local(): received = lax.ppermute(theirs, 'c', [(i, (i + 1) % nc) for i in range(nc)])  2 us
    pallas_call x1, Pallas kernels, local(): pl.pallas_call(finish_kernel, grid_spec=pltpu.PrefetchScalarGridSpec(num_...  1.75 us
  transfers between devices with their start and end apart: 5, of which 2 were waited for; matrix products, arithmetic and copies ran while one was open for 1% of the time, Pallas kernels for 0%

profile of v7, /device:TPU:6, one launch (start us, length us, event | category | flops | bytes accessed | tf_op | source)
XLA Modules:
  0.0 79.1 jit_solution(8118396677779228484)
XLA Ops:
  0.0 0.0 copy-start
  0.0 3.9 %attend.1 = bf16[16,2,8,512]{3,2,1,0:T(8,128)(2,1)} custom-call(s32[2]{0:T(128)} %lengths.1, bf16[2,576,128]{2,1,0:T(8,128)(2,1)} %bitcast.42, bf16[2,576,256]{2,1,0:T(8,128)(2,1)} %bitcast.41), custom_call_target="tpu_custom_call" | custom-call | flops 142606336 | bytes 1146880 | tf_op jit(solution)/shard_map/attend/pallas_call | solution.py:35
  3.9 0.0 copy-start.1
  3.9 7.3 %all-to-all-start.1 = ((bf16[16,2,8,512]{3,2,1,0:T(8,128)(2,1)}), bf16[16,2,8,512]{3,2,1,0:T(8,128)(2,1)S(1)}, u32[]{:S(2)}, u32[]{:S(2)}) async-start(bf16[16,2,8,512]{3,2,1,0:T(8,128)(2,1)} %attend.1), calls=%async_computation.1 | async-start | bytes 524288 | tf_op jit(solution)/shard_map/all_to_all | solution.py:82
  11.2 0.0 copy-done.1
  11.2 2.7 %collective-permute-start.2 = (bf16[1024,224]{0,1:T(8,128)(2,1)S(1)}, bf16[1024,224]{0,1:T(8,128)(2,1)S(1)}, u32[]{:S(2)}, u32[]{:S(2)}) collective-permute-start(bf16[1024,224]{0,1:T(8,128)(2,1)S(1)} %copy-done.1), channel_id=1, source_target_pairs={{0,384},{128,0},{256,128},{384,256},{1,385},{129,1},{257,129},{385... | collective-permute-start | bytes 1376264 | tf_op jit(solution)/shard_map/ppermute | solution.py:77
  14.0 4.7 %collective-permute-start.1 = (bf16[1024,224]{0,1:T(8,128)(2,1)S(1)}, bf16[1024,224]{0,1:T(8,128)(2,1)S(1)}, u32[]{:S(2)}, u32[]{:S(2)}) collective-permute-start(bf16[1024,224]{0,1:T(8,128)(2,1)S(1)} %copy-done.1), channel_id=1, source_target_pairs={{0,256},{128,384},{256,0},{384,128},{1,257},{129,385},{257,1},{385... | collective-permute-start | bytes 1376264 | tf_op jit(solution)/shard_map/ppermute | solution.py:77
  18.7 2.3 %collective-permute-start = (bf16[1024,224]{0,1:T(8,128)(2,1)S(1)}, bf16[1024,224]{0,1:T(8,128)(2,1)S(1)}, u32[]{:S(2)}, u32[]{:S(2)}) collective-permute-start(bf16[1024,224]{0,1:T(8,128)(2,1)S(1)} %copy-done.1), channel_id=1, source_target_pairs={{0,128},{128,256},{256,384},{384,0},{1,129},{129,257},{257,385},{3... | collective-permute-start | bytes 1376264 | tf_op jit(solution)/shard_map/ppermute | solution.py:77
  21.0 1.4 %all-to-all-done.1 = bf16[16,2,8,512]{3,2,1,0:T(8,128)(2,1)S(1)} async-done(((bf16[16,2,8,512]{3,2,1,0:T(8,128)(2,1)}), bf16[16,2,8,512]{3,2,1,0:T(8,128)(2,1)S(1)}, u32[]{:S(2)}, u32[]{:S(2)}) %all-to-all-start.1) | async-done | bytes 262176 | tf_op jit(solution)/shard_map/all_to_all | solution.py:82
  22.4 0.0 copy-done
  22.4 0.4 fusion
  22.8 28.9 %conditional.1 = (bf16[8,2,16,1024]{3,2,1,0:T(8,128)(2,1)S(1)}) conditional(s32[]{:T(128)} %convert_element_type.12, () %tuple.13, bf16[2,8,2,1024]{3,2,0,1:T(2,128)(2,1)S(1)} %bitcast.43), branch_computations={%region_0.0_spmd, %region_1.0_spmd} | conditional | bytes 1900552 | solution.py:91
  22.9 0.1 broadcast_in_dim.6
  23.0 28.7 %all_to_all.14 = bf16[8,2,16,1024]{3,2,1,0:T(8,128)(2,1)S(1)} all-to-all(bf16[8,2,16,1024]{3,2,1,0:T(8,128)(2,1)S(1)} %broadcast_in_dim.6), channel_id=1, replica_groups=mesh['x'=4,'z'=8,'y'=8,'c'=2] {'z'}, dimensions={0} | all-to-all | bytes 1048576 | tf_op jit(solution)/shard_map/cond/branch_1_fun/all_to_all | solution.py:89
  51.7 0.0 collective-permute-done.2
  51.7 0.0 collective-permute-done.1
  51.7 0.0 collective-permute-done
  51.8 0.3 fusion.11
  52.1 0.3 fusion.7
  52.4 0.3 fusion.10
  52.7 0.3 fusion.6
  53.0 0.3 fusion.8
  53.3 0.3 fusion.9
  53.6 2.0 %collective-permute-start.3 = (f32[128,896]{0,1:T(8,128)S(1)}, f32[128,896]{0,1:T(8,128)S(1)}, u32[]{:S(2)}, u32[]{:S(2)}) collective-permute-start(f32[128,896]{0,1:T(8,128)S(1)} %pad_maximum_fusion), channel_id=1, source_target_pairs={{0,1},{1,0},{2,3},{3,2},{4,5},{5,4},{6,7},{7,6},{8,9},{9,8},{10,11... | collective-permute-start | bytes 1376264 | tf_op jit(solution)/shard_map/ppermute | solution.py:101
  55.6 0.3 fusion.5
  55.9 0.3 fusion.4
  56.2 1.1 %collective-permute-done.3 = f32[128,896]{0,1:T(8,128)S(1)} collective-permute-done((f32[128,896]{0,1:T(8,128)S(1)}, f32[128,896]{0,1:T(8,128)S(1)}, u32[]{:S(2)}, u32[]{:S(2)}) %collective-permute-start.3) | collective-permute-done | bytes 458784 | tf_op jit(solution)/shard_map/ppermute | solution.py:101
  57.4 0.2 copy.11
  57.5 0.1 reshape.24
  57.6 19.7 %all_to_all.15 = bf16[64,2,896]{2,1,0:T(2,128)(2,1)} all-to-all(bf16[64,2,896]{2,1,0:T(2,128)(2,1)S(1)} %reshape.24), channel_id=1, replica_groups=mesh['x'=4,'z'=8,'y'=8,'c'=2] {'z','y'}, dimensions={0} | all-to-all | bytes 458752 | tf_op jit(solution)/shard_map/all_to_all | solution.py:104
  77.3 1.8 %finish.1 = bf16[2,7168]{1,0:T(2,128)(2,1)} custom-call(s32[1]{0:T(128)} %bitcast.8.place, bf16[8,8,2,896]{3,2,1,0:T(2,128)(2,1)} %bitcast.40), custom_call_target="tpu_custom_call" | custom-call | tf_op jit(solution)/shard_map/finish/pallas_call | solution.py:105
  (7 shorter events, 0.3 us)
Async XLA Ops:
  0.0 22.4 %copy-start = (bf16[8,512,128]{2,1,0:T(8,128)(2,1)S(1)}, bf16[8,512,128]{2,1,0:T(8,128)(2,1)}, u32[]{:S(2)}) copy-start(bf16[8,512,128]{2,1,0:T(8,128)(2,1)} %param.10) | copy-start | bytes 3145732
  3.9 7.4 %copy-start.1 = (bf16[1024,224]{0,1:T(8,128)(2,1)S(1)}, bf16[1024,224]{0,1:T(8,128)(2,1)}, u32[]{:S(2)}) copy-start(bf16[1024,224]{0,1:T(8,128)(2,1)} %param.11) | copy-start | bytes 1376260
  3.9 18.5 %all-to-all-start.1 = ((bf16[16,2,8,512]{3,2,1,0:T(8,128)(2,1)}), bf16[16,2,8,512]{3,2,1,0:T(8,128)(2,1)S(1)}, u32[]{:S(2)}, u32[]{:S(2)}) async-start(bf16[16,2,8,512]{3,2,1,0:T(8,128)(2,1)} %attend.1), calls=%async_computation.1 | async-start | bytes 524288 | tf_op jit(solution)/shard_map/all_to_all | solution.py:82
  11.2 40.5 %collective-permute-start.2 = (bf16[1024,224]{0,1:T(8,128)(2,1)S(1)}, bf16[1024,224]{0,1:T(8,128)(2,1)S(1)}, u32[]{:S(2)}, u32[]{:S(2)}) collective-permute-start(bf16[1024,224]{0,1:T(8,128)(2,1)S(1)} %copy-done.1), channel_id=1, source_target_pairs={{0,384},{128,0},{256,128},{384,256},{1,385},{129,1},{257,129},{385... | collective-permute-start | bytes 1376264 | tf_op jit(solution)/shard_map/ppermute | solution.py:77
  14.0 37.7 %collective-permute-start.1 = (bf16[1024,224]{0,1:T(8,128)(2,1)S(1)}, bf16[1024,224]{0,1:T(8,128)(2,1)S(1)}, u32[]{:S(2)}, u32[]{:S(2)}) collective-permute-start(bf16[1024,224]{0,1:T(8,128)(2,1)S(1)} %copy-done.1), channel_id=1, source_target_pairs={{0,256},{128,384},{256,0},{384,128},{1,257},{129,385},{257,1},{385... | collective-permute-start | bytes 1376264 | tf_op jit(solution)/shard_map/ppermute | solution.py:77
  18.7 33.0 %collective-permute-start = (bf16[1024,224]{0,1:T(8,128)(2,1)S(1)}, bf16[1024,224]{0,1:T(8,128)(2,1)S(1)}, u32[]{:S(2)}, u32[]{:S(2)}) collective-permute-start(bf16[1024,224]{0,1:T(8,128)(2,1)S(1)} %copy-done.1), channel_id=1, source_target_pairs={{0,128},{128,256},{256,384},{384,0},{1,129},{129,257},{257,385},{3... | collective-permute-start | bytes 1376264 | tf_op jit(solution)/shard_map/ppermute | solution.py:77
  53.6 3.7 %collective-permute-start.3 = (f32[128,896]{0,1:T(8,128)S(1)}, f32[128,896]{0,1:T(8,128)S(1)}, u32[]{:S(2)}, u32[]{:S(2)}) collective-permute-start(f32[128,896]{0,1:T(8,128)S(1)} %pad_maximum_fusion), channel_id=1, source_target_pairs={{0,1},{1,0},{2,3},{3,2},{4,5},{5,4},{6,7},{7,6},{8,9},{9,8},{10,11... | collective-permute-start | bytes 1376264 | tf_op jit(solution)/shard_map/ppermute | solution.py:101

commit v8 on v7

v8 whole, which is shorter than its diff:
```python
import jax
import jax.numpy as jnp
from jax import lax
from jax.experimental import pallas as pl
from jax.experimental.pallas import tpu as pltpu
from jax.sharding import Mesh
from jax.sharding import PartitionSpec as P

score_scale = 192.0 ** (-0.5)
f32 = jnp.float32
bf16 = jnp.bfloat16


def attend_kernel(lengths, queries, cache, latent, near_queries, near_cache, near_latent, arrived, left):
    requests = near_queries.shape[0]
    groups, _, heads, width = near_latent.shape
    pairs = ((queries, near_queries), (cache, near_cache))
    loads = [
        [pltpu.make_async_copy(far.at[r], near.at[r], arrived.at[i, r]) for i, (far, near) in enumerate(pairs)]
        for r in range(requests)
    ]
    for load in loads:
        for copy in load:
            copy.start()
    scores = []
    for r in range(requests):
        for copy in loads[r]:
            copy.wait()
        raw = lax.dot_general(
            near_queries[r], near_cache[r], (((0,), (0,)), ((), ())), preferred_element_type=f32
        )
        scores.append(raw * score_scale)
    stores = []
    for r in range(requests):
        alive = lax.broadcasted_iota(jnp.int32, scores[r].shape, 1) < lengths[r]
        masked = jnp.where(alive, scores[r], -1e30)
        powers = jnp.exp(masked - jnp.max(masked, axis=1, keepdims=True))
        weights = (powers / jnp.sum(powers, axis=1, keepdims=True)).astype(bf16)
        mixture = lax.dot_general(
            weights, near_cache[r, :width], (((1,), (1,)), ((), ())), preferred_element_type=f32
        )
        near_latent[:, r] = mixture.reshape(groups, heads, width).astype(bf16)
        stores.append(pltpu.make_async_copy(near_latent.at[:, r], latent.at[:, r], left.at[r]))
        stores[r].start()
    for store in stores:
        store.wait()


def attend(queries, cache, lengths, groups, width):
    requests, entries, heads = queries.shape
    slots = cache.shape[2]
    shape = (groups, requests, heads // groups, width)
    anywhere = pl.BlockSpec(memory_space=pl.ANY)
    return pl.pallas_call(
        attend_kernel,
        in_specs=[pl.BlockSpec(memory_space=pltpu.SMEM), anywhere, anywhere],
        out_specs=anywhere,
        out_shape=jax.ShapeDtypeStruct(shape, bf16),
        scratch_shapes=[
            pltpu.VMEM(queries.shape, bf16),
            pltpu.VMEM(cache.shape, bf16),
            pltpu.VMEM(shape, bf16),
            pltpu.SemaphoreType.DMA((2, requests)),
            pltpu.SemaphoreType.DMA((requests,)),
        ],
        cost_estimate=pl.CostEstimate(
            flops=2 * requests * heads * slots * (entries + width),
            transcendentals=requests * heads * slots,
            bytes_accessed=2 * requests * (entries * (heads + slots) + heads * width),
        ),
        name="attend",
    )(lengths, queries, cache)


def finish_kernel(place, total, out):
    nz, nx = total.shape[0], 4
    n = total.shape[-1] // nx
    blocks = [total[:, :, i * n : (i + 1) * n] for i in range(nx)]
    columns = []
    for at in range(nx):
        k = lax.rem(place[0] + nx - at, nx)
        block = blocks[0]
        for i in range(1, nx):
            block = jnp.where(k == i, blocks[i], block)
        columns += [block[z] for z in range(nz)]
    out[...] = jnp.concatenate(columns, axis=1).astype(bf16)


def local(queries, latent_cache, lengths, value_weight, output_weight):
    nx, nz, ny, nc = (lax.axis_size(a) for a in ("x", "z", "y", "c"))
    x, c = lax.axis_index("x"), lax.axis_index("c")
    requests = queries.shape[0]
    others = [
        lax.ppermute(output_weight, "x", [(i, (i + k) % nx) for i in range(nx)]) for k in range(1, nx)
    ]
    latent = attend(
        queries.transpose(0, 2, 1), latent_cache.transpose(0, 2, 1), lengths, ny * nc, value_weight.shape[1]
    )
    swapped = lax.all_to_all(latent, ("y", "c"), split_axis=0, concat_axis=0, tiled=True)
    values = jnp.einsum("trhd,hde->trhe", swapped, value_weight, preferred_element_type=f32)
    values = values.astype(bf16).reshape(ny, nc, requests, -1)
    values = values.transpose(1, 0, 2, 3).reshape(nc, ny * requests, -1)

    def gather(values):
        values = jnp.broadcast_to(values[None], (nz, *values.shape))
        return lax.all_to_all(values, "z", split_axis=0, concat_axis=0, tiled=True)

    everyone = lax.cond(x < nx, gather, lambda v: jnp.zeros((nz, *v.shape), bf16), values)
    everyone, others = lax.optimization_barrier((everyone, others))
    blocks = [output_weight, *others]

    def product(core):
        rows = lax.dynamic_index_in_dim(everyone, core, 1, keepdims=False)
        rows = rows.reshape(nz * ny * requests, -1)
        return jnp.concatenate([jnp.dot(rows, w, preferred_element_type=f32) for w in blocks], axis=1)

    received = lax.ppermute(product(1 - c), "c", [(i, (i + 1) % nc) for i in range(nc)])
    mine = product(c)
    summed = (mine + received).astype(bf16).reshape(nz * ny, requests, -1)
    summed, x = lax.optimization_barrier((summed, x))
    parts = lax.all_to_all(summed, ("z", "y"), split_axis=0, concat_axis=0, tiled=True)
    parts = lax.optimization_barrier(parts.astype(f32))
    total = jnp.sum(parts.reshape(nz, ny, requests, -1), axis=1)
    return pl.pallas_call(
        finish_kernel,
        in_specs=[pl.BlockSpec(memory_space=pltpu.SMEM), pl.BlockSpec(memory_space=pltpu.VMEM)],
        out_shape=jax.ShapeDtypeStruct((requests, nz * total.shape[2]), bf16),
        name="finish",
    )(x.reshape(1), total)


def solution(mesh):
    grid = Mesh(mesh.devices.reshape(4, 8, 8, 2), ("x", "z", "y", "c"))
    everything = ("x", "z", "y", "c")
    return jax.shard_map(
        local,
        mesh=grid,
        in_specs=(
            P(everything, None, None),
            P(everything, None, None),
            P(everything),
            P(("y", "c"), None, None),
            P(("y", "c"), ("x", "z")),
        ),
        out_specs=P(everything, None),
        check_vma=False,
    )
```

time: 80.2 us -> 80.6 us (level)
  other arithmetic: 0.08 us -> 0.96 us
where the time goes in v8:
time: 80.6 us; the launch traced here: 79.4 us
  blocking collectives  48.3 us (60%)
  starting transfers between devices  19.1 us (24%)
  Pallas kernels  5.16 us (6%)
  matrix products  2.67 us (3%)
  waiting for transfers between devices  2.52 us (3%)
  other arithmetic  0.96 us (1%)
    all_to_all x1, blocking collectives, gather(): return lax.all_to_all(values, 'z', split_axis=0, concat_axis=0, tiled=True)  28.7 us
    all_to_all x1, blocking collectives, local(): lax.all_to_all(summed, ('z', 'y'), split_axis=0, concat_axis=0, tiled=True)  19.6 us
    ppermute x3, starting transfers between devices, local(): lax.ppermute(output_weight, 'x', [(i, (i + k) % nx) for i in range(nx)])  9.76 us
    all_to_all x1, starting transfers between devices, local(): lax.all_to_all(latent, ('y', 'c'), split_axis=0, concat_axis=0, tiled=True)  7.35 us
    pallas_call x1, Pallas kernels, attend(): pl.pallas_call(attend_kernel, in_specs=[pl.BlockSpec(memory_space=pltpu.S...  3.4 us
    dot_general x8, matrix products, product(): jnp.dot(rows, w, preferred_element_type=f32)  2.31 us
    ppermute x1, starting transfers between devices, local(): lax.ppermute(product(1 - c), 'c', [(i, (i + 1) % nc) for i in range(nc)])  1.99 us
    pallas_call x1, Pallas kernels, local(): pl.pallas_call(finish_kernel, in_specs=[pl.BlockSpec(memory_space=pltpu.S...  1.76 us
  transfers between devices with their start and end apart: 5, of which 2 were waited for; matrix products, arithmetic and copies ran while one was open for 1% of the time, Pallas kernels for 0%

profile of v8, /device:TPU:6, one launch (start us, length us, event | category | flops | bytes accessed | tf_op | source)
XLA Modules:
  0.0 79.4 jit_solution(6329474328327815356)
XLA Ops:
  0.0 0.0 copy-start
  0.0 3.4 %attend.1 = bf16[16,2,8,512]{3,2,1,0:T(8,128)(2,1)} custom-call(s32[2]{0:T(128)} %lengths.1, bf16[2,576,128]{2,1,0:T(8,128)(2,1)} %bitcast.42, bf16[2,576,256]{2,1,0:T(8,128)(2,1)} %bitcast.41), custom_call_target="tpu_custom_call" | custom-call | flops 142606336 | bytes 1146880 | tf_op jit(solution)/shard_map/attend/pallas_call | solution.py:54
  3.4 0.0 copy-start.1
  3.4 7.4 %all-to-all-start.1 = ((bf16[16,2,8,512]{3,2,1,0:T(8,128)(2,1)}), bf16[16,2,8,512]{3,2,1,0:T(8,128)(2,1)S(1)}, u32[]{:S(2)}, u32[]{:S(2)}) async-start(bf16[16,2,8,512]{3,2,1,0:T(8,128)(2,1)} %attend.1), calls=%async_computation.1 | async-start | bytes 524288 | tf_op jit(solution)/shard_map/all_to_all | solution.py:99
  10.8 0.0 copy-done.1
  10.8 2.7 %collective-permute-start.2 = (bf16[1024,224]{0,1:T(8,128)(2,1)S(1)}, bf16[1024,224]{0,1:T(8,128)(2,1)S(1)}, u32[]{:S(2)}, u32[]{:S(2)}) collective-permute-start(bf16[1024,224]{0,1:T(8,128)(2,1)S(1)} %copy-done.1), channel_id=1, source_target_pairs={{0,384},{128,0},{256,128},{384,256},{1,385},{129,1},{257,129},{385... | collective-permute-start | bytes 1376264 | tf_op jit(solution)/shard_map/ppermute | solution.py:94
  13.5 4.7 %collective-permute-start.1 = (bf16[1024,224]{0,1:T(8,128)(2,1)S(1)}, bf16[1024,224]{0,1:T(8,128)(2,1)S(1)}, u32[]{:S(2)}, u32[]{:S(2)}) collective-permute-start(bf16[1024,224]{0,1:T(8,128)(2,1)S(1)} %copy-done.1), channel_id=1, source_target_pairs={{0,256},{128,384},{256,0},{384,128},{1,257},{129,385},{257,1},{385... | collective-permute-start | bytes 1376264 | tf_op jit(solution)/shard_map/ppermute | solution.py:94
  18.3 2.3 %collective-permute-start = (bf16[1024,224]{0,1:T(8,128)(2,1)S(1)}, bf16[1024,224]{0,1:T(8,128)(2,1)S(1)}, u32[]{:S(2)}, u32[]{:S(2)}) collective-permute-start(bf16[1024,224]{0,1:T(8,128)(2,1)S(1)} %copy-done.1), channel_id=1, source_target_pairs={{0,128},{128,256},{256,384},{384,0},{1,129},{129,257},{257,385},{3... | collective-permute-start | bytes 1376264 | tf_op jit(solution)/shard_map/ppermute | solution.py:94
  20.6 1.4 %all-to-all-done.1 = bf16[16,2,8,512]{3,2,1,0:T(8,128)(2,1)S(1)} async-done(((bf16[16,2,8,512]{3,2,1,0:T(8,128)(2,1)}), bf16[16,2,8,512]{3,2,1,0:T(8,128)(2,1)S(1)}, u32[]{:S(2)}, u32[]{:S(2)}) %all-to-all-start.1) | async-done | bytes 262176 | tf_op jit(solution)/shard_map/all_to_all | solution.py:99
  22.0 0.0 copy-done
  22.0 0.4 fusion
  22.4 28.9 %conditional.1 = (bf16[8,2,16,1024]{3,2,1,0:T(8,128)(2,1)S(1)}) conditional(s32[]{:T(128)} %convert_element_type.15, () %tuple.13, bf16[2,8,2,1024]{3,2,0,1:T(2,128)(2,1)S(1)} %bitcast.43), branch_computations={%region_0.0_spmd, %region_1.0_spmd} | conditional | bytes 1900552 | solution.py:108
  22.5 0.1 broadcast_in_dim.6
  22.5 28.7 %all_to_all.14 = bf16[8,2,16,1024]{3,2,1,0:T(8,128)(2,1)S(1)} all-to-all(bf16[8,2,16,1024]{3,2,1,0:T(8,128)(2,1)S(1)} %broadcast_in_dim.6), channel_id=1, replica_groups=mesh['x'=4,'z'=8,'y'=8,'c'=2] {'z'}, dimensions={0} | all-to-all | bytes 1048576 | tf_op jit(solution)/shard_map/cond/branch_1_fun/all_to_all | solution.py:106
  51.3 0.0 collective-permute-done.2
  51.3 0.0 collective-permute-done.1
  51.3 0.0 collective-permute-done
  51.3 0.3 fusion.11
  51.6 0.3 fusion.7
  51.9 0.3 fusion.10
  52.2 0.3 fusion.6
  52.5 0.3 fusion.8
  52.8 0.3 fusion.9
  53.2 2.0 %collective-permute-start.3 = (f32[128,896]{0,1:T(8,128)S(1)}, f32[128,896]{0,1:T(8,128)S(1)}, u32[]{:S(2)}, u32[]{:S(2)}) collective-permute-start(f32[128,896]{0,1:T(8,128)S(1)} %pad_maximum_fusion), channel_id=1, source_target_pairs={{0,1},{1,0},{2,3},{3,2},{4,5},{5,4},{6,7},{7,6},{8,9},{9,8},{10,11... | collective-permute-start | bytes 1376264 | tf_op jit(solution)/shard_map/ppermute | solution.py:117
  55.2 0.3 fusion.5
  55.4 0.3 fusion.4
  55.7 1.1 %collective-permute-done.3 = f32[128,896]{0,1:T(8,128)S(1)} collective-permute-done((f32[128,896]{0,1:T(8,128)S(1)}, f32[128,896]{0,1:T(8,128)S(1)}, u32[]{:S(2)}, u32[]{:S(2)}) %collective-permute-start.3) | collective-permute-done | bytes 458784 | tf_op jit(solution)/shard_map/ppermute | solution.py:117
  56.9 0.2 copy.10
  57.1 0.1 reshape.24
  57.2 19.6 %all_to_all.15 = bf16[64,2,896]{2,1,0:T(2,128)(2,1)S(1)} all-to-all(bf16[64,2,896]{2,1,0:T(2,128)(2,1)S(1)} %reshape.24), channel_id=1, replica_groups=mesh['x'=4,'z'=8,'y'=8,'c'=2] {'z','y'}, dimensions={0} | all-to-all | bytes 458752 | tf_op jit(solution)/shard_map/all_to_all | solution.py:121
  76.8 0.2 convert_element_type.19
  76.9 0.7 bitcast_reduce_fusion.total
  77.6 1.8 %finish.1 = bf16[2,7168]{1,0:T(2,128)(2,1)} custom-call(s32[1]{0:T(128)} %bitcast.8.place, f32[8,2,896]{2,1,0:T(2,128)} %bitcast_reduce_fusion.total), custom_call_target="tpu_custom_call" | custom-call | tf_op jit(solution)/shard_map/finish/pallas_call | solution.py:124
  (7 shorter events, 0.3 us)
Async XLA Ops:
  0.0 22.0 %copy-start = (bf16[8,512,128]{2,1,0:T(8,128)(2,1)S(1)}, bf16[8,512,128]{2,1,0:T(8,128)(2,1)}, u32[]{:S(2)}) copy-start(bf16[8,512,128]{2,1,0:T(8,128)(2,1)} %param.10) | copy-start | bytes 3145732
  3.4 7.4 %copy-start.1 = (bf16[1024,224]{0,1:T(8,128)(2,1)S(1)}, bf16[1024,224]{0,1:T(8,128)(2,1)}, u32[]{:S(2)}) copy-start(bf16[1024,224]{0,1:T(8,128)(2,1)} %param.11) | copy-start | bytes 1376260
  3.4 18.5 %all-to-all-start.1 = ((bf16[16,2,8,512]{3,2,1,0:T(8,128)(2,1)}), bf16[16,2,8,512]{3,2,1,0:T(8,128)(2,1)S(1)}, u32[]{:S(2)}, u32[]{:S(2)}) async-start(bf16[16,2,8,512]{3,2,1,0:T(8,128)(2,1)} %attend.1), calls=%async_computation.1 | async-start | bytes 524288 | tf_op jit(solution)/shard_map/all_to_all | solution.py:99
  10.8 40.5 %collective-permute-start.2 = (bf16[1024,224]{0,1:T(8,128)(2,1)S(1)}, bf16[1024,224]{0,1:T(8,128)(2,1)S(1)}, u32[]{:S(2)}, u32[]{:S(2)}) collective-permute-start(bf16[1024,224]{0,1:T(8,128)(2,1)S(1)} %copy-done.1), channel_id=1, source_target_pairs={{0,384},{128,0},{256,128},{384,256},{1,385},{129,1},{257,129},{385... | collective-permute-start | bytes 1376264 | tf_op jit(solution)/shard_map/ppermute | solution.py:94
  13.5 37.7 %collective-permute-start.1 = (bf16[1024,224]{0,1:T(8,128)(2,1)S(1)}, bf16[1024,224]{0,1:T(8,128)(2,1)S(1)}, u32[]{:S(2)}, u32[]{:S(2)}) collective-permute-start(bf16[1024,224]{0,1:T(8,128)(2,1)S(1)} %copy-done.1), channel_id=1, source_target_pairs={{0,256},{128,384},{256,0},{384,128},{1,257},{129,385},{257,1},{385... | collective-permute-start | bytes 1376264 | tf_op jit(solution)/shard_map/ppermute | solution.py:94
  18.3 33.0 %collective-permute-start = (bf16[1024,224]{0,1:T(8,128)(2,1)S(1)}, bf16[1024,224]{0,1:T(8,128)(2,1)S(1)}, u32[]{:S(2)}, u32[]{:S(2)}) collective-permute-start(bf16[1024,224]{0,1:T(8,128)(2,1)S(1)} %copy-done.1), channel_id=1, source_target_pairs={{0,128},{128,256},{256,384},{384,0},{1,129},{129,257},{257,385},{3... | collective-permute-start | bytes 1376264 | tf_op jit(solution)/shard_map/ppermute | solution.py:94
  53.2 3.7 %collective-permute-start.3 = (f32[128,896]{0,1:T(8,128)S(1)}, f32[128,896]{0,1:T(8,128)S(1)}, u32[]{:S(2)}, u32[]{:S(2)}) collective-permute-start(f32[128,896]{0,1:T(8,128)S(1)} %pad_maximum_fusion), channel_id=1, source_target_pairs={{0,1},{1,0},{2,3},{3,2},{4,5},{5,4},{6,7},{7,6},{8,9},{9,8},{10,11... | collective-permute-start | bytes 1376264 | tf_op jit(solution)/shard_map/ppermute | solution.py:117

commit v9 on v8

--- a/solution.py
+++ b/solution.py
@@ -72,20 +72,6 @@
     )(lengths, queries, cache)
 
 
-def finish_kernel(place, total, out):
-    nz, nx = total.shape[0], 4
-    n = total.shape[-1] // nx
-    blocks = [total[:, :, i * n : (i + 1) * n] for i in range(nx)]
-    columns = []
-    for at in range(nx):
-        k = lax.rem(place[0] + nx - at, nx)
-        block = blocks[0]
-        for i in range(1, nx):
-            block = jnp.where(k == i, blocks[i], block)
-        columns += [block[z] for z in range(nz)]
-    out[...] = jnp.concatenate(columns, axis=1).astype(bf16)
-
-
 def local(queries, latent_cache, lengths, value_weight, output_weight):
     nx, nz, ny, nc = (lax.axis_size(a) for a in ("x", "z", "y", "c"))
     x, c = lax.axis_index("x"), lax.axis_index("c")
@@ -109,24 +95,25 @@
     everyone, others = lax.optimization_barrier((everyone, others))
     blocks = [output_weight, *others]
 
+
     def product(core):
         rows = lax.dynamic_index_in_dim(everyone, core, 1, keepdims=False)
         rows = rows.reshape(nz * ny * requests, -1)
         return jnp.concatenate([jnp.dot(rows, w, preferred_element_type=f32) for w in blocks], axis=1)
 
     received = lax.ppermute(product(1 - c), "c", [(i, (i + 1) % nc) for i in range(nc)])
-    mine = product(c)
-    summed = (mine + received).astype(bf16).reshape(nz * ny, requests, -1)
-    summed, x = lax.optimization_barrier((summed, x))
+    summed = (product(c) + received).astype(bf16).reshape(nz * ny, requests, -1)
+    summed, turn = lax.optimization_barrier((summed, jnp.mod(nx - x, nx)))
     parts = lax.all_to_all(summed, ("z", "y"), split_axis=0, concat_axis=0, tiled=True)
-    parts = lax.optimization_barrier(parts.astype(f32))
-    total = jnp.sum(parts.reshape(nz, ny, requests, -1), axis=1)
-    return pl.pallas_call(
-        finish_kernel,
-        in_specs=[pl.BlockSpec(memory_space=pltpu.SMEM), pl.BlockSpec(memory_space=pltpu.VMEM)],
-        out_shape=jax.ShapeDtypeStruct((requests, nz * total.shape[2]), bf16),
-        name="finish",
-    )(x.reshape(1), total)
+    parts = parts.reshape(nz, ny, requests, nx, -1).astype(f32)
+    total = parts[:, 0]
+    for i in range(1, ny):
+        total = total + parts[:, i]
+    total = total.astype(bf16).transpose(1, 2, 0, 3)
+    shifted = total[:, :1], total[:, :0:-1]
+    total = jnp.concatenate([*shifted, *shifted], axis=1)
+    total = lax.dynamic_slice_in_dim(total, turn, nx, 1, allow_negative_indices=False)
+    return total.reshape(requests, -1)
 
 
 def solution(mesh):

time: 80.6 us -> 79.6 us (0.988)
  Pallas kernels: 5.16 us -> 3.41 us
  local copies, waits for them, and re-layouts: 0.49 us -> 1.91 us
    pallas_call x1 -> x0, Pallas kernels: 1.76 us -> none  [local(): pl.pallas_call(finish_kernel, in_specs=[pl.BlockSpec(memory_space=pltpu.S...]
where the time goes in v9:
time: 79.6 us; the launch traced here: 78.5 us
  blocking collectives  48.3 us (61%)
  starting transfers between devices  19.1 us (24%)
  Pallas kernels  3.41 us (4%)
  matrix products  2.66 us (3%)
  waiting for transfers between devices  2.5 us (3%)
  local copies, waits for them, and re-layouts  1.91 us (2%)
    all_to_all x1, blocking collectives, gather(): return lax.all_to_all(values, 'z', split_axis=0, concat_axis=0, tiled=True)  28.7 us
    all_to_all x1, blocking collectives, local(): lax.all_to_all(summed, ('z', 'y'), split_axis=0, concat_axis=0, tiled=True)  19.6 us
    ppermute x3, starting transfers between devices, local(): lax.ppermute(output_weight, 'x', [(i, (i + k) % nx) for i in range(nx)])  9.76 us
    all_to_all x1, starting transfers between devices, local(): lax.all_to_all(latent, ('y', 'c'), split_axis=0, concat_axis=0, tiled=True)  7.35 us
    pallas_call x1, Pallas kernels, attend(): pl.pallas_call(attend_kernel, in_specs=[pl.BlockSpec(memory_space=pltpu.S...  3.41 us
    dot_general x8, matrix products, product(): jnp.dot(rows, w, preferred_element_type=f32)  2.3 us
    ppermute x1, starting transfers between devices, local(): lax.ppermute(product(1 - c), 'c', [(i, (i + 1) % nc) for i in range(nc)])  2 us
  transfers between devices with their start and end apart: 5, of which 2 were waited for; matrix products, arithmetic and copies ran while one was open for 1% of the time, Pallas kernels for 0%

profile of v9, /device:TPU:6, one launch (start us, length us, event | category | flops | bytes accessed | tf_op | source)
XLA Modules:
  0.0 78.5 jit_solution(11266764443028837376)
XLA Ops:
  0.0 0.0 copy-start
  0.0 3.4 %attend.1 = bf16[16,2,8,512]{3,2,1,0:T(8,128)(2,1)} custom-call(s32[2]{0:T(128)} %lengths.1, bf16[2,576,128]{2,1,0:T(8,128)(2,1)} %bitcast.45, bf16[2,576,256]{2,1,0:T(8,128)(2,1)} %bitcast.44), custom_call_target="tpu_custom_call" | custom-call | flops 142606336 | bytes 1146880 | tf_op jit(solution)/shard_map/attend/pallas_call | solution.py:54
  3.4 0.0 copy-start.1
  3.4 7.4 %all-to-all-start.1 = ((bf16[16,2,8,512]{3,2,1,0:T(8,128)(2,1)}), bf16[16,2,8,512]{3,2,1,0:T(8,128)(2,1)S(1)}, u32[]{:S(2)}, u32[]{:S(2)}) async-start(bf16[16,2,8,512]{3,2,1,0:T(8,128)(2,1)} %attend.1), calls=%async_computation.1 | async-start | bytes 524288 | tf_op jit(solution)/shard_map/all_to_all | solution.py:85
  10.8 0.0 copy-done.1
  10.8 2.7 %collective-permute-start.2 = (bf16[1024,224]{0,1:T(8,128)(2,1)S(1)}, bf16[1024,224]{0,1:T(8,128)(2,1)S(1)}, u32[]{:S(2)}, u32[]{:S(2)}) collective-permute-start(bf16[1024,224]{0,1:T(8,128)(2,1)S(1)} %copy-done.1), channel_id=1, source_target_pairs={{0,384},{128,0},{256,128},{384,256},{1,385},{129,1},{257,129},{385... | collective-permute-start | bytes 1376264 | tf_op jit(solution)/shard_map/ppermute | solution.py:80
  13.5 4.7 %collective-permute-start.1 = (bf16[1024,224]{0,1:T(8,128)(2,1)S(1)}, bf16[1024,224]{0,1:T(8,128)(2,1)S(1)}, u32[]{:S(2)}, u32[]{:S(2)}) collective-permute-start(bf16[1024,224]{0,1:T(8,128)(2,1)S(1)} %copy-done.1), channel_id=1, source_target_pairs={{0,256},{128,384},{256,0},{384,128},{1,257},{129,385},{257,1},{385... | collective-permute-start | bytes 1376264 | tf_op jit(solution)/shard_map/ppermute | solution.py:80
  18.3 2.3 %collective-permute-start = (bf16[1024,224]{0,1:T(8,128)(2,1)S(1)}, bf16[1024,224]{0,1:T(8,128)(2,1)S(1)}, u32[]{:S(2)}, u32[]{:S(2)}) collective-permute-start(bf16[1024,224]{0,1:T(8,128)(2,1)S(1)} %copy-done.1), channel_id=1, source_target_pairs={{0,128},{128,256},{256,384},{384,0},{1,129},{129,257},{257,385},{3... | collective-permute-start | bytes 1376264 | tf_op jit(solution)/shard_map/ppermute | solution.py:80
  20.6 1.4 %all-to-all-done.1 = bf16[16,2,8,512]{3,2,1,0:T(8,128)(2,1)S(1)} async-done(((bf16[16,2,8,512]{3,2,1,0:T(8,128)(2,1)}), bf16[16,2,8,512]{3,2,1,0:T(8,128)(2,1)S(1)}, u32[]{:S(2)}, u32[]{:S(2)}) %all-to-all-start.1) | async-done | bytes 262176 | tf_op jit(solution)/shard_map/all_to_all | solution.py:85
  22.0 0.0 copy-done
  22.0 0.4 fusion
  22.4 28.9 %conditional.1 = (bf16[8,2,16,1024]{3,2,1,0:T(8,128)(2,1)S(1)}) conditional(s32[]{:T(128)} %convert_element_type.21, () %tuple.13, bf16[2,8,2,1024]{3,2,0,1:T(2,128)(2,1)S(1)} %bitcast.46), branch_computations={%region_0.0_spmd, %region_1.0_spmd} | conditional | bytes 1900552 | solution.py:94
  22.5 0.1 broadcast_in_dim.6
  22.6 28.7 %all_to_all.14 = bf16[8,2,16,1024]{3,2,1,0:T(8,128)(2,1)S(1)} all-to-all(bf16[8,2,16,1024]{3,2,1,0:T(8,128)(2,1)S(1)} %broadcast_in_dim.6), channel_id=1, replica_groups=mesh['x'=4,'z'=8,'y'=8,'c'=2] {'z'}, dimensions={0} | all-to-all | bytes 1048576 | tf_op jit(solution)/shard_map/cond/branch_1_fun/all_to_all | solution.py:92
  51.3 0.0 collective-permute-done.2
  51.3 0.0 collective-permute-done.1
  51.3 0.0 collective-permute-done
  51.3 0.3 fusion.16
  51.6 0.3 fusion.12
  51.9 0.3 fusion.15
  52.2 0.3 fusion.11
  52.5 0.3 fusion.13
  52.8 0.3 fusion.14
  53.2 2.0 %collective-permute-start.3 = (f32[128,896]{0,1:T(8,128)S(1)}, f32[128,896]{0,1:T(8,128)S(1)}, u32[]{:S(2)}, u32[]{:S(2)}) collective-permute-start(f32[128,896]{0,1:T(8,128)S(1)} %pad_maximum_fusion), channel_id=1, source_target_pairs={{0,1},{1,0},{2,3},{3,2},{4,5},{5,4},{6,7},{7,6},{8,9},{9,8},{10,11... | collective-permute-start | bytes 1376264 | tf_op jit(solution)/shard_map/ppermute | solution.py:104
  55.2 0.3 fusion.10
  55.5 0.3 fusion.9
  55.8 1.1 %collective-permute-done.3 = f32[128,896]{0,1:T(8,128)S(1)} collective-permute-done((f32[128,896]{0,1:T(8,128)S(1)}, f32[128,896]{0,1:T(8,128)S(1)}, u32[]{:S(2)}, u32[]{:S(2)}) %collective-permute-start.3) | collective-permute-done | bytes 458784 | tf_op jit(solution)/shard_map/ppermute | solution.py:104
  56.9 0.2 copy.18
  57.1 0.1 reshape.28
  57.2 19.6 %all_to_all.15 = bf16[64,2,896]{2,1,0:T(2,128)(2,1)S(1)} all-to-all(bf16[64,2,896]{2,1,0:T(2,128)(2,1)S(1)} %reshape.28), channel_id=1, replica_groups=mesh['x'=4,'z'=8,'y'=8,'c'=2] {'z','y'}, dimensions={0} | all-to-all | bytes 458752 | tf_op jit(solution)/shard_map/all_to_all | solution.py:107
  76.8 0.5 reshape.30
  77.3 0.1 fusion.8
  77.4 0.1 rev.3
  77.6 0.2 fusion.7
  77.8 0.7 reshape.29
  (10 shorter events, 0.3 us)
Async XLA Ops:
  0.0 22.0 %copy-start = (bf16[8,512,128]{2,1,0:T(8,128)(2,1)S(1)}, bf16[8,512,128]{2,1,0:T(8,128)(2,1)}, u32[]{:S(2)}) copy-start(bf16[8,512,128]{2,1,0:T(8,128)(2,1)} %param.10) | copy-start | bytes 3145732
  3.4 7.4 %copy-start.1 = (bf16[1024,224]{0,1:T(8,128)(2,1)S(1)}, bf16[1024,224]{0,1:T(8,128)(2,1)}, u32[]{:S(2)}) copy-start(bf16[1024,224]{0,1:T(8,128)(2,1)} %param.11) | copy-start | bytes 1376260
  3.4 18.5 %all-to-all-start.1 = ((bf16[16,2,8,512]{3,2,1,0:T(8,128)(2,1)}), bf16[16,2,8,512]{3,2,1,0:T(8,128)(2,1)S(1)}, u32[]{:S(2)}, u32[]{:S(2)}) async-start(bf16[16,2,8,512]{3,2,1,0:T(8,128)(2,1)} %attend.1), calls=%async_computation.1 | async-start | bytes 524288 | tf_op jit(solution)/shard_map/all_to_all | solution.py:85
  10.8 40.5 %collective-permute-start.2 = (bf16[1024,224]{0,1:T(8,128)(2,1)S(1)}, bf16[1024,224]{0,1:T(8,128)(2,1)S(1)}, u32[]{:S(2)}, u32[]{:S(2)}) collective-permute-start(bf16[1024,224]{0,1:T(8,128)(2,1)S(1)} %copy-done.1), channel_id=1, source_target_pairs={{0,384},{128,0},{256,128},{384,256},{1,385},{129,1},{257,129},{385... | collective-permute-start | bytes 1376264 | tf_op jit(solution)/shard_map/ppermute | solution.py:80
  13.5 37.7 %collective-permute-start.1 = (bf16[1024,224]{0,1:T(8,128)(2,1)S(1)}, bf16[1024,224]{0,1:T(8,128)(2,1)S(1)}, u32[]{:S(2)}, u32[]{:S(2)}) collective-permute-start(bf16[1024,224]{0,1:T(8,128)(2,1)S(1)} %copy-done.1), channel_id=1, source_target_pairs={{0,256},{128,384},{256,0},{384,128},{1,257},{129,385},{257,1},{385... | collective-permute-start | bytes 1376264 | tf_op jit(solution)/shard_map/ppermute | solution.py:80
  18.3 33.0 %collective-permute-start = (bf16[1024,224]{0,1:T(8,128)(2,1)S(1)}, bf16[1024,224]{0,1:T(8,128)(2,1)S(1)}, u32[]{:S(2)}, u32[]{:S(2)}) collective-permute-start(bf16[1024,224]{0,1:T(8,128)(2,1)S(1)} %copy-done.1), channel_id=1, source_target_pairs={{0,128},{128,256},{256,384},{384,0},{1,129},{129,257},{257,385},{3... | collective-permute-start | bytes 1376264 | tf_op jit(solution)/shard_map/ppermute | solution.py:80
  53.2 3.7 %collective-permute-start.3 = (f32[128,896]{0,1:T(8,128)S(1)}, f32[128,896]{0,1:T(8,128)S(1)}, u32[]{:S(2)}, u32[]{:S(2)}) collective-permute-start(f32[128,896]{0,1:T(8,128)S(1)} %pad_maximum_fusion), channel_id=1, source_target_pairs={{0,1},{1,0},{2,3},{3,2},{4,5},{5,4},{6,7},{7,6},{8,9},{9,8},{10,11... | collective-permute-start | bytes 1376264 | tf_op jit(solution)/shard_map/ppermute | solution.py:104

commit v10 on v9

--- a/solution.py
+++ b/solution.py
@@ -76,9 +76,7 @@
     nx, nz, ny, nc = (lax.axis_size(a) for a in ("x", "z", "y", "c"))
     x, c = lax.axis_index("x"), lax.axis_index("c")
     requests = queries.shape[0]
-    others = [
-        lax.ppermute(output_weight, "x", [(i, (i + k) % nx) for i in range(nx)]) for k in range(1, nx)
-    ]
+    sent = {k: lax.ppermute(output_weight, "x", [(i, (i + k) % nx) for i in range(nx)]) for k in (1, 2, 3)}
     latent = attend(
         queries.transpose(0, 2, 1), latent_cache.transpose(0, 2, 1), lengths, ny * nc, value_weight.shape[1]
     )
@@ -92,16 +90,16 @@
         return lax.all_to_all(values, "z", split_axis=0, concat_axis=0, tiled=True)
 
     everyone = lax.cond(x < nx, gather, lambda v: jnp.zeros((nz, *v.shape), bf16), values)
-    everyone, others = lax.optimization_barrier((everyone, others))
-    blocks = [output_weight, *others]
-
+    everyone, *others = lax.optimization_barrier((everyone, sent[3], sent[1], sent[2]))
+    sent = dict(zip((3,1,2), others))
+    blocks = [output_weight, *(sent[k] for k in range(1, nx))]
 
     def product(core):
         rows = lax.dynamic_index_in_dim(everyone, core, 1, keepdims=False)
         rows = rows.reshape(nz * ny * requests, -1)
         return jnp.concatenate([jnp.dot(rows, w, preferred_element_type=f32) for w in blocks], axis=1)
 
-    received = lax.ppermute(product(1 - c), "c", [(i, (i + 1) % nc) for i in range(nc)])
+    received = lax.ppermute(product(1 - c).astype(bf16), "c", [(i, (i + 1) % nc) for i in range(nc)])
     summed = (product(c) + received).astype(bf16).reshape(nz * ny, requests, -1)
     summed, turn = lax.optimization_barrier((summed, jnp.mod(nx - x, nx)))
     parts = lax.all_to_all(summed, ("z", "y"), split_axis=0, concat_axis=0, tiled=True)

time: 79.6 us -> 80.5 us (1.011)
  the two profiles are of different devices: /device:TPU:6 before, /device:TPU:8 now
where the time goes in v10:
time: 80.5 us; the launch traced here: 80.1 us
  blocking collectives  48.7 us (60%)
  starting transfers between devices  21.6 us (27%)
  Pallas kernels  3.41 us (4%)
  matrix products  2.72 us (3%)
  local copies, waits for them, and re-layouts  1.91 us (2%)
  waiting for transfers between devices  1.17 us (1%)
    all_to_all x1, blocking collectives, gather(): return lax.all_to_all(values, 'z', split_axis=0, concat_axis=0, tiled=True)  27.1 us
    all_to_all x1, blocking collectives, local(): lax.all_to_all(summed, ('z', 'y'), split_axis=0, concat_axis=0, tiled=True)  21.6 us
    ppermute x3, starting transfers between devices, local(): lax.ppermute(output_weight, 'x', [(i, (i + k) % nx) for i in range(nx)])  10.4 us
    all_to_all x1, starting transfers between devices, local(): lax.all_to_all(latent, ('y', 'c'), split_axis=0, concat_axis=0, tiled=True)  9.29 us
    pallas_call x1, Pallas kernels, attend(): pl.pallas_call(attend_kernel, in_specs=[pl.BlockSpec(memory_space=pltpu.S...  3.41 us
    dot_general x8, matrix products, product(): jnp.dot(rows, w, preferred_element_type=f32)  2.36 us
    ppermute x1, starting transfers between devices, local(): lax.ppermute(product(1 - c).astype(bf16), 'c', [(i, (i + 1) % nc) for i i...  1.92 us
  transfers between devices with their start and end apart: 5, of which 1 were waited for; matrix products, arithmetic and copies ran while one was open for 1% of the time, Pallas kernels for 0%

profile of v10, /device:TPU:8, one launch (start us, length us, event | category | flops | bytes accessed | tf_op | source)
XLA Modules:
  0.0 80.1 jit_solution(8406524368419068188)
XLA Ops:
  0.0 0.0 copy-start
  0.0 3.4 %attend.1 = bf16[16,2,8,512]{3,2,1,0:T(8,128)(2,1)} custom-call(s32[2]{0:T(128)} %lengths.1, bf16[2,576,128]{2,1,0:T(8,128)(2,1)} %bitcast.45, bf16[2,576,256]{2,1,0:T(8,128)(2,1)} %bitcast.44), custom_call_target="tpu_custom_call" | custom-call | flops 142606336 | bytes 1146880 | tf_op jit(solution)/shard_map/attend/pallas_call | solution.py:54
  3.4 0.0 copy-start.1
  3.4 9.3 %all-to-all-start.1 = ((bf16[16,2,8,512]{3,2,1,0:T(8,128)(2,1)}), bf16[16,2,8,512]{3,2,1,0:T(8,128)(2,1)S(1)}, u32[]{:S(2)}, u32[]{:S(2)}) async-start(bf16[16,2,8,512]{3,2,1,0:T(8,128)(2,1)} %attend.1), calls=%async_computation.1 | async-start | bytes 524288 | tf_op jit(solution)/shard_map/all_to_all | solution.py:83
  12.7 0.0 copy-done.1
  12.7 3.3 %collective-permute-start.2 = (bf16[1024,224]{0,1:T(8,128)(2,1)S(1)}, bf16[1024,224]{0,1:T(8,128)(2,1)S(1)}, u32[]{:S(2)}, u32[]{:S(2)}) collective-permute-start(bf16[1024,224]{0,1:T(8,128)(2,1)S(1)} %copy-done.1), channel_id=1, source_target_pairs={{0,256},{128,384},{256,0},{384,128},{1,257},{129,385},{257,1},{385... | collective-permute-start | bytes 1376264 | tf_op jit(solution)/shard_map/ppermute | solution.py:79
  16.1 2.5 %collective-permute-start.1 = (bf16[1024,224]{0,1:T(8,128)(2,1)S(1)}, bf16[1024,224]{0,1:T(8,128)(2,1)S(1)}, u32[]{:S(2)}, u32[]{:S(2)}) collective-permute-start(bf16[1024,224]{0,1:T(8,128)(2,1)S(1)} %copy-done.1), channel_id=1, source_target_pairs={{0,128},{128,256},{256,384},{384,0},{1,129},{129,257},{257,385},{3... | collective-permute-start | bytes 1376264 | tf_op jit(solution)/shard_map/ppermute | solution.py:79
  18.6 4.6 %collective-permute-start = (bf16[1024,224]{0,1:T(8,128)(2,1)S(1)}, bf16[1024,224]{0,1:T(8,128)(2,1)S(1)}, u32[]{:S(2)}, u32[]{:S(2)}) collective-permute-start(bf16[1024,224]{0,1:T(8,128)(2,1)S(1)} %copy-done.1), channel_id=1, source_target_pairs={{0,384},{128,0},{256,128},{384,256},{1,385},{129,1},{257,129},{385... | collective-permute-start | bytes 1376264 | tf_op jit(solution)/shard_map/ppermute | solution.py:79
  23.2 0.0 all-to-all-done.1
  23.2 0.0 copy-done
  23.2 0.4 fusion
  23.6 27.2 %conditional.1 = (bf16[8,2,16,1024]{3,2,1,0:T(8,128)(2,1)S(1)}) conditional(s32[]{:T(128)} %convert_element_type.25, () %tuple.13, bf16[2,8,2,1024]{3,2,0,1:T(2,128)(2,1)S(1)} %bitcast.46), branch_computations={%region_0.0_spmd, %region_1.0_spmd} | conditional | bytes 1900552 | solution.py:92
  23.7 0.1 broadcast_in_dim.6
  23.8 27.1 %all_to_all.14 = bf16[8,2,16,1024]{3,2,1,0:T(8,128)(2,1)S(1)} all-to-all(bf16[8,2,16,1024]{3,2,1,0:T(8,128)(2,1)S(1)} %broadcast_in_dim.6), channel_id=1, replica_groups=mesh['x'=4,'z'=8,'y'=8,'c'=2] {'z'}, dimensions={0} | all-to-all | bytes 1048576 | tf_op jit(solution)/shard_map/cond/branch_1_fun/all_to_all | solution.py:90
  50.9 0.0 collective-permute-done.2
  50.9 0.0 collective-permute-done.1
  50.9 0.0 collective-permute-done
  50.9 0.3 convolution_convert_fusion.1
  51.2 0.3 fusion.12
  51.5 0.3 convolution_convert_fusion.2
  51.8 0.3 fusion.11
  52.1 0.3 convolution_convert_fusion.3
  52.4 0.3 fusion.10
  52.7 0.3 convolution_convert_fusion.4
  53.1 1.9 %collective-permute-start.3 = (bf16[128,896]{0,1:T(8,128)(2,1)S(1)}, bf16[128,896]{0,1:T(8,128)(2,1)S(1)}, u32[]{:S(2)}, u32[]{:S(2)}) collective-permute-start(bf16[128,896]{0,1:T(8,128)(2,1)S(1)} %pad_maximum_fusion), channel_id=1, source_target_pairs={{0,1},{1,0},{2,3},{3,2},{4,5},{5,4},{6,7},{7,6},{8,9},{9,8},{10,11... | collective-permute-start | bytes 688136 | tf_op jit(solution)/shard_map/ppermute | solution.py:102
  55.0 0.3 fusion.9
  55.3 1.2 %collective-permute-done.3 = bf16[128,896]{0,1:T(8,128)(2,1)S(1)} collective-permute-done((bf16[128,896]{0,1:T(8,128)(2,1)S(1)}, bf16[128,896]{0,1:T(8,128)(2,1)S(1)}, u32[]{:S(2)}, u32[]{:S(2)}) %collective-permute-start.3) | collective-permute-done | bytes 229408 | tf_op jit(solution)/shard_map/ppermute | solution.py:102
  56.5 0.2 copy.18
  56.7 0.1 reshape.28
  56.8 21.6 %all_to_all.15 = bf16[64,2,896]{2,1,0:T(2,128)(2,1)S(1)} all-to-all(bf16[64,2,896]{2,1,0:T(2,128)(2,1)S(1)} %reshape.28), channel_id=1, replica_groups=mesh['x'=4,'z'=8,'y'=8,'c'=2] {'z','y'}, dimensions={0} | all-to-all | bytes 458752 | tf_op jit(solution)/shard_map/all_to_all | solution.py:105
  78.4 0.5 reshape.30
  78.9 0.1 fusion.8
  79.0 0.1 rev.3
  79.1 0.2 fusion.7
  79.3 0.7 reshape.29
  (10 shorter events, 0.3 us)
Async XLA Ops:
  0.0 23.2 %copy-start = (bf16[8,512,128]{2,1,0:T(8,128)(2,1)S(1)}, bf16[8,512,128]{2,1,0:T(8,128)(2,1)}, u32[]{:S(2)}) copy-start(bf16[8,512,128]{2,1,0:T(8,128)(2,1)} %param.10) | copy-start | bytes 3145732
  3.4 9.3 %copy-start.1 = (bf16[1024,224]{0,1:T(8,128)(2,1)S(1)}, bf16[1024,224]{0,1:T(8,128)(2,1)}, u32[]{:S(2)}) copy-start(bf16[1024,224]{0,1:T(8,128)(2,1)} %param.11) | copy-start | bytes 1376260
  3.4 19.7 %all-to-all-start.1 = ((bf16[16,2,8,512]{3,2,1,0:T(8,128)(2,1)}), bf16[16,2,8,512]{3,2,1,0:T(8,128)(2,1)S(1)}, u32[]{:S(2)}, u32[]{:S(2)}) async-start(bf16[16,2,8,512]{3,2,1,0:T(8,128)(2,1)} %attend.1), calls=%async_computation.1 | async-start | bytes 524288 | tf_op jit(solution)/shard_map/all_to_all | solution.py:83
  12.7 38.1 %collective-permute-start.2 = (bf16[1024,224]{0,1:T(8,128)(2,1)S(1)}, bf16[1024,224]{0,1:T(8,128)(2,1)S(1)}, u32[]{:S(2)}, u32[]{:S(2)}) collective-permute-start(bf16[1024,224]{0,1:T(8,128)(2,1)S(1)} %copy-done.1), channel_id=1, source_target_pairs={{0,256},{128,384},{256,0},{384,128},{1,257},{129,385},{257,1},{385... | collective-permute-start | bytes 1376264 | tf_op jit(solution)/shard_map/ppermute | solution.py:79
  16.1 34.8 %collective-permute-start.1 = (bf16[1024,224]{0,1:T(8,128)(2,1)S(1)}, bf16[1024,224]{0,1:T(8,128)(2,1)S(1)}, u32[]{:S(2)}, u32[]{:S(2)}) collective-permute-start(bf16[1024,224]{0,1:T(8,128)(2,1)S(1)} %copy-done.1), channel_id=1, source_target_pairs={{0,128},{128,256},{256,384},{384,0},{1,129},{129,257},{257,385},{3... | collective-permute-start | bytes 1376264 | tf_op jit(solution)/shard_map/ppermute | solution.py:79
  18.6 32.3 %collective-permute-start = (bf16[1024,224]{0,1:T(8,128)(2,1)S(1)}, bf16[1024,224]{0,1:T(8,128)(2,1)S(1)}, u32[]{:S(2)}, u32[]{:S(2)}) collective-permute-start(bf16[1024,224]{0,1:T(8,128)(2,1)S(1)} %copy-done.1), channel_id=1, source_target_pairs={{0,384},{128,0},{256,128},{384,256},{1,385},{129,1},{257,129},{385... | collective-permute-start | bytes 1376264 | tf_op jit(solution)/shard_map/ppermute | solution.py:79
  53.1 3.4 %collective-permute-start.3 = (bf16[128,896]{0,1:T(8,128)(2,1)S(1)}, bf16[128,896]{0,1:T(8,128)(2,1)S(1)}, u32[]{:S(2)}, u32[]{:S(2)}) collective-permute-start(bf16[128,896]{0,1:T(8,128)(2,1)S(1)} %pad_maximum_fusion), channel_id=1, source_target_pairs={{0,1},{1,0},{2,3},{3,2},{4,5},{5,4},{6,7},{7,6},{8,9},{9,8},{10,11... | collective-permute-start | bytes 688136 | tf_op jit(solution)/shard_map/ppermute | solution.py:102

commit v11 on v9

--- a/solution.py
+++ b/solution.py
@@ -2,6 +2,7 @@
 import jax.numpy as jnp
 from jax import lax
 from jax.experimental import pallas as pl
+from jax.experimental.layout import Layout, with_layout_constraint
 from jax.experimental.pallas import tpu as pltpu
 from jax.sharding import Mesh
 from jax.sharding import PartitionSpec as P
@@ -13,7 +14,7 @@
 
 def attend_kernel(lengths, queries, cache, latent, near_queries, near_cache, near_latent, arrived, left):
     requests = near_queries.shape[0]
-    groups, _, heads, width = near_latent.shape
+    cores, groups, _, heads, width = near_latent.shape
     pairs = ((queries, near_queries), (cache, near_cache))
     loads = [
         [pltpu.make_async_copy(far.at[r], near.at[r], arrived.at[i, r]) for i, (far, near) in enumerate(pairs)]
@@ -39,17 +40,19 @@
         mixture = lax.dot_general(
             weights, near_cache[r, :width], (((1,), (1,)), ((), ())), preferred_element_type=f32
         )
-        near_latent[:, r] = mixture.reshape(groups, heads, width).astype(bf16)
-        stores.append(pltpu.make_async_copy(near_latent.at[:, r], latent.at[:, r], left.at[r]))
+        mixture = mixture.reshape(groups, cores, heads, width).astype(bf16)
+        for core in range(cores):
+            near_latent[core, :, r] = mixture[:, core]
+        stores.append(pltpu.make_async_copy(near_latent.at[:, :, r], latent.at[:, :, r], left.at[r]))
         stores[r].start()
     for store in stores:
         store.wait()
 
 
-def attend(queries, cache, lengths, groups, width):
+def attend(queries, cache, lengths, groups, cores, width):
     requests, entries, heads = queries.shape
     slots = cache.shape[2]
-    shape = (groups, requests, heads // groups, width)
+    shape = (cores, groups, requests, heads // (groups * cores), width)
     anywhere = pl.BlockSpec(memory_space=pl.ANY)
     return pl.pallas_call(
         attend_kernel,
@@ -80,12 +83,13 @@
         lax.ppermute(output_weight, "x", [(i, (i + k) % nx) for i in range(nx)]) for k in range(1, nx)
     ]
     latent = attend(
-        queries.transpose(0, 2, 1), latent_cache.transpose(0, 2, 1), lengths, ny * nc, value_weight.shape[1]
+        queries.transpose(0, 2, 1), latent_cache.transpose(0, 2, 1), lengths, ny, nc, value_weight.shape[1]
     )
-    swapped = lax.all_to_all(latent, ("y", "c"), split_axis=0, concat_axis=0, tiled=True)
+    latent = latent.reshape(nc * ny, *latent.shape[2:])
+    swapped = lax.all_to_all(latent, ("c", "y"), split_axis=0, concat_axis=0, tiled=True)
+    swapped = with_layout_constraint(swapped, Layout(major_to_minor=(0, 1, 2, 3)))
     values = jnp.einsum("trhd,hde->trhe", swapped, value_weight, preferred_element_type=f32)
-    values = values.astype(bf16).reshape(ny, nc, requests, -1)
-    values = values.transpose(1, 0, 2, 3).reshape(nc, ny * requests, -1)
+    values = values.astype(bf16).reshape(nc, ny * requests, -1)
 
     def gather(values):
         values = jnp.broadcast_to(values[None], (nz, *values.shape))
@@ -102,13 +106,14 @@
         return jnp.concatenate([jnp.dot(rows, w, preferred_element_type=f32) for w in blocks], axis=1)
 
     received = lax.ppermute(product(1 - c), "c", [(i, (i + 1) % nc) for i in range(nc)])
-    summed = (product(c) + received).astype(bf16).reshape(nz * ny, requests, -1)
+    summed = (product(c) + received).astype(bf16).reshape(nz, ny, requests, -1)
+    summed = summed.transpose(1, 0, 2, 3).reshape(ny * nz, requests, -1)
     summed, turn = lax.optimization_barrier((summed, jnp.mod(nx - x, nx)))
-    parts = lax.all_to_all(summed, ("z", "y"), split_axis=0, concat_axis=0, tiled=True)
-    parts = parts.reshape(nz, ny, requests, nx, -1).astype(f32)
-    total = parts[:, 0]
+    parts = lax.all_to_all(summed, ("y", "z"), split_axis=0, concat_axis=0, tiled=True)
+    parts = parts.reshape(ny, nz, requests, nx, -1).astype(f32)
+    total = parts[0]
     for i in range(1, ny):
-        total = total + parts[:, i]
+        total = total + parts[i]
     total = total.astype(bf16).transpose(1, 2, 0, 3)
     shifted = total[:, :1], total[:, :0:-1]
     total = jnp.concatenate([*shifted, *shifted], axis=1)

time: 79.6 us -> 79.6 us (level)
    all_to_all x1, blocking collectives: 19.6 us -> 21.9 us  [local(): lax.all_to_all(summed, ('y', 'z'), split_axis=0, concat_axis=0, tiled=True)]
    all_to_all x1, blocking collectives: 28.7 us -> 27.1 us  [gather(): return lax.all_to_all(values, 'z', split_axis=0, concat_axis=0, tiled=True)]
where the time goes in v11:
time: 79.6 us; the launch traced here: 78.5 us
  blocking collectives  49 us (62%)
  starting transfers between devices  19 us (24%)
  Pallas kernels  3.41 us (4%)
  matrix products  2.68 us (3%)
  waiting for transfers between devices  1.83 us (2%)
  local copies, waits for them, and re-layouts  1.74 us (2%)
    all_to_all x1, blocking collectives, gather(): return lax.all_to_all(values, 'z', split_axis=0, concat_axis=0, tiled=True)  27.1 us
    all_to_all x1, blocking collectives, local(): lax.all_to_all(summed, ('y', 'z'), split_axis=0, concat_axis=0, tiled=True)  21.9 us
    ppermute x3, starting transfers between devices, local(): lax.ppermute(output_weight, 'x', [(i, (i + k) % nx) for i in range(nx)])  9.76 us
    all_to_all x1, starting transfers between devices, local(): lax.all_to_all(latent, ('c', 'y'), split_axis=0, concat_axis=0, tiled=True)  7.35 us
    pallas_call x1, Pallas kernels, attend(): pl.pallas_call(attend_kernel, in_specs=[pl.BlockSpec(memory_space=pltpu.S...  3.41 us
    dot_general x8, matrix products, product(): jnp.dot(rows, w, preferred_element_type=f32)  2.32 us
    ppermute x1, starting transfers between devices, local(): lax.ppermute(product(1 - c), 'c', [(i, (i + 1) % nc) for i in range(nc)])  1.92 us
  transfers between devices with their start and end apart: 5, of which 2 were waited for; matrix products, arithmetic and copies ran while one was open for 1% of the time, Pallas kernels for 0%

profile of v11, /device:TPU:6, one launch (start us, length us, event | category | flops | bytes accessed | tf_op | source)
XLA Modules:
  0.0 78.5 jit_solution(16507721465751969583)
XLA Ops:
  0.0 0.0 copy-start
  0.0 3.4 %attend.1 = bf16[2,8,2,8,512]{4,3,2,1,0:T(8,128)(2,1)} custom-call(s32[2]{0:T(128)} %lengths.1, bf16[2,576,128]{2,1,0:T(8,128)(2,1)} %bitcast.51, bf16[2,576,256]{2,1,0:T(8,128)(2,1)} %bitcast.50), custom_call_target="tpu_custom_call" | custom-call | flops 142606336 | bytes 1146880 | tf_op jit(solution)/shard_map/attend/pallas_call | solution.py:57
  3.4 0.0 copy-start.1
  3.4 7.4 %all-to-all-start.1 = ((bf16[16,2,8,512]{3,2,1,0:T(8,128)(2,1)}), bf16[16,2,8,512]{3,2,1,0:T(8,128)(2,1)S(1)}, u32[]{:S(2)}, u32[]{:S(2)}) async-start(bf16[16,2,8,512]{3,2,1,0:T(8,128)(2,1)} %bitcast.47), calls=%async_computation.1 | async-start | bytes 524288 | tf_op jit(solution)/shard_map/all_to_all | solution.py:89
  10.8 0.0 copy-done.1
  10.8 2.7 %collective-permute-start.2 = (bf16[1024,224]{0,1:T(8,128)(2,1)S(1)}, bf16[1024,224]{0,1:T(8,128)(2,1)S(1)}, u32[]{:S(2)}, u32[]{:S(2)}) collective-permute-start(bf16[1024,224]{0,1:T(8,128)(2,1)S(1)} %copy-done.1), channel_id=1, source_target_pairs={{0,384},{128,0},{256,128},{384,256},{1,385},{129,1},{257,129},{385... | collective-permute-start | bytes 1376264 | tf_op jit(solution)/shard_map/ppermute | solution.py:83
  13.5 4.7 %collective-permute-start.1 = (bf16[1024,224]{0,1:T(8,128)(2,1)S(1)}, bf16[1024,224]{0,1:T(8,128)(2,1)S(1)}, u32[]{:S(2)}, u32[]{:S(2)}) collective-permute-start(bf16[1024,224]{0,1:T(8,128)(2,1)S(1)} %copy-done.1), channel_id=1, source_target_pairs={{0,256},{128,384},{256,0},{384,128},{1,257},{129,385},{257,1},{385... | collective-permute-start | bytes 1376264 | tf_op jit(solution)/shard_map/ppermute | solution.py:83
  18.3 2.3 %collective-permute-start = (bf16[1024,224]{0,1:T(8,128)(2,1)S(1)}, bf16[1024,224]{0,1:T(8,128)(2,1)S(1)}, u32[]{:S(2)}, u32[]{:S(2)}) collective-permute-start(bf16[1024,224]{0,1:T(8,128)(2,1)S(1)} %copy-done.1), channel_id=1, source_target_pairs={{0,128},{128,256},{256,384},{384,0},{1,129},{129,257},{257,385},{3... | collective-permute-start | bytes 1376264 | tf_op jit(solution)/shard_map/ppermute | solution.py:83
  20.6 0.6 all-to-all-done.1
  21.2 0.0 copy-done
  21.2 0.4 fusion
  21.6 27.3 %conditional.1 = (bf16[8,2,16,1024]{3,2,1,0:T(8,128)(2,1)S(1)}) conditional(s32[]{:T(128)} %convert_element_type.22, () %tuple.13, bf16[16,2,8,128]{3,0,1,2:T(8,128)(2,1)S(1)} %fusion), branch_computations={%region_0.0_spmd, %region_1.0_spmd} | conditional | bytes 1900552 | solution.py:98
  21.7 0.1 broadcast_in_dim.6
  21.7 27.1 %all_to_all.14 = bf16[8,2,16,1024]{3,2,1,0:T(8,128)(2,1)S(1)} all-to-all(bf16[8,2,16,1024]{3,2,1,0:T(8,128)(2,1)S(1)} %broadcast_in_dim.6), channel_id=1, replica_groups=mesh['x'=4,'z'=8,'y'=8,'c'=2] {'z'}, dimensions={0} | all-to-all | bytes 1048576 | tf_op jit(solution)/shard_map/cond/branch_1_fun/all_to_all | solution.py:96
  48.9 0.0 collective-permute-done.2
  48.9 0.0 collective-permute-done.1
  48.9 0.0 collective-permute-done
  48.9 0.3 fusion.15
  49.2 0.3 fusion.11
  49.5 0.3 fusion.14
  49.8 0.3 fusion.10
  50.1 0.3 fusion.12
  50.4 0.3 fusion.13
  50.8 1.9 %collective-permute-start.3 = (f32[128,896]{0,1:T(8,128)S(1)}, f32[128,896]{0,1:T(8,128)S(1)}, u32[]{:S(2)}, u32[]{:S(2)}) collective-permute-start(f32[128,896]{0,1:T(8,128)S(1)} %pad_maximum_fusion), channel_id=1, source_target_pairs={{0,1},{1,0},{2,3},{3,2},{4,5},{5,4},{6,7},{7,6},{8,9},{9,8},{10,11... | collective-permute-start | bytes 1376264 | tf_op jit(solution)/shard_map/ppermute | solution.py:108
  52.7 0.3 fusion.9
  53.0 0.3 fusion.8
  53.3 1.2 %collective-permute-done.3 = f32[128,896]{0,1:T(8,128)S(1)} collective-permute-done((f32[128,896]{0,1:T(8,128)S(1)}, f32[128,896]{0,1:T(8,128)S(1)}, u32[]{:S(2)}, u32[]{:S(2)}) %collective-permute-start.3) | collective-permute-done | bytes 458784 | tf_op jit(solution)/shard_map/ppermute | solution.py:108
  54.5 0.2 copy.19
  54.7 0.1 reshape.45
  54.9 0.2 copy.21
  55.1 21.9 %all_to_all.15 = bf16[64,2,896]{2,1,0:T(2,128)(2,1)S(1)} all-to-all(bf16[64,2,896]{2,1,0:T(2,128)(2,1)S(1)} %copy.21), channel_id=1, replica_groups=mesh['x'=4,'z'=8,'y'=8,'c'=2] {'y','z'}, dimensions={0} | all-to-all | bytes 458752 | tf_op jit(solution)/shard_map/all_to_all | solution.py:112
  77.0 0.2 convert_element_type.26
  77.1 0.1 fusion.4
  77.2 0.1 reshape.54
  77.4 0.1 rev.3
  77.6 0.2 fusion.7
  77.8 0.7 reshape.47
  (10 shorter events, 0.3 us)
Async XLA Ops:
  0.0 21.2 %copy-start = (bf16[8,512,128]{2,1,0:T(8,128)(2,1)S(1)}, bf16[8,512,128]{2,1,0:T(8,128)(2,1)}, u32[]{:S(2)}) copy-start(bf16[8,512,128]{2,1,0:T(8,128)(2,1)} %param.10) | copy-start | bytes 3145732
  3.4 7.4 %copy-start.1 = (bf16[1024,224]{0,1:T(8,128)(2,1)S(1)}, bf16[1024,224]{0,1:T(8,128)(2,1)}, u32[]{:S(2)}) copy-start(bf16[1024,224]{0,1:T(8,128)(2,1)} %param.11) | copy-start | bytes 1376260
  3.4 17.8 %all-to-all-start.1 = ((bf16[16,2,8,512]{3,2,1,0:T(8,128)(2,1)}), bf16[16,2,8,512]{3,2,1,0:T(8,128)(2,1)S(1)}, u32[]{:S(2)}, u32[]{:S(2)}) async-start(bf16[16,2,8,512]{3,2,1,0:T(8,128)(2,1)} %bitcast.47), calls=%async_computation.1 | async-start | bytes 524288 | tf_op jit(solution)/shard_map/all_to_all | solution.py:89
  10.8 38.1 %collective-permute-start.2 = (bf16[1024,224]{0,1:T(8,128)(2,1)S(1)}, bf16[1024,224]{0,1:T(8,128)(2,1)S(1)}, u32[]{:S(2)}, u32[]{:S(2)}) collective-permute-start(bf16[1024,224]{0,1:T(8,128)(2,1)S(1)} %copy-done.1), channel_id=1, source_target_pairs={{0,384},{128,0},{256,128},{384,256},{1,385},{129,1},{257,129},{385... | collective-permute-start | bytes 1376264 | tf_op jit(solution)/shard_map/ppermute | solution.py:83
  13.5 35.3 %collective-permute-start.1 = (bf16[1024,224]{0,1:T(8,128)(2,1)S(1)}, bf16[1024,224]{0,1:T(8,128)(2,1)S(1)}, u32[]{:S(2)}, u32[]{:S(2)}) collective-permute-start(bf16[1024,224]{0,1:T(8,128)(2,1)S(1)} %copy-done.1), channel_id=1, source_target_pairs={{0,256},{128,384},{256,0},{384,128},{1,257},{129,385},{257,1},{385... | collective-permute-start | bytes 1376264 | tf_op jit(solution)/shard_map/ppermute | solution.py:83
  18.3 30.6 %collective-permute-start = (bf16[1024,224]{0,1:T(8,128)(2,1)S(1)}, bf16[1024,224]{0,1:T(8,128)(2,1)S(1)}, u32[]{:S(2)}, u32[]{:S(2)}) collective-permute-start(bf16[1024,224]{0,1:T(8,128)(2,1)S(1)} %copy-done.1), channel_id=1, source_target_pairs={{0,128},{128,256},{256,384},{384,0},{1,129},{129,257},{257,385},{3... | collective-permute-start | bytes 1376264 | tf_op jit(solution)/shard_map/ppermute | solution.py:83
  50.8 3.7 %collective-permute-start.3 = (f32[128,896]{0,1:T(8,128)S(1)}, f32[128,896]{0,1:T(8,128)S(1)}, u32[]{:S(2)}, u32[]{:S(2)}) collective-permute-start(f32[128,896]{0,1:T(8,128)S(1)} %pad_maximum_fusion), channel_id=1, source_target_pairs={{0,1},{1,0},{2,3},{3,2},{4,5},{5,4},{6,7},{7,6},{8,9},{9,8},{10,11... | collective-permute-start | bytes 1376264 | tf_op jit(solution)/shard_map/ppermute | solution.py:108

commit v12 on v11

--- a/solution.py
+++ b/solution.py
@@ -79,9 +79,7 @@
     nx, nz, ny, nc = (lax.axis_size(a) for a in ("x", "z", "y", "c"))
     x, c = lax.axis_index("x"), lax.axis_index("c")
     requests = queries.shape[0]
-    others = [
-        lax.ppermute(output_weight, "x", [(i, (i + k) % nx) for i in range(nx)]) for k in range(1, nx)
-    ]
+    sent = {k: lax.ppermute(output_weight, "x", [(i, (i + k) % nx) for i in range(nx)]) for k in (1, 2, 3)}
     latent = attend(
         queries.transpose(0, 2, 1), latent_cache.transpose(0, 2, 1), lengths, ny, nc, value_weight.shape[1]
     )
@@ -96,16 +94,19 @@
         return lax.all_to_all(values, "z", split_axis=0, concat_axis=0, tiled=True)
 
     everyone = lax.cond(x < nx, gather, lambda v: jnp.zeros((nz, *v.shape), bf16), values)
-    everyone, others = lax.optimization_barrier((everyone, others))
-    blocks = [output_weight, *others]
+    blocks = [output_weight, *(sent[k] for k in range(1, nx))]
 
-
-    def product(core):
+    def product(core, order=()):
         rows = lax.dynamic_index_in_dim(everyone, core, 1, keepdims=False)
         rows = rows.reshape(nz * ny * requests, -1)
-        return jnp.concatenate([jnp.dot(rows, w, preferred_element_type=f32) for w in blocks], axis=1)
+        weights, outs = dict(enumerate(blocks)), {}
+        for at, k in enumerate(order or weights):
+            if order and at > 0:
+                weights[k], outs[order[at - 1]] = lax.optimization_barrier((weights[k], outs[order[at - 1]]))
+            outs[k] = jnp.dot(rows, weights[k], preferred_element_type=f32)
+        return jnp.concatenate([outs[k] for k in weights], axis=1)
 
-    received = lax.ppermute(product(1 - c), "c", [(i, (i + 1) % nc) for i in range(nc)])
+    received = lax.ppermute(product(1 - c, (0, 2, 3, 1)), "c", [(i, (i + 1) % nc) for i in range(nc)])
     summed = (product(c) + received).astype(bf16).reshape(nz, ny, requests, -1)
     summed = summed.transpose(1, 0, 2, 3).reshape(ny * nz, requests, -1)
     summed, turn = lax.optimization_barrier((summed, jnp.mod(nx - x, nx)))

time: 79.6 us -> 79.9 us (level)
  the two profiles are of different devices: /device:TPU:6 before, /device:TPU:8 now
where the time goes in v12:
time: 79.9 us; the launch traced here: 79.5 us
  blocking collectives  47.8 us (60%)
  starting transfers between devices  21.6 us (27%)
  Pallas kernels  3.41 us (4%)
  matrix products  2.67 us (3%)
  local copies, waits for them, and re-layouts  1.73 us (2%)
  waiting for transfers between devices  1.49 us (2%)
    all_to_all x1, blocking collectives, gather(): return lax.all_to_all(values, 'z', split_axis=0, concat_axis=0, tiled=True)  26.5 us
    all_to_all x1, blocking collectives, local(): lax.all_to_all(summed, ('y', 'z'), split_axis=0, concat_axis=0, tiled=True)  21.3 us
    ppermute x3, starting transfers between devices, local(): lax.ppermute(output_weight, 'x', [(i, (i + k) % nx) for i in range(nx)])  10.4 us
    all_to_all x1, starting transfers between devices, local(): lax.all_to_all(latent, ('c', 'y'), split_axis=0, concat_axis=0, tiled=True)  9.29 us
    pallas_call x1, Pallas kernels, attend(): pl.pallas_call(attend_kernel, in_specs=[pl.BlockSpec(memory_space=pltpu.S...  3.41 us
    dot_general x8, matrix products, product(): outs[k] = jnp.dot(rows, weights[k], preferred_element_type=f32)  2.31 us
    ppermute x1, starting transfers between devices, local(): lax.ppermute(product(1 - c, (0, 2, 3, 1)), 'c', [(i, (i + 1) % nc) for i...  1.92 us
  transfers between devices with their start and end apart: 5, of which 2 were waited for; matrix products, arithmetic and copies ran while one was open for 3% of the time, Pallas kernels for 0%

profile of v12, /device:TPU:8, one launch (start us, length us, event | category | flops | bytes accessed | tf_op | source)
XLA Modules:
  0.0 79.5 jit_solution(13726952143785973265)
XLA Ops:
  0.0 0.0 copy-start
  0.0 3.4 %attend.1 = bf16[2,8,2,8,512]{4,3,2,1,0:T(8,128)(2,1)} custom-call(s32[2]{0:T(128)} %lengths.1, bf16[2,576,128]{2,1,0:T(8,128)(2,1)} %bitcast.51, bf16[2,576,256]{2,1,0:T(8,128)(2,1)} %bitcast.50), custom_call_target="tpu_custom_call" | custom-call | flops 142606336 | bytes 1146880 | tf_op jit(solution)/shard_map/attend/pallas_call | solution.py:57
  3.4 0.0 copy-start.1
  3.4 9.3 %all-to-all-start.1 = ((bf16[16,2,8,512]{3,2,1,0:T(8,128)(2,1)}), bf16[16,2,8,512]{3,2,1,0:T(8,128)(2,1)S(1)}, u32[]{:S(2)}, u32[]{:S(2)}) async-start(bf16[16,2,8,512]{3,2,1,0:T(8,128)(2,1)} %bitcast.47), calls=%async_computation.1 | async-start | bytes 524288 | tf_op jit(solution)/shard_map/all_to_all | solution.py:87
  12.7 0.0 copy-done.1
  12.7 3.4 %collective-permute-start.1 = (bf16[1024,224]{0,1:T(8,128)(2,1)S(1)}, bf16[1024,224]{0,1:T(8,128)(2,1)S(1)}, u32[]{:S(2)}, u32[]{:S(2)}) collective-permute-start(bf16[1024,224]{0,1:T(8,128)(2,1)S(1)} %copy-done.1), channel_id=1, source_target_pairs={{0,256},{128,384},{256,0},{384,128},{1,257},{129,385},{257,1},{385... | collective-permute-start | bytes 1376264 | tf_op jit(solution)/shard_map/ppermute | solution.py:82
  16.1 2.5 %collective-permute-start = (bf16[1024,224]{0,1:T(8,128)(2,1)S(1)}, bf16[1024,224]{0,1:T(8,128)(2,1)S(1)}, u32[]{:S(2)}, u32[]{:S(2)}) collective-permute-start(bf16[1024,224]{0,1:T(8,128)(2,1)S(1)} %copy-done.1), channel_id=1, source_target_pairs={{0,128},{128,256},{256,384},{384,0},{1,129},{129,257},{257,385},{3... | collective-permute-start | bytes 1376264 | tf_op jit(solution)/shard_map/ppermute | solution.py:82
  18.6 4.6 %collective-permute-start.2 = (bf16[1024,224]{0,1:T(8,128)(2,1)S(1)}, bf16[1024,224]{0,1:T(8,128)(2,1)S(1)}, u32[]{:S(2)}, u32[]{:S(2)}) collective-permute-start(bf16[1024,224]{0,1:T(8,128)(2,1)S(1)} %copy-done.1), channel_id=1, source_target_pairs={{0,384},{128,0},{256,128},{384,256},{1,385},{129,1},{257,129},{385... | collective-permute-start | bytes 1376264 | tf_op jit(solution)/shard_map/ppermute | solution.py:82
  23.2 0.6 all-to-all-done.1
  23.7 0.0 copy-done
  23.7 0.4 fusion
  24.1 26.7 %conditional.1 = (bf16[8,2,16,1024]{3,2,1,0:T(8,128)(2,1)S(1)}) conditional(s32[]{:T(128)} %convert_element_type.22, () %tuple.15, bf16[16,2,8,128]{3,0,1,2:T(8,128)(2,1)S(1)} %fusion), branch_computations={%region_0.0_spmd, %region_1.0_spmd} | conditional | bytes 1900552 | solution.py:96
  24.2 0.1 broadcast_in_dim.6
  24.3 26.5 %all_to_all.14 = bf16[8,2,16,1024]{3,2,1,0:T(8,128)(2,1)S(1)} all-to-all(bf16[8,2,16,1024]{3,2,1,0:T(8,128)(2,1)S(1)} %broadcast_in_dim.6), channel_id=1, replica_groups=mesh['x'=4,'z'=8,'y'=8,'c'=2] {'z'}, dimensions={0} | all-to-all | bytes 1048576 | tf_op jit(solution)/shard_map/cond/branch_1_fun/all_to_all | solution.py:94
  50.8 0.3 fusion.12
  51.1 0.0 collective-permute-done.1
  51.1 0.3 fusion.13
  51.4 0.0 collective-permute-done.2
  51.5 0.3 fusion.8
  51.7 0.3 fusion.14
  52.1 0.0 collective-permute-done
  52.1 0.3 fusion.15
  52.4 1.9 %collective-permute-start.3 = (f32[128,896]{0,1:T(8,128)S(1)}, f32[128,896]{0,1:T(8,128)S(1)}, u32[]{:S(2)}, u32[]{:S(2)}) collective-permute-start(f32[128,896]{0,1:T(8,128)S(1)} %pad_maximum_fusion), channel_id=1, source_target_pairs={{0,1},{1,0},{2,3},{3,2},{4,5},{5,4},{6,7},{7,6},{8,9},{9,8},{10,11... | collective-permute-start | bytes 1376264 | tf_op jit(solution)/shard_map/ppermute | solution.py:109
  54.3 0.3 fusion.10
  54.6 0.3 fusion.9
  54.9 0.3 fusion.11
  55.2 0.9 %collective-permute-done.3 = f32[128,896]{0,1:T(8,128)S(1)} collective-permute-done((f32[128,896]{0,1:T(8,128)S(1)}, f32[128,896]{0,1:T(8,128)S(1)}, u32[]{:S(2)}, u32[]{:S(2)}) %collective-permute-start.3) | collective-permute-done | bytes 458784 | tf_op jit(solution)/shard_map/ppermute | solution.py:109
  56.2 0.2 copy.19
  56.3 0.1 reshape.45
  56.5 0.2 copy.21
  56.7 21.3 %all_to_all.15 = bf16[64,2,896]{2,1,0:T(2,128)(2,1)S(1)} all-to-all(bf16[64,2,896]{2,1,0:T(2,128)(2,1)S(1)} %copy.21), channel_id=1, replica_groups=mesh['x'=4,'z'=8,'y'=8,'c'=2] {'y','z'}, dimensions={0} | all-to-all | bytes 458752 | tf_op jit(solution)/shard_map/all_to_all | solution.py:113
  78.0 0.2 convert_element_type.26
  78.2 0.1 fusion.4
  78.3 0.1 reshape.54
  78.4 0.1 rev.3
  78.6 0.2 fusion.7
  78.8 0.7 reshape.47
  (10 shorter events, 0.3 us)
Async XLA Ops:
  0.0 23.7 %copy-start = (bf16[8,512,128]{2,1,0:T(8,128)(2,1)S(1)}, bf16[8,512,128]{2,1,0:T(8,128)(2,1)}, u32[]{:S(2)}) copy-start(bf16[8,512,128]{2,1,0:T(8,128)(2,1)} %param.10) | copy-start | bytes 3145732
  3.4 9.3 %copy-start.1 = (bf16[1024,224]{0,1:T(8,128)(2,1)S(1)}, bf16[1024,224]{0,1:T(8,128)(2,1)}, u32[]{:S(2)}) copy-start(bf16[1024,224]{0,1:T(8,128)(2,1)} %param.11) | copy-start | bytes 1376260
  3.4 20.3 %all-to-all-start.1 = ((bf16[16,2,8,512]{3,2,1,0:T(8,128)(2,1)}), bf16[16,2,8,512]{3,2,1,0:T(8,128)(2,1)S(1)}, u32[]{:S(2)}, u32[]{:S(2)}) async-start(bf16[16,2,8,512]{3,2,1,0:T(8,128)(2,1)} %bitcast.47), calls=%async_computation.1 | async-start | bytes 524288 | tf_op jit(solution)/shard_map/all_to_all | solution.py:87
  12.7 38.4 %collective-permute-start.1 = (bf16[1024,224]{0,1:T(8,128)(2,1)S(1)}, bf16[1024,224]{0,1:T(8,128)(2,1)S(1)}, u32[]{:S(2)}, u32[]{:S(2)}) collective-permute-start(bf16[1024,224]{0,1:T(8,128)(2,1)S(1)} %copy-done.1), channel_id=1, source_target_pairs={{0,256},{128,384},{256,0},{384,128},{1,257},{129,385},{257,1},{385... | collective-permute-start | bytes 1376264 | tf_op jit(solution)/shard_map/ppermute | solution.py:82
  16.1 36.0 %collective-permute-start = (bf16[1024,224]{0,1:T(8,128)(2,1)S(1)}, bf16[1024,224]{0,1:T(8,128)(2,1)S(1)}, u32[]{:S(2)}, u32[]{:S(2)}) collective-permute-start(bf16[1024,224]{0,1:T(8,128)(2,1)S(1)} %copy-done.1), channel_id=1, source_target_pairs={{0,128},{128,256},{256,384},{384,0},{1,129},{129,257},{257,385},{3... | collective-permute-start | bytes 1376264 | tf_op jit(solution)/shard_map/ppermute | solution.py:82
  18.6 32.8 %collective-permute-start.2 = (bf16[1024,224]{0,1:T(8,128)(2,1)S(1)}, bf16[1024,224]{0,1:T(8,128)(2,1)S(1)}, u32[]{:S(2)}, u32[]{:S(2)}) collective-permute-start(bf16[1024,224]{0,1:T(8,128)(2,1)S(1)} %copy-done.1), channel_id=1, source_target_pairs={{0,384},{128,0},{256,128},{384,256},{1,385},{129,1},{257,129},{385... | collective-permute-start | bytes 1376264 | tf_op jit(solution)/shard_map/ppermute | solution.py:82
  52.4 3.7 %collective-permute-start.3 = (f32[128,896]{0,1:T(8,128)S(1)}, f32[128,896]{0,1:T(8,128)S(1)}, u32[]{:S(2)}, u32[]{:S(2)}) collective-permute-start(f32[128,896]{0,1:T(8,128)S(1)} %pad_maximum_fusion), channel_id=1, source_target_pairs={{0,1},{1,0},{2,3},{3,2},{4,5},{5,4},{6,7},{7,6},{8,9},{9,8},{10,11... | collective-permute-start | bytes 1376264 | tf_op jit(solution)/shard_map/ppermute | solution.py:109

commit v13 on v11

--- a/solution.py
+++ b/solution.py
@@ -79,9 +79,7 @@
     nx, nz, ny, nc = (lax.axis_size(a) for a in ("x", "z", "y", "c"))
     x, c = lax.axis_index("x"), lax.axis_index("c")
     requests = queries.shape[0]
-    others = [
-        lax.ppermute(output_weight, "x", [(i, (i + k) % nx) for i in range(nx)]) for k in range(1, nx)
-    ]
+    sent = {k: lax.ppermute(output_weight, "x", [(i, (i + k) % nx) for i in range(nx)]) for k in (1, 3, 2)}
     latent = attend(
         queries.transpose(0, 2, 1), latent_cache.transpose(0, 2, 1), lengths, ny, nc, value_weight.shape[1]
     )
@@ -96,9 +94,9 @@
         return lax.all_to_all(values, "z", split_axis=0, concat_axis=0, tiled=True)
 
     everyone = lax.cond(x < nx, gather, lambda v: jnp.zeros((nz, *v.shape), bf16), values)
-    everyone, others = lax.optimization_barrier((everyone, others))
-    blocks = [output_weight, *others]
-
+    everyone, *others = lax.optimization_barrier((everyone, *sent.values()))
+    sent = dict(zip(sent, others))
+    blocks = [output_weight, *(sent[k] for k in range(1, nx))]
 
     def product(core):
         rows = lax.dynamic_index_in_dim(everyone, core, 1, keepdims=False)
@@ -106,14 +104,13 @@
         return jnp.concatenate([jnp.dot(rows, w, preferred_element_type=f32) for w in blocks], axis=1)
 
     received = lax.ppermute(product(1 - c), "c", [(i, (i + 1) % nc) for i in range(nc)])
-    summed = (product(c) + received).astype(bf16).reshape(nz, ny, requests, -1)
-    summed = summed.transpose(1, 0, 2, 3).reshape(ny * nz, requests, -1)
+    summed = (product(c) + received).astype(bf16).reshape(nz * ny, requests, -1)
     summed, turn = lax.optimization_barrier((summed, jnp.mod(nx - x, nx)))
-    parts = lax.all_to_all(summed, ("y", "z"), split_axis=0, concat_axis=0, tiled=True)
-    parts = parts.reshape(ny, nz, requests, nx, -1).astype(f32)
-    total = parts[0]
+    parts = lax.all_to_all(summed, ("z", "y"), split_axis=0, concat_axis=0, tiled=True)
+    parts = parts.reshape(nz, ny, requests, nx, -1).astype(f32)
+    total = parts[:, 0]
     for i in range(1, ny):
-        total = total + parts[i]
+        total = total + parts[:, i]
     total = total.astype(bf16).transpose(1, 2, 0, 3)
     shifted = total[:, :1], total[:, :0:-1]
     total = jnp.concatenate([*shifted, *shifted], axis=1)

time: 79.6 us -> 79.4 us (level)
  transfers between devices with their start and end apart: 5 -> 5, of which waited for: 2 -> 1; matrix products, arithmetic and copies ran while one was open for 1% -> 1% of each run, Pallas kernels for 0% -> 0%
where the time goes in v13:
time: 79.4 us; the launch traced here: 79 us
  blocking collectives  49.6 us (62%)
  starting transfers between devices  19.6 us (25%)
  Pallas kernels  3.41 us (4%)
  matrix products  2.68 us (3%)
  local copies, waits for them, and re-layouts  1.84 us (2%)
  waiting for transfers between devices  1.23 us (2%)
    all_to_all x1, blocking collectives, gather(): return lax.all_to_all(values, 'z', split_axis=0, concat_axis=0, tiled=True)  27.4 us
    all_to_all x1, blocking collectives, local(): lax.all_to_all(summed, ('z', 'y'), split_axis=0, concat_axis=0, tiled=True)  22.2 us
    ppermute x3, starting transfers between devices, local(): lax.ppermute(output_weight, 'x', [(i, (i + k) % nx) for i in range(nx)])  10.4 us
    all_to_all x1, starting transfers between devices, local(): lax.all_to_all(latent, ('c', 'y'), split_axis=0, concat_axis=0, tiled=True)  7.35 us
    pallas_call x1, Pallas kernels, attend(): pl.pallas_call(attend_kernel, in_specs=[pl.BlockSpec(memory_space=pltpu.S...  3.41 us
    dot_general x8, matrix products, product(): jnp.dot(rows, w, preferred_element_type=f32)  2.32 us
    ppermute x1, starting transfers between devices, local(): lax.ppermute(product(1 - c), 'c', [(i, (i + 1) % nc) for i in range(nc)])  1.92 us
  transfers between devices with their start and end apart: 5, of which 1 were waited for; matrix products, arithmetic and copies ran while one was open for 1% of the time, Pallas kernels for 0%

profile of v13, /device:TPU:6, one launch (start us, length us, event | category | flops | bytes accessed | tf_op | source)
XLA Modules:
  0.0 79.0 jit_solution(984922970495846468)
XLA Ops:
  0.0 0.0 copy-start
  0.0 3.4 %attend.1 = bf16[2,8,2,8,512]{4,3,2,1,0:T(8,128)(2,1)} custom-call(s32[2]{0:T(128)} %lengths.1, bf16[2,576,128]{2,1,0:T(8,128)(2,1)} %bitcast.46, bf16[2,576,256]{2,1,0:T(8,128)(2,1)} %bitcast.45), custom_call_target="tpu_custom_call" | custom-call | flops 142606336 | bytes 1146880 | tf_op jit(solution)/shard_map/attend/pallas_call | solution.py:57
  3.4 0.0 copy-start.1
  3.4 7.4 %all-to-all-start.1 = ((bf16[16,2,8,512]{3,2,1,0:T(8,128)(2,1)}), bf16[16,2,8,512]{3,2,1,0:T(8,128)(2,1)S(1)}, u32[]{:S(2)}, u32[]{:S(2)}) async-start(bf16[16,2,8,512]{3,2,1,0:T(8,128)(2,1)} %bitcast.44), calls=%async_computation.1 | async-start | bytes 524288 | tf_op jit(solution)/shard_map/all_to_all | solution.py:87
  10.8 0.0 copy-done.1
  10.8 3.3 %collective-permute-start.2 = (bf16[1024,224]{0,1:T(8,128)(2,1)S(1)}, bf16[1024,224]{0,1:T(8,128)(2,1)S(1)}, u32[]{:S(2)}, u32[]{:S(2)}) collective-permute-start(bf16[1024,224]{0,1:T(8,128)(2,1)S(1)} %copy-done.1), channel_id=1, source_target_pairs={{0,256},{128,384},{256,0},{384,128},{1,257},{129,385},{257,1},{385... | collective-permute-start | bytes 1376264 | tf_op jit(solution)/shard_map/ppermute | solution.py:82
  14.1 3.5 %collective-permute-start.1 = (bf16[1024,224]{0,1:T(8,128)(2,1)S(1)}, bf16[1024,224]{0,1:T(8,128)(2,1)S(1)}, u32[]{:S(2)}, u32[]{:S(2)}) collective-permute-start(bf16[1024,224]{0,1:T(8,128)(2,1)S(1)} %copy-done.1), channel_id=1, source_target_pairs={{0,384},{128,0},{256,128},{384,256},{1,385},{129,1},{257,129},{385... | collective-permute-start | bytes 1376264 | tf_op jit(solution)/shard_map/ppermute | solution.py:82
  17.7 3.5 %collective-permute-start = (bf16[1024,224]{0,1:T(8,128)(2,1)S(1)}, bf16[1024,224]{0,1:T(8,128)(2,1)S(1)}, u32[]{:S(2)}, u32[]{:S(2)}) collective-permute-start(bf16[1024,224]{0,1:T(8,128)(2,1)S(1)} %copy-done.1), channel_id=1, source_target_pairs={{0,128},{128,256},{256,384},{384,0},{1,129},{129,257},{257,385},{3... | collective-permute-start | bytes 1376264 | tf_op jit(solution)/shard_map/ppermute | solution.py:82
  21.2 0.0 all-to-all-done.1
  21.2 0.0 copy-done
  21.2 0.4 fusion
  21.6 27.6 %conditional.1 = (bf16[8,2,16,1024]{3,2,1,0:T(8,128)(2,1)S(1)}) conditional(s32[]{:T(128)} %convert_element_type.24, () %tuple.13, bf16[16,2,8,128]{3,0,1,2:T(8,128)(2,1)S(1)} %fusion), branch_computations={%region_0.0_spmd, %region_1.0_spmd} | conditional | bytes 1900552 | solution.py:96
  21.7 0.1 broadcast_in_dim.6
  21.7 27.4 %all_to_all.14 = bf16[8,2,16,1024]{3,2,1,0:T(8,128)(2,1)S(1)} all-to-all(bf16[8,2,16,1024]{3,2,1,0:T(8,128)(2,1)S(1)} %broadcast_in_dim.6), channel_id=1, replica_groups=mesh['x'=4,'z'=8,'y'=8,'c'=2] {'z'}, dimensions={0} | all-to-all | bytes 1048576 | tf_op jit(solution)/shard_map/cond/branch_1_fun/all_to_all | solution.py:94
  49.2 0.0 collective-permute-done.2
  49.2 0.0 collective-permute-done.1
  49.2 0.0 collective-permute-done
  49.2 0.3 fusion.16
  49.5 0.3 fusion.12
  49.8 0.3 fusion.15
  50.1 0.3 fusion.11
  50.4 0.3 fusion.13
  50.7 0.3 fusion.14
  51.1 1.9 %collective-permute-start.3 = (f32[128,896]{0,1:T(8,128)S(1)}, f32[128,896]{0,1:T(8,128)S(1)}, u32[]{:S(2)}, u32[]{:S(2)}) collective-permute-start(f32[128,896]{0,1:T(8,128)S(1)} %pad_maximum_fusion), channel_id=1, source_target_pairs={{0,1},{1,0},{2,3},{3,2},{4,5},{5,4},{6,7},{7,6},{8,9},{9,8},{10,11... | collective-permute-start | bytes 1376264 | tf_op jit(solution)/shard_map/ppermute | solution.py:106
  53.0 0.3 fusion.10
  53.3 0.3 fusion.9
  53.6 1.2 %collective-permute-done.3 = f32[128,896]{0,1:T(8,128)S(1)} collective-permute-done((f32[128,896]{0,1:T(8,128)S(1)}, f32[128,896]{0,1:T(8,128)S(1)}, u32[]{:S(2)}, u32[]{:S(2)}) %collective-permute-start.3) | collective-permute-done | bytes 458784 | tf_op jit(solution)/shard_map/ppermute | solution.py:106
  54.8 0.2 copy.18
  55.0 0.1 reshape.28
  55.1 22.2 %all_to_all.15 = bf16[64,2,896]{2,1,0:T(2,128)(2,1)S(1)} all-to-all(bf16[64,2,896]{2,1,0:T(2,128)(2,1)S(1)} %reshape.28), channel_id=1, replica_groups=mesh['x'=4,'z'=8,'y'=8,'c'=2] {'z','y'}, dimensions={0} | all-to-all | bytes 458752 | tf_op jit(solution)/shard_map/all_to_all | solution.py:109
  77.3 0.5 reshape.30
  77.8 0.1 fusion.8
  77.9 0.1 rev.3
  78.1 0.2 fusion.7
  78.3 0.7 reshape.29
  (8 shorter events, 0.2 us)
Async XLA Ops:
  0.0 21.2 %copy-start = (bf16[8,512,128]{2,1,0:T(8,128)(2,1)S(1)}, bf16[8,512,128]{2,1,0:T(8,128)(2,1)}, u32[]{:S(2)}) copy-start(bf16[8,512,128]{2,1,0:T(8,128)(2,1)} %param.10) | copy-start | bytes 3145732
  3.4 7.4 %copy-start.1 = (bf16[1024,224]{0,1:T(8,128)(2,1)S(1)}, bf16[1024,224]{0,1:T(8,128)(2,1)}, u32[]{:S(2)}) copy-start(bf16[1024,224]{0,1:T(8,128)(2,1)} %param.11) | copy-start | bytes 1376260
  3.4 17.8 %all-to-all-start.1 = ((bf16[16,2,8,512]{3,2,1,0:T(8,128)(2,1)}), bf16[16,2,8,512]{3,2,1,0:T(8,128)(2,1)S(1)}, u32[]{:S(2)}, u32[]{:S(2)}) async-start(bf16[16,2,8,512]{3,2,1,0:T(8,128)(2,1)} %bitcast.44), calls=%async_computation.1 | async-start | bytes 524288 | tf_op jit(solution)/shard_map/all_to_all | solution.py:87
  10.8 38.4 %collective-permute-start.2 = (bf16[1024,224]{0,1:T(8,128)(2,1)S(1)}, bf16[1024,224]{0,1:T(8,128)(2,1)S(1)}, u32[]{:S(2)}, u32[]{:S(2)}) collective-permute-start(bf16[1024,224]{0,1:T(8,128)(2,1)S(1)} %copy-done.1), channel_id=1, source_target_pairs={{0,256},{128,384},{256,0},{384,128},{1,257},{129,385},{257,1},{385... | collective-permute-start | bytes 1376264 | tf_op jit(solution)/shard_map/ppermute | solution.py:82
  14.1 35.1 %collective-permute-start.1 = (bf16[1024,224]{0,1:T(8,128)(2,1)S(1)}, bf16[1024,224]{0,1:T(8,128)(2,1)S(1)}, u32[]{:S(2)}, u32[]{:S(2)}) collective-permute-start(bf16[1024,224]{0,1:T(8,128)(2,1)S(1)} %copy-done.1), channel_id=1, source_target_pairs={{0,384},{128,0},{256,128},{384,256},{1,385},{129,1},{257,129},{385... | collective-permute-start | bytes 1376264 | tf_op jit(solution)/shard_map/ppermute | solution.py:82
  17.7 31.5 %collective-permute-start = (bf16[1024,224]{0,1:T(8,128)(2,1)S(1)}, bf16[1024,224]{0,1:T(8,128)(2,1)S(1)}, u32[]{:S(2)}, u32[]{:S(2)}) collective-permute-start(bf16[1024,224]{0,1:T(8,128)(2,1)S(1)} %copy-done.1), channel_id=1, source_target_pairs={{0,128},{128,256},{256,384},{384,0},{1,129},{129,257},{257,385},{3... | collective-permute-start | bytes 1376264 | tf_op jit(solution)/shard_map/ppermute | solution.py:82
  51.1 3.7 %collective-permute-start.3 = (f32[128,896]{0,1:T(8,128)S(1)}, f32[128,896]{0,1:T(8,128)S(1)}, u32[]{:S(2)}, u32[]{:S(2)}) collective-permute-start(f32[128,896]{0,1:T(8,128)S(1)} %pad_maximum_fusion), channel_id=1, source_target_pairs={{0,1},{1,0},{2,3},{3,2},{4,5},{5,4},{6,7},{7,6},{8,9},{9,8},{10,11... | collective-permute-start | bytes 1376264 | tf_op jit(solution)/shard_map/ppermute | solution.py:106

commit v14 on v13

--- a/solution.py
+++ b/solution.py
@@ -91,7 +91,9 @@
 
     def gather(values):
         values = jnp.broadcast_to(values[None], (nz, *values.shape))
-        return lax.all_to_all(values, "z", split_axis=0, concat_axis=0, tiled=True)
+        return lax.all_to_all(
+            values, "z", split_axis=0, concat_axis=0, tiled=True, axis_index_groups=[list(range(nz - 1, -1, -1))]
+        )
 
     everyone = lax.cond(x < nx, gather, lambda v: jnp.zeros((nz, *v.shape), bf16), values)
     everyone, *others = lax.optimization_barrier((everyone, *sent.values()))
@@ -106,12 +108,15 @@
     received = lax.ppermute(product(1 - c), "c", [(i, (i + 1) % nc) for i in range(nc)])
     summed = (product(c) + received).astype(bf16).reshape(nz * ny, requests, -1)
     summed, turn = lax.optimization_barrier((summed, jnp.mod(nx - x, nx)))
-    parts = lax.all_to_all(summed, ("z", "y"), split_axis=0, concat_axis=0, tiled=True)
+    downward = [[z * ny + y for z in range(nz - 1, -1, -1) for y in range(ny)]]
+    parts = lax.all_to_all(
+        summed, ("z", "y"), split_axis=0, concat_axis=0, tiled=True, axis_index_groups=downward
+    )
     parts = parts.reshape(nz, ny, requests, nx, -1).astype(f32)
     total = parts[:, 0]
     for i in range(1, ny):
         total = total + parts[:, i]
-    total = total.astype(bf16).transpose(1, 2, 0, 3)
+    total = total[::-1].astype(bf16).transpose(1, 2, 0, 3)
     shifted = total[:, :1], total[:, :0:-1]
     total = jnp.concatenate([*shifted, *shifted], axis=1)
     total = lax.dynamic_slice_in_dim(total, turn, nx, 1, allow_negative_indices=False)

time: 79.4 us -> 78.3 us (0.986)
  blocking collectives: 49.6 us -> 48.5 us
    all_to_all x2, blocking collectives: 49.6 us -> 48.5 us  [the longest x1 24.6 us: local(): lax.all_to_all(summed, ('z', 'y'), split_axis=0, concat_axis=0, tiled=Tru...]
where the time goes in v14:
time: 78.3 us; the launch traced here: 77.9 us
  blocking collectives  48.5 us (62%)
  starting transfers between devices  19.6 us (25%)
  Pallas kernels  3.41 us (4%)
  matrix products  2.68 us (3%)
  local copies, waits for them, and re-layouts  1.85 us (2%)
  waiting for transfers between devices  1.23 us (2%)
    all_to_all x1, blocking collectives, local(): lax.all_to_all(summed, ('z', 'y'), split_axis=0, concat_axis=0, tiled=Tru...  24.6 us
    all_to_all x1, blocking collectives, gather(): lax.all_to_all(values, 'z', split_axis=0, concat_axis=0, tiled=True, axis...  23.9 us
    ppermute x3, starting transfers between devices, local(): lax.ppermute(output_weight, 'x', [(i, (i + k) % nx) for i in range(nx)])  10.4 us
    all_to_all x1, starting transfers between devices, local(): lax.all_to_all(latent, ('c', 'y'), split_axis=0, concat_axis=0, tiled=True)  7.35 us
    pallas_call x1, Pallas kernels, attend(): pl.pallas_call(attend_kernel, in_specs=[pl.BlockSpec(memory_space=pltpu.S...  3.41 us
    dot_general x8, matrix products, product(): jnp.dot(rows, w, preferred_element_type=f32)  2.32 us
    ppermute x1, starting transfers between devices, local(): lax.ppermute(product(1 - c), 'c', [(i, (i + 1) % nc) for i in range(nc)])  1.92 us
  transfers between devices with their start and end apart: 5, of which 1 were waited for; matrix products, arithmetic and copies ran while one was open for 1% of the time, Pallas kernels for 0%

profile of v14, /device:TPU:6, one launch (start us, length us, event | category | flops | bytes accessed | tf_op | source)
XLA Modules:
  0.0 77.9 jit_solution(9606004847068700672)
XLA Ops:
  0.0 0.0 copy-start
  0.0 3.4 %attend.1 = bf16[2,8,2,8,512]{4,3,2,1,0:T(8,128)(2,1)} custom-call(s32[2]{0:T(128)} %lengths.1, bf16[2,576,128]{2,1,0:T(8,128)(2,1)} %bitcast.46, bf16[2,576,256]{2,1,0:T(8,128)(2,1)} %bitcast.45), custom_call_target="tpu_custom_call" | custom-call | flops 142606336 | bytes 1146880 | tf_op jit(solution)/shard_map/attend/pallas_call | solution.py:57
  3.4 0.0 copy-start.1
  3.4 7.4 %all-to-all-start.1 = ((bf16[16,2,8,512]{3,2,1,0:T(8,128)(2,1)}), bf16[16,2,8,512]{3,2,1,0:T(8,128)(2,1)S(1)}, u32[]{:S(2)}, u32[]{:S(2)}) async-start(bf16[16,2,8,512]{3,2,1,0:T(8,128)(2,1)} %bitcast.44), calls=%async_computation.1 | async-start | bytes 524288 | tf_op jit(solution)/shard_map/all_to_all | solution.py:87
  10.8 0.0 copy-done.1
  10.8 3.3 %collective-permute-start.2 = (bf16[1024,224]{0,1:T(8,128)(2,1)S(1)}, bf16[1024,224]{0,1:T(8,128)(2,1)S(1)}, u32[]{:S(2)}, u32[]{:S(2)}) collective-permute-start(bf16[1024,224]{0,1:T(8,128)(2,1)S(1)} %copy-done.1), channel_id=1, source_target_pairs={{0,256},{128,384},{256,0},{384,128},{1,257},{129,385},{257,1},{385... | collective-permute-start | bytes 1376264 | tf_op jit(solution)/shard_map/ppermute | solution.py:82
  14.1 3.5 %collective-permute-start.1 = (bf16[1024,224]{0,1:T(8,128)(2,1)S(1)}, bf16[1024,224]{0,1:T(8,128)(2,1)S(1)}, u32[]{:S(2)}, u32[]{:S(2)}) collective-permute-start(bf16[1024,224]{0,1:T(8,128)(2,1)S(1)} %copy-done.1), channel_id=1, source_target_pairs={{0,384},{128,0},{256,128},{384,256},{1,385},{129,1},{257,129},{385... | collective-permute-start | bytes 1376264 | tf_op jit(solution)/shard_map/ppermute | solution.py:82
  17.7 3.5 %collective-permute-start = (bf16[1024,224]{0,1:T(8,128)(2,1)S(1)}, bf16[1024,224]{0,1:T(8,128)(2,1)S(1)}, u32[]{:S(2)}, u32[]{:S(2)}) collective-permute-start(bf16[1024,224]{0,1:T(8,128)(2,1)S(1)} %copy-done.1), channel_id=1, source_target_pairs={{0,128},{128,256},{256,384},{384,0},{1,129},{129,257},{257,385},{3... | collective-permute-start | bytes 1376264 | tf_op jit(solution)/shard_map/ppermute | solution.py:82
  21.2 0.0 all-to-all-done.1
  21.2 0.0 copy-done
  21.2 0.4 fusion
  21.6 24.1 %conditional.1 = (bf16[8,2,16,1024]{3,2,1,0:T(8,128)(2,1)S(1)}) conditional(s32[]{:T(128)} %convert_element_type.24, () %tuple.13, bf16[16,2,8,128]{3,0,1,2:T(8,128)(2,1)S(1)} %fusion), branch_computations={%region_0.0_spmd, %region_1.0_spmd} | conditional | bytes 1900552 | solution.py:98
  21.7 0.1 broadcast_in_dim.6
  21.7 23.9 %all_to_all.14 = bf16[8,2,16,1024]{3,2,1,0:T(8,128)(2,1)S(1)} all-to-all(bf16[8,2,16,1024]{3,2,1,0:T(8,128)(2,1)S(1)} %broadcast_in_dim.6), channel_id=1, replica_groups={{112,96,80,64,48,32,16,0},{113,97,81,65,49,33,17,1},{114,98,82,66,50,34..., dimensions={0} | all-to-all | bytes 1048576 | tf_op jit(solution)/shard_map/cond/branch_1_fun/all_to_all | solution.py:94
  45.7 0.0 collective-permute-done.2
  45.7 0.0 collective-permute-done.1
  45.7 0.0 collective-permute-done
  45.7 0.3 fusion.16
  46.0 0.3 fusion.12
  46.3 0.3 fusion.15
  46.6 0.3 fusion.11
  46.9 0.3 fusion.13
  47.2 0.3 fusion.14
  47.6 1.9 %collective-permute-start.3 = (f32[128,896]{0,1:T(8,128)S(1)}, f32[128,896]{0,1:T(8,128)S(1)}, u32[]{:S(2)}, u32[]{:S(2)}) collective-permute-start(f32[128,896]{0,1:T(8,128)S(1)} %pad_maximum_fusion), channel_id=1, source_target_pairs={{0,1},{1,0},{2,3},{3,2},{4,5},{5,4},{6,7},{7,6},{8,9},{9,8},{10,11... | collective-permute-start | bytes 1376264 | tf_op jit(solution)/shard_map/ppermute | solution.py:108
  49.5 0.3 fusion.10
  49.8 0.3 fusion.9
  50.1 1.2 %collective-permute-done.3 = f32[128,896]{0,1:T(8,128)S(1)} collective-permute-done((f32[128,896]{0,1:T(8,128)S(1)}, f32[128,896]{0,1:T(8,128)S(1)}, u32[]{:S(2)}, u32[]{:S(2)}) %collective-permute-start.3) | collective-permute-done | bytes 458784 | tf_op jit(solution)/shard_map/ppermute | solution.py:108
  51.3 0.2 copy.18
  51.5 0.1 reshape.28
  51.6 24.6 %all_to_all.15 = bf16[64,2,896]{2,1,0:T(2,128)(2,1)S(1)} all-to-all(bf16[64,2,896]{2,1,0:T(2,128)(2,1)S(1)} %reshape.28), channel_id=1, replica_groups={{112,114,116,118,120,122,124,126,96,98,100,102,104,106,108,110,80,82,84..., dimensions={0} | all-to-all | bytes 458752 | tf_op jit(solution)/shard_map/all_to_all | solution.py:112
  76.2 0.5 reshape.30
  76.7 0.1 fusion.4
  76.8 0.1 rev.7
  77.0 0.2 fusion.8
  77.2 0.7 reshape.29
  (9 shorter events, 0.2 us)
Async XLA Ops:
  0.0 21.2 %copy-start = (bf16[8,512,128]{2,1,0:T(8,128)(2,1)S(1)}, bf16[8,512,128]{2,1,0:T(8,128)(2,1)}, u32[]{:S(2)}) copy-start(bf16[8,512,128]{2,1,0:T(8,128)(2,1)} %param.10) | copy-start | bytes 3145732
  3.4 7.4 %copy-start.1 = (bf16[1024,224]{0,1:T(8,128)(2,1)S(1)}, bf16[1024,224]{0,1:T(8,128)(2,1)}, u32[]{:S(2)}) copy-start(bf16[1024,224]{0,1:T(8,128)(2,1)} %param.11) | copy-start | bytes 1376260
  3.4 17.8 %all-to-all-start.1 = ((bf16[16,2,8,512]{3,2,1,0:T(8,128)(2,1)}), bf16[16,2,8,512]{3,2,1,0:T(8,128)(2,1)S(1)}, u32[]{:S(2)}, u32[]{:S(2)}) async-start(bf16[16,2,8,512]{3,2,1,0:T(8,128)(2,1)} %bitcast.44), calls=%async_computation.1 | async-start | bytes 524288 | tf_op jit(solution)/shard_map/all_to_all | solution.py:87
  10.8 34.8 %collective-permute-start.2 = (bf16[1024,224]{0,1:T(8,128)(2,1)S(1)}, bf16[1024,224]{0,1:T(8,128)(2,1)S(1)}, u32[]{:S(2)}, u32[]{:S(2)}) collective-permute-start(bf16[1024,224]{0,1:T(8,128)(2,1)S(1)} %copy-done.1), channel_id=1, source_target_pairs={{0,256},{128,384},{256,0},{384,128},{1,257},{129,385},{257,1},{385... | collective-permute-start | bytes 1376264 | tf_op jit(solution)/shard_map/ppermute | solution.py:82
  14.1 31.5 %collective-permute-start.1 = (bf16[1024,224]{0,1:T(8,128)(2,1)S(1)}, bf16[1024,224]{0,1:T(8,128)(2,1)S(1)}, u32[]{:S(2)}, u32[]{:S(2)}) collective-permute-start(bf16[1024,224]{0,1:T(8,128)(2,1)S(1)} %copy-done.1), channel_id=1, source_target_pairs={{0,384},{128,0},{256,128},{384,256},{1,385},{129,1},{257,129},{385... | collective-permute-start | bytes 1376264 | tf_op jit(solution)/shard_map/ppermute | solution.py:82
  17.7 28.0 %collective-permute-start = (bf16[1024,224]{0,1:T(8,128)(2,1)S(1)}, bf16[1024,224]{0,1:T(8,128)(2,1)S(1)}, u32[]{:S(2)}, u32[]{:S(2)}) collective-permute-start(bf16[1024,224]{0,1:T(8,128)(2,1)S(1)} %copy-done.1), channel_id=1, source_target_pairs={{0,128},{128,256},{256,384},{384,0},{1,129},{129,257},{257,385},{3... | collective-permute-start | bytes 1376264 | tf_op jit(solution)/shard_map/ppermute | solution.py:82
  47.6 3.7 %collective-permute-start.3 = (f32[128,896]{0,1:T(8,128)S(1)}, f32[128,896]{0,1:T(8,128)S(1)}, u32[]{:S(2)}, u32[]{:S(2)}) collective-permute-start(f32[128,896]{0,1:T(8,128)S(1)} %pad_maximum_fusion), channel_id=1, source_target_pairs={{0,1},{1,0},{2,3},{3,2},{4,5},{5,4},{6,7},{7,6},{8,9},{9,8},{10,11... | collective-permute-start | bytes 1376264 | tf_op jit(solution)/shard_map/ppermute | solution.py:108

commit v15 on v14

--- a/solution.py
+++ b/solution.py
@@ -79,7 +79,7 @@
     nx, nz, ny, nc = (lax.axis_size(a) for a in ("x", "z", "y", "c"))
     x, c = lax.axis_index("x"), lax.axis_index("c")
     requests = queries.shape[0]
-    sent = {k: lax.ppermute(output_weight, "x", [(i, (i + k) % nx) for i in range(nx)]) for k in (1, 3, 2)}
+    sent = {k: lax.ppermute(output_weight, "x", [(i, (i + k) % nx) for i in range(nx)]) for k in (3, 2, 1)}
     latent = attend(
         queries.transpose(0, 2, 1), latent_cache.transpose(0, 2, 1), lengths, ny, nc, value_weight.shape[1]
     )
@@ -100,13 +100,12 @@
     sent = dict(zip(sent, others))
     blocks = [output_weight, *(sent[k] for k in range(1, nx))]
 
-    def product(core):
-        rows = lax.dynamic_index_in_dim(everyone, core, 1, keepdims=False)
-        rows = rows.reshape(nz * ny * requests, -1)
-        return jnp.concatenate([jnp.dot(rows, w, preferred_element_type=f32) for w in blocks], axis=1)
-
-    received = lax.ppermute(product(1 - c), "c", [(i, (i + 1) % nc) for i in range(nc)])
-    summed = (product(c) + received).astype(bf16).reshape(nz * ny, requests, -1)
+    rows = everyone.transpose(1, 0, 2, 3).reshape(nc * nz * ny * requests, -1)
+    both = jnp.concatenate([jnp.dot(rows, w, preferred_element_type=f32) for w in blocks], axis=1)
+    first, second = jnp.split(both, nc)
+    theirs, mine = jnp.where(c == 0, second, first), jnp.where(c == 0, first, second)
+    received = lax.ppermute(theirs, "c", [(i, (i + 1) % nc) for i in range(nc)])
+    summed = (mine + received).astype(bf16).reshape(nz * ny, requests, -1)
     summed, turn = lax.optimization_barrier((summed, jnp.mod(nx - x, nx)))
     downward = [[z * ny + y for z in range(nz - 1, -1, -1) for y in range(ny)]]
     parts = lax.all_to_all(

time: 78.3 us -> 78 us (level)
  matrix products: 2.68 us -> 1.71 us
    dot_general x8 -> x4, matrix products: 2.32 us -> 1.35 us  [local(): jnp.dot(rows, w, preferred_element_type=f32)]
where the time goes in v15:
time: 78 us; the launch traced here: 77.6 us
  blocking collectives  48.5 us (62%)
  starting transfers between devices  19.6 us (25%)
  Pallas kernels  3.4 us (4%)
  local copies, waits for them, and re-layouts  1.85 us (2%)
  waiting for transfers between devices  1.81 us (2%)
  matrix products  1.71 us (2%)
    all_to_all x1, blocking collectives, local(): lax.all_to_all(summed, ('z', 'y'), split_axis=0, concat_axis=0, tiled=Tru...  24.6 us
    all_to_all x1, blocking collectives, gather(): lax.all_to_all(values, 'z', split_axis=0, concat_axis=0, tiled=True, axis...  23.9 us
    ppermute x3, starting transfers between devices, local(): lax.ppermute(output_weight, 'x', [(i, (i + k) % nx) for i in range(nx)])  10.4 us
    all_to_all x1, starting transfers between devices, local(): lax.all_to_all(latent, ('c', 'y'), split_axis=0, concat_axis=0, tiled=True)  7.35 us
    pallas_call x1, Pallas kernels, attend(): pl.pallas_call(attend_kernel, in_specs=[pl.BlockSpec(memory_space=pltpu.S...  3.4 us
    ppermute x1, starting transfers between devices, local(): received = lax.ppermute(theirs, 'c', [(i, (i + 1) % nc) for i in range(nc)])  1.92 us
    ppermute x1, waiting for transfers between devices, local(): received = lax.ppermute(theirs, 'c', [(i, (i + 1) % nc) for i in range(nc)])  1.77 us
  transfers between devices with their start and end apart: 5, of which 1 were waited for; matrix products, arithmetic and copies ran while one was open for 1% of the time, Pallas kernels for 0%

profile of v15, /device:TPU:6, one launch (start us, length us, event | category | flops | bytes accessed | tf_op | source)
XLA Modules:
  0.0 77.6 jit_solution(1098848177782923231)
XLA Ops:
  0.0 0.0 copy-start
  0.0 3.4 %attend.1 = bf16[2,8,2,8,512]{4,3,2,1,0:T(8,128)(2,1)} custom-call(s32[2]{0:T(128)} %lengths.1, bf16[2,576,128]{2,1,0:T(8,128)(2,1)} %bitcast.35, bf16[2,576,256]{2,1,0:T(8,128)(2,1)} %bitcast.34), custom_call_target="tpu_custom_call" | custom-call | flops 142606336 | bytes 1146880 | tf_op jit(solution)/shard_map/attend/pallas_call | solution.py:57
  3.4 0.0 copy-start.1
  3.4 7.4 %all-to-all-start.1 = ((bf16[16,2,8,512]{3,2,1,0:T(8,128)(2,1)}), bf16[16,2,8,512]{3,2,1,0:T(8,128)(2,1)S(1)}, u32[]{:S(2)}, u32[]{:S(2)}) async-start(bf16[16,2,8,512]{3,2,1,0:T(8,128)(2,1)} %bitcast.33), calls=%async_computation.1 | async-start | bytes 524288 | tf_op jit(solution)/shard_map/all_to_all | solution.py:87
  10.8 0.0 copy-done.1
  10.8 3.3 %collective-permute-start.1 = (bf16[1024,224]{0,1:T(8,128)(2,1)S(1)}, bf16[1024,224]{0,1:T(8,128)(2,1)S(1)}, u32[]{:S(2)}, u32[]{:S(2)}) collective-permute-start(bf16[1024,224]{0,1:T(8,128)(2,1)S(1)} %copy-done.1), channel_id=1, source_target_pairs={{0,256},{128,384},{256,0},{384,128},{1,257},{129,385},{257,1},{385... | collective-permute-start | bytes 1376264 | tf_op jit(solution)/shard_map/ppermute | solution.py:82
  14.1 3.5 %collective-permute-start = (bf16[1024,224]{0,1:T(8,128)(2,1)S(1)}, bf16[1024,224]{0,1:T(8,128)(2,1)S(1)}, u32[]{:S(2)}, u32[]{:S(2)}) collective-permute-start(bf16[1024,224]{0,1:T(8,128)(2,1)S(1)} %copy-done.1), channel_id=1, source_target_pairs={{0,384},{128,0},{256,128},{384,256},{1,385},{129,1},{257,129},{385... | collective-permute-start | bytes 1376264 | tf_op jit(solution)/shard_map/ppermute | solution.py:82
  17.7 3.5 %collective-permute-start.2 = (bf16[1024,224]{0,1:T(8,128)(2,1)S(1)}, bf16[1024,224]{0,1:T(8,128)(2,1)S(1)}, u32[]{:S(2)}, u32[]{:S(2)}) collective-permute-start(bf16[1024,224]{0,1:T(8,128)(2,1)S(1)} %copy-done.1), channel_id=1, source_target_pairs={{0,128},{128,256},{256,384},{384,0},{1,129},{129,257},{257,385},{3... | collective-permute-start | bytes 1376264 | tf_op jit(solution)/shard_map/ppermute | solution.py:82
  21.2 0.0 all-to-all-done.1
  21.2 0.0 copy-done
  21.2 0.4 fusion
  21.6 24.1 %conditional.1 = (bf16[8,2,16,1024]{3,2,1,0:T(8,128)(2,1)S(1)}) conditional(s32[]{:T(128)} %convert_element_type.24, () %tuple.13, bf16[16,2,8,128]{3,0,1,2:T(8,128)(2,1)S(1)} %fusion), branch_computations={%region_0.0_spmd, %region_1.0_spmd} | conditional | bytes 1900552 | solution.py:98
  21.7 0.1 broadcast_in_dim.6
  21.7 23.9 %all_to_all.14 = bf16[8,2,16,1024]{3,2,1,0:T(8,128)(2,1)S(1)} all-to-all(bf16[8,2,16,1024]{3,2,1,0:T(8,128)(2,1)S(1)} %broadcast_in_dim.6), channel_id=1, replica_groups={{112,96,80,64,48,32,16,0},{113,97,81,65,49,33,17,1},{114,98,82,66,50,34..., dimensions={0} | all-to-all | bytes 1048576 | tf_op jit(solution)/shard_map/cond/branch_1_fun/all_to_all | solution.py:94
  45.6 0.0 collective-permute-done.1
  45.6 0.0 collective-permute-done
  45.6 0.0 collective-permute-done.2
  45.7 0.3 fusion.8
  46.0 0.3 fusion.11
  46.4 0.3 fusion.10
  46.7 0.3 fusion.9
  47.1 0.1 pad_maximum_fusion
  47.2 1.9 %collective-permute-start.3 = (f32[128,896]{0,1:T(8,128)S(1)}, f32[128,896]{0,1:T(8,128)S(1)}, u32[]{:S(2)}, u32[]{:S(2)}) collective-permute-start(f32[128,896]{0,1:T(8,128)S(1)} %slice_select_fusion), channel_id=1, source_target_pairs={{0,1},{1,0},{2,3},{3,2},{4,5},{5,4},{6,7},{7,6},{8,9},{9,8},{10,11... | collective-permute-start | bytes 1376264 | tf_op jit(solution)/shard_map/ppermute | solution.py:107
  49.1 1.8 %collective-permute-done.3 = f32[128,896]{0,1:T(8,128)S(1)} collective-permute-done((f32[128,896]{0,1:T(8,128)S(1)}, f32[128,896]{0,1:T(8,128)S(1)}, u32[]{:S(2)}, u32[]{:S(2)}) %collective-permute-start.3) | collective-permute-done | bytes 458784 | tf_op jit(solution)/shard_map/ppermute | solution.py:107
  50.9 0.1 add_convert_fusion
  51.0 0.2 copy.19
  51.2 0.1 reshape.22
  51.3 24.6 %all_to_all.15 = bf16[64,2,896]{2,1,0:T(2,128)(2,1)S(1)} all-to-all(bf16[64,2,896]{2,1,0:T(2,128)(2,1)S(1)} %reshape.22), channel_id=1, replica_groups={{112,114,116,118,120,122,124,126,96,98,100,102,104,106,108,110,80,82,84..., dimensions={0} | all-to-all | bytes 458752 | tf_op jit(solution)/shard_map/all_to_all | solution.py:111
  75.9 0.5 reshape.24
  76.4 0.1 fusion.3
  76.5 0.1 rev.7
  76.7 0.2 fusion.7
  76.9 0.7 reshape.23
  (8 shorter events, 0.2 us)
Async XLA Ops:
  0.0 21.2 %copy-start = (bf16[8,512,128]{2,1,0:T(8,128)(2,1)S(1)}, bf16[8,512,128]{2,1,0:T(8,128)(2,1)}, u32[]{:S(2)}) copy-start(bf16[8,512,128]{2,1,0:T(8,128)(2,1)} %param.10) | copy-start | bytes 3145732
  3.4 7.4 %copy-start.1 = (bf16[1024,224]{0,1:T(8,128)(2,1)S(1)}, bf16[1024,224]{0,1:T(8,128)(2,1)}, u32[]{:S(2)}) copy-start(bf16[1024,224]{0,1:T(8,128)(2,1)} %param.11) | copy-start | bytes 1376260
  3.4 17.8 %all-to-all-start.1 = ((bf16[16,2,8,512]{3,2,1,0:T(8,128)(2,1)}), bf16[16,2,8,512]{3,2,1,0:T(8,128)(2,1)S(1)}, u32[]{:S(2)}, u32[]{:S(2)}) async-start(bf16[16,2,8,512]{3,2,1,0:T(8,128)(2,1)} %bitcast.33), calls=%async_computation.1 | async-start | bytes 524288 | tf_op jit(solution)/shard_map/all_to_all | solution.py:87
  10.8 34.8 %collective-permute-start.1 = (bf16[1024,224]{0,1:T(8,128)(2,1)S(1)}, bf16[1024,224]{0,1:T(8,128)(2,1)S(1)}, u32[]{:S(2)}, u32[]{:S(2)}) collective-permute-start(bf16[1024,224]{0,1:T(8,128)(2,1)S(1)} %copy-done.1), channel_id=1, source_target_pairs={{0,256},{128,384},{256,0},{384,128},{1,257},{129,385},{257,1},{385... | collective-permute-start | bytes 1376264 | tf_op jit(solution)/shard_map/ppermute | solution.py:82
  14.1 31.5 %collective-permute-start = (bf16[1024,224]{0,1:T(8,128)(2,1)S(1)}, bf16[1024,224]{0,1:T(8,128)(2,1)S(1)}, u32[]{:S(2)}, u32[]{:S(2)}) collective-permute-start(bf16[1024,224]{0,1:T(8,128)(2,1)S(1)} %copy-done.1), channel_id=1, source_target_pairs={{0,384},{128,0},{256,128},{384,256},{1,385},{129,1},{257,129},{385... | collective-permute-start | bytes 1376264 | tf_op jit(solution)/shard_map/ppermute | solution.py:82
  17.7 28.0 %collective-permute-start.2 = (bf16[1024,224]{0,1:T(8,128)(2,1)S(1)}, bf16[1024,224]{0,1:T(8,128)(2,1)S(1)}, u32[]{:S(2)}, u32[]{:S(2)}) collective-permute-start(bf16[1024,224]{0,1:T(8,128)(2,1)S(1)} %copy-done.1), channel_id=1, source_target_pairs={{0,128},{128,256},{256,384},{384,0},{1,129},{129,257},{257,385},{3... | collective-permute-start | bytes 1376264 | tf_op jit(solution)/shard_map/ppermute | solution.py:82
  47.2 3.7 %collective-permute-start.3 = (f32[128,896]{0,1:T(8,128)S(1)}, f32[128,896]{0,1:T(8,128)S(1)}, u32[]{:S(2)}, u32[]{:S(2)}) collective-permute-start(f32[128,896]{0,1:T(8,128)S(1)} %slice_select_fusion), channel_id=1, source_target_pairs={{0,1},{1,0},{2,3},{3,2},{4,5},{5,4},{6,7},{7,6},{8,9},{9,8},{10,11... | collective-permute-start | bytes 1376264 | tf_op jit(solution)/shard_map/ppermute | solution.py:107

commit v16 on v15

--- a/solution.py
+++ b/solution.py
@@ -111,11 +111,12 @@
     parts = lax.all_to_all(
         summed, ("z", "y"), split_axis=0, concat_axis=0, tiled=True, axis_index_groups=downward
     )
-    parts = parts.reshape(nz, ny, requests, nx, -1).astype(f32)
+    parts = parts.reshape(nz, ny, requests, -1).astype(f32)
     total = parts[:, 0]
     for i in range(1, ny):
         total = total + parts[:, i]
-    total = total[::-1].astype(bf16).transpose(1, 2, 0, 3)
+    total = lax.optimization_barrier(total.astype(bf16)).reshape(nz, requests, nx, -1)
+    total = total[::-1].transpose(1, 2, 0, 3)
     shifted = total[:, :1], total[:, :0:-1]
     total = jnp.concatenate([*shifted, *shifted], axis=1)
     total = lax.dynamic_slice_in_dim(total, turn, nx, 1, allow_negative_indices=False)

time: 78 us -> 77.7 us (level)
  no operation moved by 1% of the time
where the time goes in v16:
time: 77.7 us; the launch traced here: 77.3 us
  blocking collectives  48.5 us (62%)
  starting transfers between devices  19.6 us (25%)
  Pallas kernels  3.41 us (4%)
  waiting for transfers between devices  1.81 us (2%)
  matrix products  1.71 us (2%)
  local copies, waits for them, and re-layouts  1.61 us (2%)
    all_to_all x1, blocking collectives, local(): lax.all_to_all(summed, ('z', 'y'), split_axis=0, concat_axis=0, tiled=Tru...  24.6 us
    all_to_all x1, blocking collectives, gather(): lax.all_to_all(values, 'z', split_axis=0, concat_axis=0, tiled=True, axis...  23.9 us
    ppermute x3, starting transfers between devices, local(): lax.ppermute(output_weight, 'x', [(i, (i + k) % nx) for i in range(nx)])  10.4 us
    all_to_all x1, starting transfers between devices, local(): lax.all_to_all(latent, ('c', 'y'), split_axis=0, concat_axis=0, tiled=True)  7.35 us
    pallas_call x1, Pallas kernels, attend(): pl.pallas_call(attend_kernel, in_specs=[pl.BlockSpec(memory_space=pltpu.S...  3.41 us
    ppermute x1, starting transfers between devices, local(): received = lax.ppermute(theirs, 'c', [(i, (i + 1) % nc) for i in range(nc)])  1.92 us
    ppermute x1, waiting for transfers between devices, local(): received = lax.ppermute(theirs, 'c', [(i, (i + 1) % nc) for i in range(nc)])  1.77 us
  transfers between devices with their start and end apart: 5, of which 1 were waited for; matrix products, arithmetic and copies ran while one was open for 1% of the time, Pallas kernels for 0%

profile of v16, /device:TPU:6, one launch (start us, length us, event | category | flops | bytes accessed | tf_op | source)
XLA Modules:
  0.0 77.3 jit_solution(3400534532237791848)
XLA Ops:
  0.0 0.0 copy-start
  0.0 3.4 %attend.1 = bf16[2,8,2,8,512]{4,3,2,1,0:T(8,128)(2,1)} custom-call(s32[2]{0:T(128)} %lengths.1, bf16[2,576,128]{2,1,0:T(8,128)(2,1)} %bitcast.40, bf16[2,576,256]{2,1,0:T(8,128)(2,1)} %bitcast.39), custom_call_target="tpu_custom_call" | custom-call | flops 142606336 | bytes 1146880 | tf_op jit(solution)/shard_map/attend/pallas_call | solution.py:57
  3.4 0.0 copy-start.1
  3.4 7.4 %all-to-all-start.1 = ((bf16[16,2,8,512]{3,2,1,0:T(8,128)(2,1)}), bf16[16,2,8,512]{3,2,1,0:T(8,128)(2,1)S(1)}, u32[]{:S(2)}, u32[]{:S(2)}) async-start(bf16[16,2,8,512]{3,2,1,0:T(8,128)(2,1)} %bitcast.38), calls=%async_computation.1 | async-start | bytes 524288 | tf_op jit(solution)/shard_map/all_to_all | solution.py:87
  10.8 0.0 copy-done.1
  10.8 3.3 %collective-permute-start.1 = (bf16[1024,224]{0,1:T(8,128)(2,1)S(1)}, bf16[1024,224]{0,1:T(8,128)(2,1)S(1)}, u32[]{:S(2)}, u32[]{:S(2)}) collective-permute-start(bf16[1024,224]{0,1:T(8,128)(2,1)S(1)} %copy-done.1), channel_id=1, source_target_pairs={{0,256},{128,384},{256,0},{384,128},{1,257},{129,385},{257,1},{385... | collective-permute-start | bytes 1376264 | tf_op jit(solution)/shard_map/ppermute | solution.py:82
  14.1 3.5 %collective-permute-start = (bf16[1024,224]{0,1:T(8,128)(2,1)S(1)}, bf16[1024,224]{0,1:T(8,128)(2,1)S(1)}, u32[]{:S(2)}, u32[]{:S(2)}) collective-permute-start(bf16[1024,224]{0,1:T(8,128)(2,1)S(1)} %copy-done.1), channel_id=1, source_target_pairs={{0,384},{128,0},{256,128},{384,256},{1,385},{129,1},{257,129},{385... | collective-permute-start | bytes 1376264 | tf_op jit(solution)/shard_map/ppermute | solution.py:82
  17.7 3.5 %collective-permute-start.2 = (bf16[1024,224]{0,1:T(8,128)(2,1)S(1)}, bf16[1024,224]{0,1:T(8,128)(2,1)S(1)}, u32[]{:S(2)}, u32[]{:S(2)}) collective-permute-start(bf16[1024,224]{0,1:T(8,128)(2,1)S(1)} %copy-done.1), channel_id=1, source_target_pairs={{0,128},{128,256},{256,384},{384,0},{1,129},{129,257},{257,385},{3... | collective-permute-start | bytes 1376264 | tf_op jit(solution)/shard_map/ppermute | solution.py:82
  21.2 0.0 all-to-all-done.1
  21.2 0.0 copy-done
  21.2 0.4 fusion
  21.6 24.1 %conditional.1 = (bf16[8,2,16,1024]{3,2,1,0:T(8,128)(2,1)S(1)}) conditional(s32[]{:T(128)} %convert_element_type.24, () %tuple.13, bf16[16,2,8,128]{3,0,1,2:T(8,128)(2,1)S(1)} %fusion), branch_computations={%region_0.0_spmd, %region_1.0_spmd} | conditional | bytes 1900552 | solution.py:98
  21.7 0.1 broadcast_in_dim.6
  21.7 23.9 %all_to_all.14 = bf16[8,2,16,1024]{3,2,1,0:T(8,128)(2,1)S(1)} all-to-all(bf16[8,2,16,1024]{3,2,1,0:T(8,128)(2,1)S(1)} %broadcast_in_dim.6), channel_id=1, replica_groups={{112,96,80,64,48,32,16,0},{113,97,81,65,49,33,17,1},{114,98,82,66,50,34..., dimensions={0} | all-to-all | bytes 1048576 | tf_op jit(solution)/shard_map/cond/branch_1_fun/all_to_all | solution.py:94
  45.7 0.0 collective-permute-done.1
  45.7 0.0 collective-permute-done
  45.7 0.0 collective-permute-done.2
  45.7 0.3 fusion.9
  46.1 0.3 fusion.12
  46.4 0.3 fusion.11
  46.8 0.3 fusion.10
  47.1 0.1 pad_maximum_fusion
  47.2 1.9 %collective-permute-start.3 = (f32[128,896]{0,1:T(8,128)S(1)}, f32[128,896]{0,1:T(8,128)S(1)}, u32[]{:S(2)}, u32[]{:S(2)}) collective-permute-start(f32[128,896]{0,1:T(8,128)S(1)} %slice_select_fusion), channel_id=1, source_target_pairs={{0,1},{1,0},{2,3},{3,2},{4,5},{5,4},{6,7},{7,6},{8,9},{9,8},{10,11... | collective-permute-start | bytes 1376264 | tf_op jit(solution)/shard_map/ppermute | solution.py:107
  49.2 1.8 %collective-permute-done.3 = f32[128,896]{0,1:T(8,128)S(1)} collective-permute-done((f32[128,896]{0,1:T(8,128)S(1)}, f32[128,896]{0,1:T(8,128)S(1)}, u32[]{:S(2)}, u32[]{:S(2)}) %collective-permute-start.3) | collective-permute-done | bytes 458784 | tf_op jit(solution)/shard_map/ppermute | solution.py:107
  50.9 0.1 add_convert_fusion
  51.0 0.2 copy.23
  51.2 0.1 reshape.25
  51.3 24.6 %all_to_all.15 = bf16[64,2,896]{2,1,0:T(2,128)(2,1)S(1)} all-to-all(bf16[64,2,896]{2,1,0:T(2,128)(2,1)S(1)} %reshape.25), channel_id=1, replica_groups={{112,114,116,118,120,122,124,126,96,98,100,102,104,106,108,110,80,82,84..., dimensions={0} | all-to-all | bytes 458752 | tf_op jit(solution)/shard_map/all_to_all | solution.py:111
  75.9 0.2 fusion.8
  76.1 0.1 reshape.26
  76.2 0.1 rev.7
  76.4 0.2 fusion.6
  76.6 0.7 reshape.27
  (9 shorter events, 0.2 us)
Async XLA Ops:
  0.0 21.2 %copy-start = (bf16[8,512,128]{2,1,0:T(8,128)(2,1)S(1)}, bf16[8,512,128]{2,1,0:T(8,128)(2,1)}, u32[]{:S(2)}) copy-start(bf16[8,512,128]{2,1,0:T(8,128)(2,1)} %param.10) | copy-start | bytes 3145732
  3.4 7.4 %copy-start.1 = (bf16[1024,224]{0,1:T(8,128)(2,1)S(1)}, bf16[1024,224]{0,1:T(8,128)(2,1)}, u32[]{:S(2)}) copy-start(bf16[1024,224]{0,1:T(8,128)(2,1)} %param.11) | copy-start | bytes 1376260
  3.4 17.8 %all-to-all-start.1 = ((bf16[16,2,8,512]{3,2,1,0:T(8,128)(2,1)}), bf16[16,2,8,512]{3,2,1,0:T(8,128)(2,1)S(1)}, u32[]{:S(2)}, u32[]{:S(2)}) async-start(bf16[16,2,8,512]{3,2,1,0:T(8,128)(2,1)} %bitcast.38), calls=%async_computation.1 | async-start | bytes 524288 | tf_op jit(solution)/shard_map/all_to_all | solution.py:87
  10.8 34.8 %collective-permute-start.1 = (bf16[1024,224]{0,1:T(8,128)(2,1)S(1)}, bf16[1024,224]{0,1:T(8,128)(2,1)S(1)}, u32[]{:S(2)}, u32[]{:S(2)}) collective-permute-start(bf16[1024,224]{0,1:T(8,128)(2,1)S(1)} %copy-done.1), channel_id=1, source_target_pairs={{0,256},{128,384},{256,0},{384,128},{1,257},{129,385},{257,1},{385... | collective-permute-start | bytes 1376264 | tf_op jit(solution)/shard_map/ppermute | solution.py:82
  14.1 31.5 %collective-permute-start = (bf16[1024,224]{0,1:T(8,128)(2,1)S(1)}, bf16[1024,224]{0,1:T(8,128)(2,1)S(1)}, u32[]{:S(2)}, u32[]{:S(2)}) collective-permute-start(bf16[1024,224]{0,1:T(8,128)(2,1)S(1)} %copy-done.1), channel_id=1, source_target_pairs={{0,384},{128,0},{256,128},{384,256},{1,385},{129,1},{257,129},{385... | collective-permute-start | bytes 1376264 | tf_op jit(solution)/shard_map/ppermute | solution.py:82
  17.7 28.0 %collective-permute-start.2 = (bf16[1024,224]{0,1:T(8,128)(2,1)S(1)}, bf16[1024,224]{0,1:T(8,128)(2,1)S(1)}, u32[]{:S(2)}, u32[]{:S(2)}) collective-permute-start(bf16[1024,224]{0,1:T(8,128)(2,1)S(1)} %copy-done.1), channel_id=1, source_target_pairs={{0,128},{128,256},{256,384},{384,0},{1,129},{129,257},{257,385},{3... | collective-permute-start | bytes 1376264 | tf_op jit(solution)/shard_map/ppermute | solution.py:82
  47.2 3.7 %collective-permute-start.3 = (f32[128,896]{0,1:T(8,128)S(1)}, f32[128,896]{0,1:T(8,128)S(1)}, u32[]{:S(2)}, u32[]{:S(2)}) collective-permute-start(f32[128,896]{0,1:T(8,128)S(1)} %slice_select_fusion), channel_id=1, source_target_pairs={{0,1},{1,0},{2,3},{3,2},{4,5},{5,4},{6,7},{7,6},{8,9},{9,8},{10,11... | collective-permute-start | bytes 1376264 | tf_op jit(solution)/shard_map/ppermute | solution.py:107

commit v17 on v16

--- a/solution.py
+++ b/solution.py
@@ -104,7 +104,7 @@
     both = jnp.concatenate([jnp.dot(rows, w, preferred_element_type=f32) for w in blocks], axis=1)
     first, second = jnp.split(both, nc)
     theirs, mine = jnp.where(c == 0, second, first), jnp.where(c == 0, first, second)
-    received = lax.ppermute(theirs, "c", [(i, (i + 1) % nc) for i in range(nc)])
+    received = lax.ppermute(theirs.astype(bf16), "c", [(i, (i + 1) % nc) for i in range(nc)])
     summed = (mine + received).astype(bf16).reshape(nz * ny, requests, -1)
     summed, turn = lax.optimization_barrier((summed, jnp.mod(nx - x, nx)))
     downward = [[z * ny + y for z in range(nz - 1, -1, -1) for y in range(ny)]]

time: 77.7 us -> 77.4 us (level)
  no operation moved by 1% of the time
where the time goes in v17:
time: 77.4 us; the launch traced here: 77 us
  blocking collectives  48.5 us (63%)
  starting transfers between devices  19.6 us (25%)
  Pallas kernels  3.41 us (4%)
  matrix products  1.71 us (2%)
  local copies, waits for them, and re-layouts  1.61 us (2%)
  waiting for transfers between devices  1.48 us (2%)
    all_to_all x1, blocking collectives, local(): lax.all_to_all(summed, ('z', 'y'), split_axis=0, concat_axis=0, tiled=Tru...  24.6 us
    all_to_all x1, blocking collectives, gather(): lax.all_to_all(values, 'z', split_axis=0, concat_axis=0, tiled=True, axis...  23.9 us
    ppermute x3, starting transfers between devices, local(): lax.ppermute(output_weight, 'x', [(i, (i + k) % nx) for i in range(nx)])  10.4 us
    all_to_all x1, starting transfers between devices, local(): lax.all_to_all(latent, ('c', 'y'), split_axis=0, concat_axis=0, tiled=True)  7.35 us
    pallas_call x1, Pallas kernels, attend(): pl.pallas_call(attend_kernel, in_specs=[pl.BlockSpec(memory_space=pltpu.S...  3.41 us
    ppermute x1, starting transfers between devices, local(): lax.ppermute(theirs.astype(bf16), 'c', [(i, (i + 1) % nc) for i in range(...  1.92 us
  transfers between devices with their start and end apart: 5, of which 1 were waited for; matrix products, arithmetic and copies ran while one was open for 1% of the time, Pallas kernels for 0%

profile of v17, /device:TPU:6, one launch (start us, length us, event | category | flops | bytes accessed | tf_op | source)
XLA Modules:
  0.0 77.0 jit_solution(14740356979767711567)
XLA Ops:
  0.0 0.0 copy-start
  0.0 3.4 %attend.1 = bf16[2,8,2,8,512]{4,3,2,1,0:T(8,128)(2,1)} custom-call(s32[2]{0:T(128)} %lengths.1, bf16[2,576,128]{2,1,0:T(8,128)(2,1)} %bitcast.40, bf16[2,576,256]{2,1,0:T(8,128)(2,1)} %bitcast.39), custom_call_target="tpu_custom_call" | custom-call | flops 142606336 | bytes 1146880 | tf_op jit(solution)/shard_map/attend/pallas_call | solution.py:57
  3.4 0.0 copy-start.1
  3.4 7.4 %all-to-all-start.1 = ((bf16[16,2,8,512]{3,2,1,0:T(8,128)(2,1)}), bf16[16,2,8,512]{3,2,1,0:T(8,128)(2,1)S(1)}, u32[]{:S(2)}, u32[]{:S(2)}) async-start(bf16[16,2,8,512]{3,2,1,0:T(8,128)(2,1)} %bitcast.38), calls=%async_computation.1 | async-start | bytes 524288 | tf_op jit(solution)/shard_map/all_to_all | solution.py:87
  10.8 0.0 copy-done.1
  10.8 3.3 %collective-permute-start.1 = (bf16[1024,224]{0,1:T(8,128)(2,1)S(1)}, bf16[1024,224]{0,1:T(8,128)(2,1)S(1)}, u32[]{:S(2)}, u32[]{:S(2)}) collective-permute-start(bf16[1024,224]{0,1:T(8,128)(2,1)S(1)} %copy-done.1), channel_id=1, source_target_pairs={{0,256},{128,384},{256,0},{384,128},{1,257},{129,385},{257,1},{385... | collective-permute-start | bytes 1376264 | tf_op jit(solution)/shard_map/ppermute | solution.py:82
  14.1 3.5 %collective-permute-start = (bf16[1024,224]{0,1:T(8,128)(2,1)S(1)}, bf16[1024,224]{0,1:T(8,128)(2,1)S(1)}, u32[]{:S(2)}, u32[]{:S(2)}) collective-permute-start(bf16[1024,224]{0,1:T(8,128)(2,1)S(1)} %copy-done.1), channel_id=1, source_target_pairs={{0,384},{128,0},{256,128},{384,256},{1,385},{129,1},{257,129},{385... | collective-permute-start | bytes 1376264 | tf_op jit(solution)/shard_map/ppermute | solution.py:82
  17.7 3.5 %collective-permute-start.2 = (bf16[1024,224]{0,1:T(8,128)(2,1)S(1)}, bf16[1024,224]{0,1:T(8,128)(2,1)S(1)}, u32[]{:S(2)}, u32[]{:S(2)}) collective-permute-start(bf16[1024,224]{0,1:T(8,128)(2,1)S(1)} %copy-done.1), channel_id=1, source_target_pairs={{0,128},{128,256},{256,384},{384,0},{1,129},{129,257},{257,385},{3... | collective-permute-start | bytes 1376264 | tf_op jit(solution)/shard_map/ppermute | solution.py:82
  21.2 0.0 all-to-all-done.1
  21.2 0.0 copy-done
  21.2 0.4 fusion
  21.6 24.1 %conditional.1 = (bf16[8,2,16,1024]{3,2,1,0:T(8,128)(2,1)S(1)}) conditional(s32[]{:T(128)} %convert_element_type.30, () %tuple.13, bf16[16,2,8,128]{3,0,1,2:T(8,128)(2,1)S(1)} %fusion), branch_computations={%region_0.0_spmd, %region_1.0_spmd} | conditional | bytes 1900552 | solution.py:98
  21.7 0.1 broadcast_in_dim.6
  21.7 23.9 %all_to_all.14 = bf16[8,2,16,1024]{3,2,1,0:T(8,128)(2,1)S(1)} all-to-all(bf16[8,2,16,1024]{3,2,1,0:T(8,128)(2,1)S(1)} %broadcast_in_dim.6), channel_id=1, replica_groups={{112,96,80,64,48,32,16,0},{113,97,81,65,49,33,17,1},{114,98,82,66,50,34..., dimensions={0} | all-to-all | bytes 1048576 | tf_op jit(solution)/shard_map/cond/branch_1_fun/all_to_all | solution.py:94
  45.7 0.0 collective-permute-done.1
  45.7 0.0 collective-permute-done
  45.7 0.0 collective-permute-done.2
  45.7 0.3 fusion.9
  46.1 0.3 fusion.12
  46.4 0.3 fusion.11
  46.8 0.3 fusion.10
  47.1 0.1 pad_maximum_fusion
  47.2 1.9 %collective-permute-start.3 = (bf16[128,896]{0,1:T(8,128)(2,1)S(1)}, bf16[128,896]{0,1:T(8,128)(2,1)S(1)}, u32[]{:S(2)}, u32[]{:S(2)}) collective-permute-start(bf16[128,896]{0,1:T(8,128)(2,1)S(1)} %select_convert_fusion), channel_id=1, source_target_pairs={{0,1},{1,0},{2,3},{3,2},{4,5},{5,4},{6,7},{7,6},{8,9},{9,8},{10,11... | collective-permute-start | bytes 688136 | tf_op jit(solution)/shard_map/ppermute | solution.py:107
  49.2 1.4 %collective-permute-done.3 = bf16[128,896]{0,1:T(8,128)(2,1)S(1)} collective-permute-done((bf16[128,896]{0,1:T(8,128)(2,1)S(1)}, bf16[128,896]{0,1:T(8,128)(2,1)S(1)}, u32[]{:S(2)}, u32[]{:S(2)}) %collective-permute-start.3) | collective-permute-done | bytes 229408 | tf_op jit(solution)/shard_map/ppermute | solution.py:107
  50.6 0.1 add_convert_fusion
  50.7 0.2 copy.23
  50.8 0.1 reshape.25
  50.9 24.6 %all_to_all.15 = bf16[64,2,896]{2,1,0:T(2,128)(2,1)S(1)} all-to-all(bf16[64,2,896]{2,1,0:T(2,128)(2,1)S(1)} %reshape.25), channel_id=1, replica_groups={{112,114,116,118,120,122,124,126,96,98,100,102,104,106,108,110,80,82,84..., dimensions={0} | all-to-all | bytes 458752 | tf_op jit(solution)/shard_map/all_to_all | solution.py:111
  75.5 0.2 fusion.8
  75.7 0.1 reshape.26
  75.9 0.1 rev.7
  76.1 0.2 fusion.6
  76.3 0.7 reshape.27
  (9 shorter events, 0.2 us)
Async XLA Ops:
  0.0 21.2 %copy-start = (bf16[8,512,128]{2,1,0:T(8,128)(2,1)S(1)}, bf16[8,512,128]{2,1,0:T(8,128)(2,1)}, u32[]{:S(2)}) copy-start(bf16[8,512,128]{2,1,0:T(8,128)(2,1)} %param.10) | copy-start | bytes 3145732
  3.4 7.4 %copy-start.1 = (bf16[1024,224]{0,1:T(8,128)(2,1)S(1)}, bf16[1024,224]{0,1:T(8,128)(2,1)}, u32[]{:S(2)}) copy-start(bf16[1024,224]{0,1:T(8,128)(2,1)} %param.11) | copy-start | bytes 1376260
  3.4 17.8 %all-to-all-start.1 = ((bf16[16,2,8,512]{3,2,1,0:T(8,128)(2,1)}), bf16[16,2,8,512]{3,2,1,0:T(8,128)(2,1)S(1)}, u32[]{:S(2)}, u32[]{:S(2)}) async-start(bf16[16,2,8,512]{3,2,1,0:T(8,128)(2,1)} %bitcast.38), calls=%async_computation.1 | async-start | bytes 524288 | tf_op jit(solution)/shard_map/all_to_all | solution.py:87
  10.8 34.8 %collective-permute-start.1 = (bf16[1024,224]{0,1:T(8,128)(2,1)S(1)}, bf16[1024,224]{0,1:T(8,128)(2,1)S(1)}, u32[]{:S(2)}, u32[]{:S(2)}) collective-permute-start(bf16[1024,224]{0,1:T(8,128)(2,1)S(1)} %copy-done.1), channel_id=1, source_target_pairs={{0,256},{128,384},{256,0},{384,128},{1,257},{129,385},{257,1},{385... | collective-permute-start | bytes 1376264 | tf_op jit(solution)/shard_map/ppermute | solution.py:82
  14.1 31.5 %collective-permute-start = (bf16[1024,224]{0,1:T(8,128)(2,1)S(1)}, bf16[1024,224]{0,1:T(8,128)(2,1)S(1)}, u32[]{:S(2)}, u32[]{:S(2)}) collective-permute-start(bf16[1024,224]{0,1:T(8,128)(2,1)S(1)} %copy-done.1), channel_id=1, source_target_pairs={{0,384},{128,0},{256,128},{384,256},{1,385},{129,1},{257,129},{385... | collective-permute-start | bytes 1376264 | tf_op jit(solution)/shard_map/ppermute | solution.py:82
  17.7 28.0 %collective-permute-start.2 = (bf16[1024,224]{0,1:T(8,128)(2,1)S(1)}, bf16[1024,224]{0,1:T(8,128)(2,1)S(1)}, u32[]{:S(2)}, u32[]{:S(2)}) collective-permute-start(bf16[1024,224]{0,1:T(8,128)(2,1)S(1)} %copy-done.1), channel_id=1, source_target_pairs={{0,128},{128,256},{256,384},{384,0},{1,129},{129,257},{257,385},{3... | collective-permute-start | bytes 1376264 | tf_op jit(solution)/shard_map/ppermute | solution.py:82
  47.2 3.4 %collective-permute-start.3 = (bf16[128,896]{0,1:T(8,128)(2,1)S(1)}, bf16[128,896]{0,1:T(8,128)(2,1)S(1)}, u32[]{:S(2)}, u32[]{:S(2)}) collective-permute-start(bf16[128,896]{0,1:T(8,128)(2,1)S(1)} %select_convert_fusion), channel_id=1, source_target_pairs={{0,1},{1,0},{2,3},{3,2},{4,5},{5,4},{6,7},{7,6},{8,9},{9,8},{10,11... | collective-permute-start | bytes 688136 | tf_op jit(solution)/shard_map/ppermute | solution.py:107

commit v18 on v17

--- a/solution.py
+++ b/solution.py
@@ -98,7 +98,7 @@
     everyone = lax.cond(x < nx, gather, lambda v: jnp.zeros((nz, *v.shape), bf16), values)
     everyone, *others = lax.optimization_barrier((everyone, *sent.values()))
     sent = dict(zip(sent, others))
-    blocks = [output_weight, *(sent[k] for k in range(1, nx))]
+    blocks = [output_weight, *(sent[k] for k in range(nx - 1, 0, -1))]
 
     rows = everyone.transpose(1, 0, 2, 3).reshape(nc * nz * ny * requests, -1)
     both = jnp.concatenate([jnp.dot(rows, w, preferred_element_type=f32) for w in blocks], axis=1)
@@ -117,8 +117,7 @@
         total = total + parts[:, i]
     total = lax.optimization_barrier(total.astype(bf16)).reshape(nz, requests, nx, -1)
     total = total[::-1].transpose(1, 2, 0, 3)
-    shifted = total[:, :1], total[:, :0:-1]
-    total = jnp.concatenate([*shifted, *shifted], axis=1)
+    total = jnp.concatenate([total, total], axis=1)
     total = lax.dynamic_slice_in_dim(total, turn, nx, 1, allow_negative_indices=False)
     return total.reshape(requests, -1)
 

time: 77.4 us -> 77.1 us (level)
  no operation moved by 1% of the time
where the time goes in v18:
time: 77.1 us; the launch traced here: 76.7 us
  blocking collectives  48.5 us (63%)
  starting transfers between devices  19.6 us (25%)
  Pallas kernels  3.41 us (4%)
  matrix products  1.71 us (2%)
  waiting for transfers between devices  1.48 us (2%)
  local copies, waits for them, and re-layouts  1.43 us (2%)
    all_to_all x1, blocking collectives, local(): lax.all_to_all(summed, ('z', 'y'), split_axis=0, concat_axis=0, tiled=Tru...  24.6 us
    all_to_all x1, blocking collectives, gather(): lax.all_to_all(values, 'z', split_axis=0, concat_axis=0, tiled=True, axis...  23.9 us
    ppermute x3, starting transfers between devices, local(): lax.ppermute(output_weight, 'x', [(i, (i + k) % nx) for i in range(nx)])  10.4 us
    all_to_all x1, starting transfers between devices, local(): lax.all_to_all(latent, ('c', 'y'), split_axis=0, concat_axis=0, tiled=True)  7.35 us
    pallas_call x1, Pallas kernels, attend(): pl.pallas_call(attend_kernel, in_specs=[pl.BlockSpec(memory_space=pltpu.S...  3.41 us
    ppermute x1, starting transfers between devices, local(): lax.ppermute(theirs.astype(bf16), 'c', [(i, (i + 1) % nc) for i in range(...  1.92 us
  transfers between devices with their start and end apart: 5, of which 1 were waited for; matrix products, arithmetic and copies ran while one was open for 1% of the time, Pallas kernels for 0%

profile of v18, /device:TPU:6, one launch (start us, length us, event | category | flops | bytes accessed | tf_op | source)
XLA Modules:
  0.0 76.7 jit_solution(17251937309221287599)
XLA Ops:
  0.0 0.0 copy-start
  0.0 3.4 %attend.1 = bf16[2,8,2,8,512]{4,3,2,1,0:T(8,128)(2,1)} custom-call(s32[2]{0:T(128)} %lengths.1, bf16[2,576,128]{2,1,0:T(8,128)(2,1)} %bitcast.40, bf16[2,576,256]{2,1,0:T(8,128)(2,1)} %bitcast.39), custom_call_target="tpu_custom_call" | custom-call | flops 142606336 | bytes 1146880 | tf_op jit(solution)/shard_map/attend/pallas_call | solution.py:57
  3.4 0.0 copy-start.1
  3.4 7.4 %all-to-all-start.1 = ((bf16[16,2,8,512]{3,2,1,0:T(8,128)(2,1)}), bf16[16,2,8,512]{3,2,1,0:T(8,128)(2,1)S(1)}, u32[]{:S(2)}, u32[]{:S(2)}) async-start(bf16[16,2,8,512]{3,2,1,0:T(8,128)(2,1)} %bitcast.38), calls=%async_computation.1 | async-start | bytes 524288 | tf_op jit(solution)/shard_map/all_to_all | solution.py:87
  10.8 0.0 copy-done.1
  10.8 3.3 %collective-permute-start.1 = (bf16[1024,224]{0,1:T(8,128)(2,1)S(1)}, bf16[1024,224]{0,1:T(8,128)(2,1)S(1)}, u32[]{:S(2)}, u32[]{:S(2)}) collective-permute-start(bf16[1024,224]{0,1:T(8,128)(2,1)S(1)} %copy-done.1), channel_id=1, source_target_pairs={{0,256},{128,384},{256,0},{384,128},{1,257},{129,385},{257,1},{385... | collective-permute-start | bytes 1376264 | tf_op jit(solution)/shard_map/ppermute | solution.py:82
  14.1 3.5 %collective-permute-start = (bf16[1024,224]{0,1:T(8,128)(2,1)S(1)}, bf16[1024,224]{0,1:T(8,128)(2,1)S(1)}, u32[]{:S(2)}, u32[]{:S(2)}) collective-permute-start(bf16[1024,224]{0,1:T(8,128)(2,1)S(1)} %copy-done.1), channel_id=1, source_target_pairs={{0,384},{128,0},{256,128},{384,256},{1,385},{129,1},{257,129},{385... | collective-permute-start | bytes 1376264 | tf_op jit(solution)/shard_map/ppermute | solution.py:82
  17.7 3.5 %collective-permute-start.2 = (bf16[1024,224]{0,1:T(8,128)(2,1)S(1)}, bf16[1024,224]{0,1:T(8,128)(2,1)S(1)}, u32[]{:S(2)}, u32[]{:S(2)}) collective-permute-start(bf16[1024,224]{0,1:T(8,128)(2,1)S(1)} %copy-done.1), channel_id=1, source_target_pairs={{0,128},{128,256},{256,384},{384,0},{1,129},{129,257},{257,385},{3... | collective-permute-start | bytes 1376264 | tf_op jit(solution)/shard_map/ppermute | solution.py:82
  21.2 0.0 all-to-all-done.1
  21.2 0.0 copy-done
  21.2 0.4 fusion
  21.6 24.1 %conditional.1 = (bf16[8,2,16,1024]{3,2,1,0:T(8,128)(2,1)S(1)}) conditional(s32[]{:T(128)} %convert_element_type.30, () %tuple.13, bf16[16,2,8,128]{3,0,1,2:T(8,128)(2,1)S(1)} %fusion), branch_computations={%region_0.0_spmd, %region_1.0_spmd} | conditional | bytes 1900552 | solution.py:98
  21.7 0.1 broadcast_in_dim.6
  21.7 23.9 %all_to_all.14 = bf16[8,2,16,1024]{3,2,1,0:T(8,128)(2,1)S(1)} all-to-all(bf16[8,2,16,1024]{3,2,1,0:T(8,128)(2,1)S(1)} %broadcast_in_dim.6), channel_id=1, replica_groups={{112,96,80,64,48,32,16,0},{113,97,81,65,49,33,17,1},{114,98,82,66,50,34..., dimensions={0} | all-to-all | bytes 1048576 | tf_op jit(solution)/shard_map/cond/branch_1_fun/all_to_all | solution.py:94
  45.7 0.0 collective-permute-done.1
  45.7 0.0 collective-permute-done
  45.7 0.0 collective-permute-done.2
  45.7 0.3 fusion.7
  46.1 0.3 fusion.10
  46.4 0.3 fusion.9
  46.8 0.3 fusion.8
  47.1 0.1 pad_maximum_fusion
  47.2 1.9 %collective-permute-start.3 = (bf16[128,896]{0,1:T(8,128)(2,1)S(1)}, bf16[128,896]{0,1:T(8,128)(2,1)S(1)}, u32[]{:S(2)}, u32[]{:S(2)}) collective-permute-start(bf16[128,896]{0,1:T(8,128)(2,1)S(1)} %select_convert_fusion), channel_id=1, source_target_pairs={{0,1},{1,0},{2,3},{3,2},{4,5},{5,4},{6,7},{7,6},{8,9},{9,8},{10,11... | collective-permute-start | bytes 688136 | tf_op jit(solution)/shard_map/ppermute | solution.py:107
  49.2 1.4 %collective-permute-done.3 = bf16[128,896]{0,1:T(8,128)(2,1)S(1)} collective-permute-done((bf16[128,896]{0,1:T(8,128)(2,1)S(1)}, bf16[128,896]{0,1:T(8,128)(2,1)S(1)}, u32[]{:S(2)}, u32[]{:S(2)}) %collective-permute-start.3) | collective-permute-done | bytes 229408 | tf_op jit(solution)/shard_map/ppermute | solution.py:107
  50.6 0.1 add_convert_fusion
  50.7 0.2 copy.23
  50.8 0.1 reshape.25
  50.9 24.6 %all_to_all.15 = bf16[64,2,896]{2,1,0:T(2,128)(2,1)S(1)} all-to-all(bf16[64,2,896]{2,1,0:T(2,128)(2,1)S(1)} %reshape.25), channel_id=1, replica_groups={{112,114,116,118,120,122,124,126,96,98,100,102,104,106,108,110,80,82,84..., dimensions={0} | all-to-all | bytes 458752 | tf_op jit(solution)/shard_map/all_to_all | solution.py:111
  75.5 0.2 fusion.6
  75.7 0.1 reshape.26
  75.9 0.1 fusion.4
  76.0 0.7 reshape.27
  (7 shorter events, 0.2 us)
Async XLA Ops:
  0.0 21.2 %copy-start = (bf16[8,512,128]{2,1,0:T(8,128)(2,1)S(1)}, bf16[8,512,128]{2,1,0:T(8,128)(2,1)}, u32[]{:S(2)}) copy-start(bf16[8,512,128]{2,1,0:T(8,128)(2,1)} %param.10) | copy-start | bytes 3145732
  3.4 7.4 %copy-start.1 = (bf16[1024,224]{0,1:T(8,128)(2,1)S(1)}, bf16[1024,224]{0,1:T(8,128)(2,1)}, u32[]{:S(2)}) copy-start(bf16[1024,224]{0,1:T(8,128)(2,1)} %param.11) | copy-start | bytes 1376260
  3.4 17.8 %all-to-all-start.1 = ((bf16[16,2,8,512]{3,2,1,0:T(8,128)(2,1)}), bf16[16,2,8,512]{3,2,1,0:T(8,128)(2,1)S(1)}, u32[]{:S(2)}, u32[]{:S(2)}) async-start(bf16[16,2,8,512]{3,2,1,0:T(8,128)(2,1)} %bitcast.38), calls=%async_computation.1 | async-start | bytes 524288 | tf_op jit(solution)/shard_map/all_to_all | solution.py:87
  10.8 34.8 %collective-permute-start.1 = (bf16[1024,224]{0,1:T(8,128)(2,1)S(1)}, bf16[1024,224]{0,1:T(8,128)(2,1)S(1)}, u32[]{:S(2)}, u32[]{:S(2)}) collective-permute-start(bf16[1024,224]{0,1:T(8,128)(2,1)S(1)} %copy-done.1), channel_id=1, source_target_pairs={{0,256},{128,384},{256,0},{384,128},{1,257},{129,385},{257,1},{385... | collective-permute-start | bytes 1376264 | tf_op jit(solution)/shard_map/ppermute | solution.py:82
  14.1 31.5 %collective-permute-start = (bf16[1024,224]{0,1:T(8,128)(2,1)S(1)}, bf16[1024,224]{0,1:T(8,128)(2,1)S(1)}, u32[]{:S(2)}, u32[]{:S(2)}) collective-permute-start(bf16[1024,224]{0,1:T(8,128)(2,1)S(1)} %copy-done.1), channel_id=1, source_target_pairs={{0,384},{128,0},{256,128},{384,256},{1,385},{129,1},{257,129},{385... | collective-permute-start | bytes 1376264 | tf_op jit(solution)/shard_map/ppermute | solution.py:82
  17.7 28.0 %collective-permute-start.2 = (bf16[1024,224]{0,1:T(8,128)(2,1)S(1)}, bf16[1024,224]{0,1:T(8,128)(2,1)S(1)}, u32[]{:S(2)}, u32[]{:S(2)}) collective-permute-start(bf16[1024,224]{0,1:T(8,128)(2,1)S(1)} %copy-done.1), channel_id=1, source_target_pairs={{0,128},{128,256},{256,384},{384,0},{1,129},{129,257},{257,385},{3... | collective-permute-start | bytes 1376264 | tf_op jit(solution)/shard_map/ppermute | solution.py:82
  47.2 3.4 %collective-permute-start.3 = (bf16[128,896]{0,1:T(8,128)(2,1)S(1)}, bf16[128,896]{0,1:T(8,128)(2,1)S(1)}, u32[]{:S(2)}, u32[]{:S(2)}) collective-permute-start(bf16[128,896]{0,1:T(8,128)(2,1)S(1)} %select_convert_fusion), channel_id=1, source_target_pairs={{0,1},{1,0},{2,3},{3,2},{4,5},{5,4},{6,7},{7,6},{8,9},{9,8},{10,11... | collective-permute-start | bytes 688136 | tf_op jit(solution)/shard_map/ppermute | solution.py:107
